TPU v7x, 512 devices: a whole 4x8x8 slice. The times are simulated.
512 devices in a mesh: shot: 16 (over x, y_hi), dom: 32 (over y_lo, z, core).
Axes of the slice: x: 4, y: 8 (y_hi: 4, y_lo: 2; y = y_hi * 2 + y_lo), z: 8, core: 2. Of those that a mesh axis runs over, the one named last changes fastest.
Arguments:
- velocity: float32 [512, 8, 8, 128], P(('shot', 'dom')), may hold values from 1.5 to 4.5
- aperture: int32 [16, 32, 2], P('shot', 'dom'), may hold values from 0 to 511, as said below
- source_cell: int32 [16], P('shot'), may hold values from 0 to 524287
- wavelet: float32 [16, 64], P('shot'), may hold values from -6 to 6
- observed: float32 [16, 64, 256], P('shot'), may hold values from -6 to 6
- receivers: int32 [16, 256], P('shot'), may hold values from 0 to 524287
- checkpoint: int32 [16], P('shot'), may hold values from 0 to 56
- forward_previous: float32 [16, 256, 16, 128], P('shot', 'dom'), may hold values from -6 to 6
- forward_current: float32 [16, 256, 16, 128], P('shot', 'dom'), may hold values from -6 to 6
- adjoint_next: float32 [16, 256, 16, 128], P('shot', 'dom'), may hold values from -6 to 6
- adjoint_current: float32 [16, 256, 16, 128], P('shot', 'dom'), may hold values from -6 to 6
Outputs:
- gradient: float32 [512, 8, 8, 128], P(('shot', 'dom'))
Inputs may be any that keep to these rules, and one draw needn't show every extreme that they name: For each group g there is a start row s_g with aperture[g, d, k] = (s_g + k) * 32 + d: the group's aperture is 2 consecutive rows of tiles across all slabs. Start rows repeat among groups.
All inputs are finite; a program needn't handle non-finite values.
Results may differ from a plain program's by a relative error of at most 0.0003.
Values sent between devices are 32-bit elements; how exact they have to be, the bound alone decides.
No kernel may reach another device: no remote copies, remote signals or barrier semaphores. Data moves between devices by JAX's collectives and lax.ppermute only.
A program may use at most 64 MiB of HBM per device.

v0:
```python
import jax
import jax.numpy as jnp
from jax import lax
from jax.sharding import PartitionSpec as P

STEPS = 8


STENCIL_WEIGHTS = (-205.0 / 72.0, 8.0 / 5.0, -1.0 / 5.0, 8.0 / 315.0, -1.0 / 560.0)
STEP_SCALE = 0.088


def with_halo(cells, sides, width):
    for axis, dim in sides:
        count = lax.axis_size(axis)
        ends = count - 1
        head = lax.slice_in_dim(cells, 0, width, axis=dim)
        tail = lax.slice_in_dim(cells, cells.shape[dim] - width, cells.shape[dim], axis=dim)
        cells = jnp.concatenate(
            [
                lax.ppermute(tail, axis, [(i, (i + 1) % count) for i in range(ends)]),
                cells,
                lax.ppermute(head, axis, [((i + 1) % count, i) for i in range(ends)]),
            ],
            axis=dim,
        )
    return cells


def laplace(field, padded_x):
    extent_x, extent_y, extent_z = field.shape
    padded = jnp.pad(padded_x, ((0, 0), (4, 4), (4, 4)))
    middle = padded[4 : 4 + extent_x, 4 : 4 + extent_y, 4 : 4 + extent_z]
    accumulated = 3.0 * STENCIL_WEIGHTS[0] * middle
    for offset in range(1, 5):
        neighbours = (
            padded[4 + offset : 4 + offset + extent_x, 4 : 4 + extent_y, 4 : 4 + extent_z]
            + padded[4 - offset : 4 - offset + extent_x, 4 : 4 + extent_y, 4 : 4 + extent_z]
        )
        neighbours = (
            neighbours
            + padded[4 : 4 + extent_x, 4 + offset : 4 + offset + extent_y, 4 : 4 + extent_z]
            + padded[4 : 4 + extent_x, 4 - offset : 4 - offset + extent_y, 4 : 4 + extent_z]
        )
        neighbours = (
            neighbours
            + padded[4 : 4 + extent_x, 4 : 4 + extent_y, 4 + offset : 4 + offset + extent_z]
            + padded[4 : 4 + extent_x, 4 : 4 + extent_y, 4 - offset : 4 - offset + extent_z]
        )
        accumulated = accumulated + STENCIL_WEIGHTS[offset] * neighbours
    return accumulated


def stencil(field):
    padded_x = with_halo(field, (("dom", 0),), 4)
    return laplace(field, padded_x)


def localize(flat_index, first_x, extent_x, plane_cells):
    plane_x = flat_index // plane_cells
    within = flat_index % plane_cells
    local_x = plane_x - first_x
    inside = (local_x >= 0) & (local_x < extent_x)
    clipped = jnp.clip(local_x, 0, extent_x - 1) * plane_cells + within
    return (clipped, inside)


def inject(field, places, inside, values):
    added = jnp.where(inside, values, 0.0)
    return field.reshape(-1).at[places].add(added).reshape(field.shape)


def body(
    velocity,
    aperture,
    source_cell,
    wavelet,
    observed,
    receivers,
    checkpoint,
    forward_previous,
    forward_current,
    adjoint_next,
    adjoint_current,
):
    slabs = lax.axis_size("dom")
    shot_index = lax.axis_index("shot")
    dom_index = lax.axis_index("dom")
    tile_x, tile_y, tile_z = (velocity.shape[1], velocity.shape[2], velocity.shape[3])
    layers = aperture.shape[2]
    lists = lax.all_gather(aperture, "shot", axis=0, tiled=True)
    rows_mine = aperture[0, 0] // slabs
    portion = lax.all_gather(velocity, "shot", axis=0, tiled=True)
    amount = portion.shape[0]
    wanted = jnp.arange(amount, dtype=jnp.int32)
    matches = rows_mine[:, None] == wanted[None, :]
    gathered_tiles = jnp.sum(jnp.where(matches[:, :, None, None, None], portion[None], 0.0), axis=1)
    speed = gathered_tiles.transpose(1, 0, 2, 3).reshape(tile_x, layers * tile_y, tile_z)
    courant = (STEP_SCALE * speed) ** 2
    plane_cells = speed.shape[1] * speed.shape[2]
    first_x = dom_index * tile_x
    source_clipped, source_inside = localize(source_cell[0], first_x, tile_x, plane_cells)
    receiver_clipped, receiver_inside = localize(receivers[0], first_x, tile_x, plane_cells)
    amplitudes = lax.dynamic_slice_in_dim(wavelet[0], checkpoint[0], STEPS, 0)
    recorded = lax.dynamic_slice_in_dim(observed[0], checkpoint[0], STEPS, 0)
    forward_fields = [forward_previous[0], forward_current[0]]
    for moment in range(STEPS):
        present = forward_fields[-1]
        advanced = 2.0 * present - forward_fields[-2] + courant * stencil(present)
        advanced = inject(advanced, source_clipped, source_inside, amplitudes[moment])
        forward_fields.append(advanced)
    misfits = {}
    for moment in range(1, STEPS + 1):
        sampled = forward_fields[moment + 1].reshape(-1)[receiver_clipped]
        misfits[moment] = jnp.where(receiver_inside, sampled - recorded[moment - 1], 0.0)
    later = adjoint_next[0]
    present = adjoint_current[0]
    imaging = jnp.zeros_like(speed)
    for moment in range(STEPS, 0, -1):
        earlier = 2.0 * present - later + courant * stencil(present)
        earlier = (
            earlier.reshape(-1).at[receiver_clipped].add(misfits[moment]).reshape(present.shape)
        )
        index_n = moment - 1
        curvature = (
            forward_fields[index_n + 2]
            - 2.0 * forward_fields[index_n + 1]
            + forward_fields[index_n]
        )
        imaging = imaging + earlier * curvature
        later = present
        present = earlier
    gradient_term = 2.0 / speed**3 * imaging
    term_tiles = gradient_term.reshape(tile_x, layers, tile_y, tile_z).transpose(1, 0, 2, 3)
    portion = lax.all_gather(term_tiles[None], "shot", axis=0, tiled=True)
    owners = lists[:, 0, :] // slabs
    matches = owners == shot_index
    return jnp.sum(jnp.where(matches[:, :, None, None, None], portion, 0.0), axis=(0, 1))[None]


def solution(mesh):
    placed = (
        P(("shot", "dom"), None, None, None),
        P("shot", "dom", None),
        P("shot"),
        P("shot", None),
        P("shot", None, None),
        P("shot", None),
        P("shot"),
        P("shot", "dom", None, None),
        P("shot", "dom", None, None),
        P("shot", "dom", None, None),
        P("shot", "dom", None, None),
    )
    return jax.shard_map(
        body,
        mesh=mesh,
        in_specs=placed,
        out_specs=P(("shot", "dom"), None, None, None),
        check_vma=False,
    )
```

profile of v0, /device:TPU:64, one launch (start us, length us, event | category | flops | bytes accessed | tf_op | source)
XLA Modules:
  0.0 302.3 jit_solution(13464330915979955404)
XLA Ops:
  9.3 2.4 collective-permute-start.3
  12.3 48.5 %all_gather.10 = f32[16,8,8,128]{3,2,1,0:T(8,128)S(1)} all-gather(f32[1,8,8,128]{3,2,1,0:T(8,128)S(1)} %copy-done.5), channel_id=1, replica_groups=mesh['shot'=16,'dom'=32] {'shot'}, dimensions={0}, use_global_device_ids=true | all-gather | bytes 557056 | tf_op jit(solution)/shard_map/all_gather | solution.py:93
  66.7 2.4 collective-permute-start.5
  69.1 3.2 %collective-permute-start = (f32[4,16,128]{2,1,0:T(8,128)S(1)}, f32[4,16,128]{2,1,0:T(8,128)S(1)}, u32[]{:S(2)}, u32[]{:S(2)}) collective-permute-start(f32[4,16,128]{2,1,0:T(8,128)S(1)} %get-tuple-element.141), channel_id=1, source_target_pairs={{1,0},{2,1},{3,2},{4,3},{5,4},{6,5},{7,6},{8,7},{9,8},{10,9},{11,1... | collective-permute-start | bytes 98312 | tf_op jit(solution)/shard_map/ppermute | solution.py:23
  72.3 2.7 collective-permute-start.1
  76.3 2.9 collective-permute-start.6
  79.2 2.7 collective-permute-start.7
  87.1 2.4 collective-permute-start.9
  95.1 2.7 collective-permute-start.11
  101.0 2.8 collective-permute-start.12
  103.9 2.7 collective-permute-start.13
  106.8 2.4 collective-permute-done.13
  111.9 2.4 collective-permute-start.15
  117.9 2.4 collective-permute-start.16
  120.3 3.4 %collective-permute-start.17 = (f32[4,16,128]{2,1,0:T(8,128)S(1)}, f32[4,16,128]{2,1,0:T(8,128)S(1)}, u32[]{:S(2)}, u32[]{:S(2)}) collective-permute-start(f32[4,16,128]{2,1,0:T(8,128)S(1)} %bitcast.303), channel_id=1, source_target_pairs={{0,1},{1,2},{2,3},{3,4},{4,5},{5,6},{6,7},{7,8},{8,9},{9,10},{10,1... | collective-permute-start | bytes 98312 | tf_op jit(solution)/shard_map/ppermute | solution.py:21
  140.8 5.5 %collective-permute-start.19 = (f32[4,16,128]{2,1,0:T(8,128)S(1)}, f32[4,16,128]{2,1,0:T(8,128)S(1)}, u32[]{:S(2)}, u32[]{:S(2)}) collective-permute-start(f32[4,16,128]{2,1,0:T(8,128)S(1)} %bitcast.311), channel_id=1, source_target_pairs={{0,1},{1,2},{2,3},{3,4},{4,5},{5,6},{6,7},{7,8},{8,9},{9,10},{10,1... | collective-permute-start | bytes 98312 | tf_op jit(solution)/shard_map/ppermute | solution.py:21
  151.5 4.8 %collective-permute-start.21 = (f32[4,16,128]{2,1,0:T(8,128)S(1)}, f32[4,16,128]{2,1,0:T(8,128)S(1)}, u32[]{:S(2)}, u32[]{:S(2)}) collective-permute-start(f32[4,16,128]{2,1,0:T(8,128)S(1)} %bitcast.312), channel_id=1, source_target_pairs={{0,1},{1,2},{2,3},{3,4},{4,5},{5,6},{6,7},{7,8},{8,9},{9,10},{10,1... | collective-permute-start | bytes 98312 | tf_op jit(solution)/shard_map/ppermute | solution.py:21
  161.6 5.0 %collective-permute-start.23 = (f32[4,16,128]{2,1,0:T(8,128)S(1)}, f32[4,16,128]{2,1,0:T(8,128)S(1)}, u32[]{:S(2)}, u32[]{:S(2)}) collective-permute-start(f32[4,16,128]{2,1,0:T(8,128)S(1)} %bitcast.313), channel_id=1, source_target_pairs={{0,1},{1,2},{2,3},{3,4},{4,5},{5,6},{6,7},{7,8},{8,9},{9,10},{10,1... | collective-permute-start | bytes 98312 | tf_op jit(solution)/shard_map/ppermute | solution.py:21
  172.0 5.6 %collective-permute-start.25 = (f32[4,16,128]{2,1,0:T(8,128)S(1)}, f32[4,16,128]{2,1,0:T(8,128)S(1)}, u32[]{:S(2)}, u32[]{:S(2)}) collective-permute-start(f32[4,16,128]{2,1,0:T(8,128)S(1)} %bitcast.314), channel_id=1, source_target_pairs={{0,1},{1,2},{2,3},{3,4},{4,5},{5,6},{6,7},{7,8},{8,9},{9,10},{10,1... | collective-permute-start | bytes 98312 | tf_op jit(solution)/shard_map/ppermute | solution.py:21
  182.9 4.8 %collective-permute-start.27 = (f32[4,16,128]{2,1,0:T(8,128)S(1)}, f32[4,16,128]{2,1,0:T(8,128)S(1)}, u32[]{:S(2)}, u32[]{:S(2)}) collective-permute-start(f32[4,16,128]{2,1,0:T(8,128)S(1)} %bitcast.315), channel_id=1, source_target_pairs={{0,1},{1,2},{2,3},{3,4},{4,5},{5,6},{6,7},{7,8},{8,9},{9,10},{10,1... | collective-permute-start | bytes 98312 | tf_op jit(solution)/shard_map/ppermute | solution.py:21
  193.0 5.0 %collective-permute-start.29 = (f32[4,16,128]{2,1,0:T(8,128)S(1)}, f32[4,16,128]{2,1,0:T(8,128)S(1)}, u32[]{:S(2)}, u32[]{:S(2)}) collective-permute-start(f32[4,16,128]{2,1,0:T(8,128)S(1)} %bitcast.316), channel_id=1, source_target_pairs={{0,1},{1,2},{2,3},{3,4},{4,5},{5,6},{6,7},{7,8},{8,9},{9,10},{10,1... | collective-permute-start | bytes 98312 | tf_op jit(solution)/shard_map/ppermute | solution.py:21
  203.4 5.6 %collective-permute-start.31 = (f32[4,16,128]{2,1,0:T(8,128)S(1)}, f32[4,16,128]{2,1,0:T(8,128)S(1)}, u32[]{:S(2)}, u32[]{:S(2)}) collective-permute-start(f32[4,16,128]{2,1,0:T(8,128)S(1)} %bitcast.317), channel_id=1, source_target_pairs={{0,1},{1,2},{2,3},{3,4},{4,5},{5,6},{6,7},{7,8},{8,9},{9,10},{10,1... | collective-permute-start | bytes 98312 | tf_op jit(solution)/shard_map/ppermute | solution.py:21
  213.1 38.0 %all_gather.9 = s32[16,1,2]{2,1,0:T(1,128)S(1)} all-gather(s32[1,1,2]{2,1,0:T(1,128)S(1)} %copy-done.7), channel_id=1, replica_groups=mesh['shot'=16,'dom'=32] {'shot'}, dimensions={0}, use_global_device_ids=true | all-gather | bytes 136 | tf_op jit(solution)/shard_map/all_gather | solution.py:91
  251.3 42.2 %all-gather.3.cloned.1.call-done = f32[32,8,8,128]{3,2,1,0:T(8,128)} async-done(((f32[2,8,8,128]{3,2,1,0:T(8,128)}), f32[32,8,8,128]{3,2,1,0:T(8,128)}) %all-gather.3.cloned.1.call-update) | async-done | bytes 1048592 | tf_op jit(solution)/shard_map/all_gather | solution.py:135
  (148 shorter events, 79.1 us)
Async XLA Ops:
  6.5 286.9 %all-gather.3.cloned.1.call-start = ((), (), s32[]{:S(2)}) async-start(), calls=%async_computation | async-start | bytes 1114112 | tf_op jit(solution)/shard_map/all_gather | solution.py:135
  7.3 55.8 %collective-permute-start.2 = (f32[4,16,128]{2,1,0:T(8,128)S(1)}, f32[4,16,128]{2,1,0:T(8,128)S(1)}, u32[]{:S(2)}, u32[]{:S(2)}) collective-permute-start(f32[4,16,128]{2,1,0:T(8,128)S(1)} %get-tuple-element.139), channel_id=1, source_target_pairs={{1,0},{2,1},{3,2},{4,3},{5,4},{6,5},{7,6},{8,7},{9,8},{10,9},{11,1... | collective-permute-start | bytes 98312 | tf_op jit(solution)/shard_map/ppermute | solution.py:23
  9.3 53.9 %collective-permute-start.3 = (f32[4,16,128]{2,1,0:T(8,128)S(1)}, f32[4,16,128]{2,1,0:T(8,128)S(1)}, u32[]{:S(2)}, u32[]{:S(2)}) collective-permute-start(f32[4,16,128]{2,1,0:T(8,128)S(1)} %get-tuple-element.140), channel_id=1, source_target_pairs={{0,1},{1,2},{2,3},{3,4},{4,5},{5,6},{6,7},{7,8},{8,9},{9,10},{10,1... | collective-permute-start | bytes 98312 | tf_op jit(solution)/shard_map/ppermute | solution.py:21
  64.6 11.0 %collective-permute-start.4 = (f32[4,16,128]{2,1,0:T(8,128)S(1)}, f32[4,16,128]{2,1,0:T(8,128)S(1)}, u32[]{:S(2)}, u32[]{:S(2)}) collective-permute-start(f32[4,16,128]{2,1,0:T(8,128)S(1)} %bitcast.304), channel_id=1, source_target_pairs={{1,0},{2,1},{3,2},{4,3},{5,4},{6,5},{7,6},{8,7},{9,8},{10,9},{11,1... | collective-permute-start | bytes 98312 | tf_op jit(solution)/shard_map/ppermute | solution.py:23
  66.7 8.9 %collective-permute-start.5 = (f32[4,16,128]{2,1,0:T(8,128)S(1)}, f32[4,16,128]{2,1,0:T(8,128)S(1)}, u32[]{:S(2)}, u32[]{:S(2)}) collective-permute-start(f32[4,16,128]{2,1,0:T(8,128)S(1)} %bitcast.300), channel_id=1, source_target_pairs={{0,1},{1,2},{2,3},{3,4},{4,5},{5,6},{6,7},{7,8},{8,9},{9,10},{10,1... | collective-permute-start | bytes 98312 | tf_op jit(solution)/shard_map/ppermute | solution.py:21
  69.1 37.5 %collective-permute-start = (f32[4,16,128]{2,1,0:T(8,128)S(1)}, f32[4,16,128]{2,1,0:T(8,128)S(1)}, u32[]{:S(2)}, u32[]{:S(2)}) collective-permute-start(f32[4,16,128]{2,1,0:T(8,128)S(1)} %get-tuple-element.141), channel_id=1, source_target_pairs={{1,0},{2,1},{3,2},{4,3},{5,4},{6,5},{7,6},{8,7},{9,8},{10,9},{11,1... | collective-permute-start | bytes 98312 | tf_op jit(solution)/shard_map/ppermute | solution.py:23
  72.3 34.3 %collective-permute-start.1 = (f32[4,16,128]{2,1,0:T(8,128)S(1)}, f32[4,16,128]{2,1,0:T(8,128)S(1)}, u32[]{:S(2)}, u32[]{:S(2)}) collective-permute-start(f32[4,16,128]{2,1,0:T(8,128)S(1)} %get-tuple-element.142), channel_id=1, source_target_pairs={{0,1},{1,2},{2,3},{3,4},{4,5},{5,6},{6,7},{7,8},{8,9},{9,10},{10,1... | collective-permute-start | bytes 98312 | tf_op jit(solution)/shard_map/ppermute | solution.py:21
  76.3 6.2 %collective-permute-start.6 = (f32[4,16,128]{2,1,0:T(8,128)S(1)}, f32[4,16,128]{2,1,0:T(8,128)S(1)}, u32[]{:S(2)}, u32[]{:S(2)}) collective-permute-start(f32[4,16,128]{2,1,0:T(8,128)S(1)} %bitcast.301), channel_id=1, source_target_pairs={{1,0},{2,1},{3,2},{4,3},{5,4},{6,5},{7,6},{8,7},{9,8},{10,9},{11,1... | collective-permute-start | bytes 98312 | tf_op jit(solution)/shard_map/ppermute | solution.py:23
  85.2 6.0 %collective-permute-start.8 = (f32[4,16,128]{2,1,0:T(8,128)S(1)}, f32[4,16,128]{2,1,0:T(8,128)S(1)}, u32[]{:S(2)}, u32[]{:S(2)}) collective-permute-start(f32[4,16,128]{2,1,0:T(8,128)S(1)} %bitcast.299), channel_id=1, source_target_pairs={{1,0},{2,1},{3,2},{4,3},{5,4},{6,5},{7,6},{8,7},{9,8},{10,9},{11,1... | collective-permute-start | bytes 98312 | tf_op jit(solution)/shard_map/ppermute | solution.py:23
  93.0 7.2 %collective-permute-start.10 = (f32[4,16,128]{2,1,0:T(8,128)S(1)}, f32[4,16,128]{2,1,0:T(8,128)S(1)}, u32[]{:S(2)}, u32[]{:S(2)}) collective-permute-start(f32[4,16,128]{2,1,0:T(8,128)S(1)} %bitcast.305), channel_id=1, source_target_pairs={{1,0},{2,1},{3,2},{4,3},{5,4},{6,5},{7,6},{8,7},{9,8},{10,9},{11,1... | collective-permute-start | bytes 98312 | tf_op jit(solution)/shard_map/ppermute | solution.py:23
  109.8 6.6 %collective-permute-start.14 = (f32[4,16,128]{2,1,0:T(8,128)S(1)}, f32[4,16,128]{2,1,0:T(8,128)S(1)}, u32[]{:S(2)}, u32[]{:S(2)}) collective-permute-start(f32[4,16,128]{2,1,0:T(8,128)S(1)} %bitcast.310), channel_id=1, source_target_pairs={{1,0},{2,1},{3,2},{4,3},{5,4},{6,5},{7,6},{8,7},{9,8},{10,9},{11,1... | collective-permute-start | bytes 98312 | tf_op jit(solution)/shard_map/ppermute | solution.py:23
  117.9 16.3 %collective-permute-start.16 = (f32[4,16,128]{2,1,0:T(8,128)S(1)}, f32[4,16,128]{2,1,0:T(8,128)S(1)}, u32[]{:S(2)}, u32[]{:S(2)}) collective-permute-start(f32[4,16,128]{2,1,0:T(8,128)S(1)} %bitcast.307), channel_id=1, source_target_pairs={{1,0},{2,1},{3,2},{4,3},{5,4},{6,5},{7,6},{8,7},{9,8},{10,9},{11,1... | collective-permute-start | bytes 98312 | tf_op jit(solution)/shard_map/ppermute | solution.py:23
  120.3 13.8 %collective-permute-start.17 = (f32[4,16,128]{2,1,0:T(8,128)S(1)}, f32[4,16,128]{2,1,0:T(8,128)S(1)}, u32[]{:S(2)}, u32[]{:S(2)}) collective-permute-start(f32[4,16,128]{2,1,0:T(8,128)S(1)} %bitcast.303), channel_id=1, source_target_pairs={{0,1},{1,2},{2,3},{3,4},{4,5},{5,6},{6,7},{7,8},{8,9},{9,10},{10,1... | collective-permute-start | bytes 98312 | tf_op jit(solution)/shard_map/ppermute | solution.py:21
  138.6 7.7 %collective-permute-start.18 = (f32[4,16,128]{2,1,0:T(8,128)S(1)}, f32[4,16,128]{2,1,0:T(8,128)S(1)}, u32[]{:S(2)}, u32[]{:S(2)}) collective-permute-start(f32[4,16,128]{2,1,0:T(8,128)S(1)} %bitcast.318), channel_id=1, source_target_pairs={{1,0},{2,1},{3,2},{4,3},{5,4},{6,5},{7,6},{8,7},{9,8},{10,9},{11,1... | collective-permute-start | bytes 98312 | tf_op jit(solution)/shard_map/ppermute | solution.py:23
  140.8 6.2 %collective-permute-start.19 = (f32[4,16,128]{2,1,0:T(8,128)S(1)}, f32[4,16,128]{2,1,0:T(8,128)S(1)}, u32[]{:S(2)}, u32[]{:S(2)}) collective-permute-start(f32[4,16,128]{2,1,0:T(8,128)S(1)} %bitcast.311), channel_id=1, source_target_pairs={{0,1},{1,2},{2,3},{3,4},{4,5},{5,6},{6,7},{7,8},{8,9},{9,10},{10,1... | collective-permute-start | bytes 98312 | tf_op jit(solution)/shard_map/ppermute | solution.py:21
  149.5 6.8 %collective-permute-start.20 = (f32[4,16,128]{2,1,0:T(8,128)S(1)}, f32[4,16,128]{2,1,0:T(8,128)S(1)}, u32[]{:S(2)}, u32[]{:S(2)}) collective-permute-start(f32[4,16,128]{2,1,0:T(8,128)S(1)} %bitcast.319), channel_id=1, source_target_pairs={{1,0},{2,1},{3,2},{4,3},{5,4},{6,5},{7,6},{8,7},{9,8},{10,9},{11,1... | collective-permute-start | bytes 98312 | tf_op jit(solution)/shard_map/ppermute | solution.py:23
  159.7 7.0 %collective-permute-start.22 = (f32[4,16,128]{2,1,0:T(8,128)S(1)}, f32[4,16,128]{2,1,0:T(8,128)S(1)}, u32[]{:S(2)}, u32[]{:S(2)}) collective-permute-start(f32[4,16,128]{2,1,0:T(8,128)S(1)} %bitcast.320), channel_id=1, source_target_pairs={{1,0},{2,1},{3,2},{4,3},{5,4},{6,5},{7,6},{8,7},{9,8},{10,9},{11,1... | collective-permute-start | bytes 98312 | tf_op jit(solution)/shard_map/ppermute | solution.py:23
  161.6 5.9 %collective-permute-start.23 = (f32[4,16,128]{2,1,0:T(8,128)S(1)}, f32[4,16,128]{2,1,0:T(8,128)S(1)}, u32[]{:S(2)}, u32[]{:S(2)}) collective-permute-start(f32[4,16,128]{2,1,0:T(8,128)S(1)} %bitcast.313), channel_id=1, source_target_pairs={{0,1},{1,2},{2,3},{3,4},{4,5},{5,6},{6,7},{7,8},{8,9},{9,10},{10,1... | collective-permute-start | bytes 98312 | tf_op jit(solution)/shard_map/ppermute | solution.py:21
  170.0 7.5 %collective-permute-start.24 = (f32[4,16,128]{2,1,0:T(8,128)S(1)}, f32[4,16,128]{2,1,0:T(8,128)S(1)}, u32[]{:S(2)}, u32[]{:S(2)}) collective-permute-start(f32[4,16,128]{2,1,0:T(8,128)S(1)} %bitcast.321), channel_id=1, source_target_pairs={{1,0},{2,1},{3,2},{4,3},{5,4},{6,5},{7,6},{8,7},{9,8},{10,9},{11,1... | collective-permute-start | bytes 98312 | tf_op jit(solution)/shard_map/ppermute | solution.py:23
  172.0 6.4 %collective-permute-start.25 = (f32[4,16,128]{2,1,0:T(8,128)S(1)}, f32[4,16,128]{2,1,0:T(8,128)S(1)}, u32[]{:S(2)}, u32[]{:S(2)}) collective-permute-start(f32[4,16,128]{2,1,0:T(8,128)S(1)} %bitcast.314), channel_id=1, source_target_pairs={{0,1},{1,2},{2,3},{3,4},{4,5},{5,6},{6,7},{7,8},{8,9},{9,10},{10,1... | collective-permute-start | bytes 98312 | tf_op jit(solution)/shard_map/ppermute | solution.py:21
  180.9 6.8 %collective-permute-start.26 = (f32[4,16,128]{2,1,0:T(8,128)S(1)}, f32[4,16,128]{2,1,0:T(8,128)S(1)}, u32[]{:S(2)}, u32[]{:S(2)}) collective-permute-start(f32[4,16,128]{2,1,0:T(8,128)S(1)} %bitcast.322), channel_id=1, source_target_pairs={{1,0},{2,1},{3,2},{4,3},{5,4},{6,5},{7,6},{8,7},{9,8},{10,9},{11,1... | collective-permute-start | bytes 98312 | tf_op jit(solution)/shard_map/ppermute | solution.py:23
  191.1 6.9 %collective-permute-start.28 = (f32[4,16,128]{2,1,0:T(8,128)S(1)}, f32[4,16,128]{2,1,0:T(8,128)S(1)}, u32[]{:S(2)}, u32[]{:S(2)}) collective-permute-start(f32[4,16,128]{2,1,0:T(8,128)S(1)} %bitcast.323), channel_id=1, source_target_pairs={{1,0},{2,1},{3,2},{4,3},{5,4},{6,5},{7,6},{8,7},{9,8},{10,9},{11,1... | collective-permute-start | bytes 98312 | tf_op jit(solution)/shard_map/ppermute | solution.py:23
  201.4 7.5 %collective-permute-start.30 = (f32[4,16,128]{2,1,0:T(8,128)S(1)}, f32[4,16,128]{2,1,0:T(8,128)S(1)}, u32[]{:S(2)}, u32[]{:S(2)}) collective-permute-start(f32[4,16,128]{2,1,0:T(8,128)S(1)} %bitcast.324), channel_id=1, source_target_pairs={{1,0},{2,1},{3,2},{4,3},{5,4},{6,5},{7,6},{8,7},{9,8},{10,9},{11,1... | collective-permute-start | bytes 98312 | tf_op jit(solution)/shard_map/ppermute | solution.py:23
  203.4 6.4 %collective-permute-start.31 = (f32[4,16,128]{2,1,0:T(8,128)S(1)}, f32[4,16,128]{2,1,0:T(8,128)S(1)}, u32[]{:S(2)}, u32[]{:S(2)}) collective-permute-start(f32[4,16,128]{2,1,0:T(8,128)S(1)} %bitcast.317), channel_id=1, source_target_pairs={{0,1},{1,2},{2,3},{3,4},{4,5},{5,6},{6,7},{7,8},{8,9},{9,10},{10,1... | collective-permute-start | bytes 98312 | tf_op jit(solution)/shard_map/ppermute | solution.py:21
  (17 other events, 172.4 us)
Sparse Core Ops, SparseCore 0:
  213.2 80.1 all-gather.2
where the time goes:
time: 304 us; the launch traced here: 302 us
  starting transfers between devices  95.1 us (31%)
  blocking collectives  86.5 us (28%)
  waiting for transfers between devices  54.1 us (18%)
  other arithmetic  28.6 us (9%)
  between operations  20.7 us (7%)
  local copies, waits for them, and re-layouts  17.3 us (6%)
    ppermute x16, starting transfers between devices, with_halo(): lax.ppermute(tail, axis, [(i, (i + 1) % count) for i in range(ends)])  60.1 us
    all_gather x1, blocking collectives, body(): portion = lax.all_gather(velocity, 'shot', axis=0, tiled=True)  48.5 us
    all_gather x1, waiting for transfers between devices, body(): portion = lax.all_gather(term_tiles[None], 'shot', axis=0, tiled=True)  42.2 us
    all_gather x1, blocking collectives, body(): lists = lax.all_gather(aperture, 'shot', axis=0, tiled=True)  38 us
    ppermute x16, starting transfers between devices, with_halo(): lax.ppermute(head, axis, [((i + 1) % count, i) for i in range(ends)])  35 us
    scatter-add x8, other arithmetic, body(): earlier.reshape(-1).at[receiver_clipped].add(misfits[moment])  16.1 us
    gather x8, local copies, waits for them, and re-layouts, body(): sampled = forward_fields[moment + 1].reshape(-1)[receiver_clipped]  13.8 us
    ppermute x16, waiting for transfers between devices, with_halo(): lax.ppermute(tail, axis, [(i, (i + 1) % count) for i in range(ends)])  11.8 us
  transfers between devices with their start and end apart: 33, of which 13 were waited for; matrix products, arithmetic and copies ran while one was open for 6% of the time, Pallas kernels for 0%

commit v1 on v0

v1 whole, which is shorter than its diff:
```python
import jax
import jax.numpy as jnp
from jax import lax
from jax.experimental import pallas as pl
from jax.experimental.pallas import tpu as pltpu
from jax.sharding import Mesh, PartitionSpec as P

STEPS = 8
STENCIL_WEIGHTS = (-205.0 / 72.0, 8.0 / 5.0, -1.0 / 5.0, 8.0 / 315.0, -1.0 / 560.0)
STEP_SCALE = 0.088
DOM = ("yl", "z", "c")
SHOT = ("x", "yh")
SLABS = 32
TX, AY, TZ = 8, 16, 128
PLANES = 9 * TX
OWN = 4 * TX
PAD = 8
NREC = 256


def laplace_plane(field, cur, p, lane):
    middle = field[cur, p, PAD : PAD + AY, :]
    acc = (3.0 * STENCIL_WEIGHTS[0]) * middle
    for s in range(1, 5):
        near = field[cur, p + s, PAD : PAD + AY, :] + field[cur, p - s, PAD : PAD + AY, :]
        near = near + field[cur, p, PAD + s : PAD + AY + s, :] + field[cur, p, PAD - s : PAD + AY - s, :]
        near = near + jnp.where(lane < TZ - s, pltpu.roll(middle, TZ - s, 1), 0.0)
        near = near + jnp.where(lane >= s, pltpu.roll(middle, s, 1), 0.0)
        acc = acc + STENCIL_WEIGHTS[s] * near
    return middle, acc


def assemble(field, which, item, slab, own, left, right, far_left, far_right):
    pieces = [far_left[k, item] for k in range(3)] + [left[item], own[item], right[item]] + [far_right[k, item] for k in range(3)]
    for j in range(9):
        there = slab + (j - 4)
        inside = (there >= 0) & (there < SLABS)
        field[which, TX * j : TX * (j + 1), PAD : PAD + AY, :] = jnp.where(inside, pieces[j], 0.0)


def clear_pads(field):
    zero = jnp.zeros((PLANES, PAD, TZ), jnp.float32)
    for b in range(2):
        field[b, :, 0:PAD, :] = zero
        field[b, :, PAD + AY : PAD + AY + PAD, :] = zero


def split3(x):
    high = x.astype(jnp.bfloat16)
    rest = x - high.astype(jnp.float32)
    mid = rest.astype(jnp.bfloat16)
    low = (rest - mid.astype(jnp.float32)).astype(jnp.bfloat16)
    return high, mid, low


def forward_kernel(
    aperture, source, checkpoint, wavelet, observed, receivers,
    own, left, right, far_left, far_right,
    vel, vel_left, vel_right, vel_far_left, vel_far_right,
    curvature, misfit, courant,
    field, update, samples,
):
    slab = aperture[0, 0, 0] & (SLABS - 1)
    clear_pads(field)
    for item in range(2):
        assemble(field, item, item, slab, own, left, right, far_left, far_right)
    tiles = (
        [(vel_far_left, k) for k in range(3)] + [(vel_left, None), (vel, None), (vel_right, None)] + [(vel_far_right, k) for k in range(3)]
    )
    for j in range(9):
        there = slab + (j - 4)
        inside = (there >= 0) & (there < SLABS)
        ref, k = tiles[j]
        for row in range(2):
            speed = ref[row] if k is None else ref[k, row]
            speed = jnp.where(inside, STEP_SCALE * speed, 0.0)
            courant[TX * j : TX * (j + 1), 8 * row : 8 * row + 8, :] = speed * speed

    lane = lax.broadcasted_iota(jnp.int32, (AY, TZ), 1)
    suby = lax.broadcasted_iota(jnp.int32, (AY, TZ), 0)
    cell = source[0]
    source_x = (cell >> 11) - (slab - 4) * TX
    source_here = (source_x >= 0) & (source_x < PLANES)
    source_own = (source_x >= OWN) & (source_x < OWN + TX)
    spot = (suby == ((cell >> 7) & 15)) & (lane == (cell & 127))
    start = checkpoint[0]

    def step(n, _):
        prev = n & 1
        cur = 1 - prev

        def planes(b, _):
            for q in range(4):
                p = 4 * b + q
                middle, acc = laplace_plane(field, cur, p, lane)
                change = courant[p] * acc
                update[p] = change
                field[prev, p, PAD : PAD + AY, :] = 2.0 * middle - field[prev, p, PAD : PAD + AY, :] + change
            return 0

        lax.fori_loop(1 + n, 17 - n, planes, 0)
        pulse = jnp.where(spot, wavelet[0, start + n], 0.0)

        @pl.when(source_here)
        def _():
            field[prev, source_x, PAD : PAD + AY, :] = field[prev, source_x, PAD : PAD + AY, :] + pulse

        @pl.when(source_own)
        def _():
            update[source_x] = update[source_x] + pulse

        curvature[n] = update[OWN : OWN + TX]
        samples[n] = field[prev, OWN : OWN + TX, PAD : PAD + AY, :].reshape(TX * AY, TZ)
        return 0

    lax.fori_loop(0, STEPS, step, 0)

    spots = receivers[...]
    row = (spots >> 7) - slab * (TX * AY)
    rows = lax.broadcasted_iota(jnp.int32, (TX * AY, NREC), 0)
    at_row = jnp.where(rows == row, 1.0, 0.0)
    at_lane = jnp.where(rows == (spots & 127), 1.0, 0.0).astype(jnp.bfloat16)
    here = (row >= 0) & (row < TX * AY)
    taken = []
    for n in range(STEPS):
        total = None
        for part in split3(samples[n]):
            product = jnp.dot(part, at_lane, preferred_element_type=jnp.float32)
            total = product if total is None else total + product
        recorded = observed[0, pl.ds(start + n, 1), :]
        taken.append(jnp.sum(total * at_row, axis=0, keepdims=True) - jnp.where(here, recorded, 0.0))
    misfit[...] = jnp.concatenate(taken, axis=0)


def adjoint_kernel(
    aperture, receivers, misfit_near, misfit_left, misfit_right,
    own, left, right, far_left, far_right,
    vel, courant, curvature,
    out,
    field, injected, image,
):
    slab = aperture[0, 0, 0] & (SLABS - 1)
    first_row = aperture[0, 0, 0] >> 5
    clear_pads(field)
    for item in range(2):
        assemble(field, item, item, slab, own, left, right, far_left, far_right)
    lane = lax.broadcasted_iota(jnp.int32, (AY, TZ), 1)
    misfit = misfit_near[...] + misfit_left[...] + misfit_right[...]
    spots = receivers[...]
    row = (spots >> 7) - (slab - 4) * (TX * AY)
    rows = lax.broadcasted_iota(jnp.int32, (PLANES * AY, NREC), 0)
    at_row = jnp.where(rows == row, 1.0, 0.0).astype(jnp.bfloat16)
    at_lane = rows[0:TZ] == (spots & 127)
    image[...] = jnp.zeros((TX, AY, TZ), jnp.float32)
    for i in range(STEPS):
        n = STEPS - i
        prev, cur = i & 1, 1 - (i & 1)
        low, high = 4 + 4 * i, PLANES - 4 - 4 * i
        parts = [jnp.where(at_lane, part.astype(jnp.float32), 0.0).astype(jnp.bfloat16) for part in split3(misfit[n - 1 : n])]
        total = None
        for part in parts:
            product = lax.dot_general(
                at_row[low * AY : high * AY], part, (((1,), (1,)), ((), ())), preferred_element_type=jnp.float32
            )
            total = product if total is None else total + product
        injected[low:high] = total.reshape(high - low, AY, TZ)

        def planes(b, _, prev=prev, cur=cur):
            for q in range(4):
                p = 4 * b + q
                middle, acc = laplace_plane(field, cur, p, lane)
                field[prev, p, PAD : PAD + AY, :] = (
                    2.0 * middle - field[prev, p, PAD : PAD + AY, :] + courant[p] * acc + injected[p]
                )
            return 0

        lax.fori_loop(low // 4, high // 4, planes, 0)
        image[...] += field[prev, OWN : OWN + TX, PAD : PAD + AY, :] * curvature[n - 1]
    out[...] = jnp.zeros(out.shape, jnp.float32)
    for k in range(2):
        speed = vel[k]
        out[first_row + k] = 2.0 / (speed * speed * speed) * image[:, 8 * k : 8 * k + 8, :]


def whole(shape):
    return pl.BlockSpec(shape, lambda i: (0,) * len(shape))


def pair(shape, which):
    place = len(shape) - 4
    return pl.BlockSpec(shape, lambda i: tuple(which if k == place else 0 for k in range(len(shape))))


def scalars(shape):
    return pl.BlockSpec(shape, lambda i: (0,) * len(shape), memory_space=pltpu.SMEM)


def fields_specs(which):
    near, far = (2, TX, AY, TZ), (3, 2, TX, AY, TZ)
    return [pair(near, which)] * 3 + [pair(far, which)] * 2


def body(
    velocity,
    aperture,
    source_cell,
    wavelet,
    observed,
    receivers,
    checkpoint,
    forward_previous,
    forward_current,
    adjoint_next,
    adjoint_current,
):
    def shift(cells, by):
        return lax.ppermute(cells, DOM, [(i, (i + by) % SLABS) for i in range(SLABS)])

    fields = jnp.concatenate([forward_previous, forward_current, adjoint_next, adjoint_current], axis=0)
    left, right = shift(fields, 1), shift(fields, -1)

    column = lax.all_to_all(jnp.broadcast_to(velocity, (4,) + velocity.shape[1:]), "yh", 0, 0, tiled=True)

    packed = jnp.stack([left, fields, right])
    far_left, far_right = shift(packed, 3), shift(packed, -3)

    rows = lax.all_to_all(jnp.broadcast_to(column[None], (4,) + column.shape), "x", 0, 0, tiled=True)
    rows = rows.reshape((16,) + velocity.shape[1:])
    vel = lax.dynamic_slice_in_dim(rows, aperture[0, 0, 0] // SLABS, 2, 0)
    vel_left, vel_right = shift(vel, 1), shift(vel, -1)
    vel_packed = jnp.stack([vel_left, vel, vel_right])
    vel_far_left, vel_far_right = shift(vel_packed, 3), shift(vel_packed, -3)

    tile, tiles = (2, TX, 8, TZ), (3, 2, TX, 8, TZ)
    slab_steps = (STEPS, TX, AY, TZ)
    region = (PLANES, AY, TZ)
    f32 = jnp.float32
    curvature, misfit, courant = pl.pallas_call(
        forward_kernel,
        grid=(1,),
        in_specs=[scalars((1, 1, 2)), scalars((1,)), scalars((1,)), scalars((1, 64)), whole((1, 64, NREC)), whole((1, NREC))]
        + fields_specs(0)
        + [whole(tile)] * 3
        + [whole(tiles)] * 2,
        out_specs=[whole(slab_steps), whole((STEPS, NREC)), whole(region)],
        out_shape=[
            jax.ShapeDtypeStruct(slab_steps, f32),
            jax.ShapeDtypeStruct((STEPS, NREC), f32),
            jax.ShapeDtypeStruct(region, f32),
        ],
        scratch_shapes=[
            pltpu.VMEM((2, PLANES, AY + 2 * PAD, TZ), f32),
            pltpu.VMEM(region, f32),
            pltpu.VMEM((STEPS, TX * AY, TZ), f32),
        ],
        name="forward",
    )(
        aperture, source_cell, checkpoint, wavelet, observed, receivers,
        fields, left, right, far_left, far_right,
        vel, vel_left, vel_right, vel_far_left, vel_far_right,
    )

    near = misfit + shift(misfit, 1) + shift(misfit, -1)
    misfit_left, misfit_right = shift(near, 3), shift(near, -3)

    slots = (16, TX, 8, TZ)
    terms = pl.pallas_call(
        adjoint_kernel,
        grid=(1,),
        in_specs=[scalars((1, 1, 2)), whole((1, NREC))]
        + [whole((STEPS, NREC))] * 3
        + fields_specs(1)
        + [whole(tile), whole(region), whole(slab_steps)],
        out_specs=whole(slots),
        out_shape=jax.ShapeDtypeStruct(slots, f32),
        scratch_shapes=[
            pltpu.VMEM((2, PLANES, AY + 2 * PAD, TZ), f32),
            pltpu.VMEM(region, f32),
            pltpu.VMEM((TX, AY, TZ), f32),
        ],
        name="adjoint",
    )(
        aperture, receivers, near, misfit_left, misfit_right,
        fields, left, right, far_left, far_right,
        vel, courant, curvature,
    )
    landed = lax.all_to_all(terms, SHOT, 0, 0, tiled=True)
    return jnp.sum(landed, axis=0, keepdims=True)


def solution(mesh):
    split = Mesh(mesh.devices.reshape(4, 4, 2, 8, 2), SHOT + DOM)
    placed = (
        P(SHOT + DOM, None, None, None),
        P(SHOT, DOM, None),
        P(SHOT),
        P(SHOT, None),
        P(SHOT, None, None),
        P(SHOT, None),
        P(SHOT),
        P(SHOT, DOM, None, None),
        P(SHOT, DOM, None, None),
        P(SHOT, DOM, None, None),
        P(SHOT, DOM, None, None),
    )
    return jax.shard_map(
        body,
        mesh=split,
        in_specs=placed,
        out_specs=P(SHOT + DOM, None, None, None),
        check_vma=False,
    )
```

time: 304 us -> 178 us (0.59)
  the two profiles are of different devices: /device:TPU:64 before, /device:TPU:72 now
where the time goes in v1:
time: 178 us; the launch traced here: 177 us
  starting transfers between devices  49.2 us (28%)
  Pallas kernels  47 us (26%)
  blocking collectives  36.7 us (21%)
  waiting for transfers between devices  33.2 us (19%)
  local copies, waits for them, and re-layouts  7.91 us (4%)
    ppermute x12, starting transfers between devices, shift(): lax.ppermute(cells, DOM, [(i, (i + by) % SLABS) for i in range(SLABS)])  44.9 us
    ppermute x12, waiting for transfers between devices, shift(): lax.ppermute(cells, DOM, [(i, (i + by) % SLABS) for i in range(SLABS)])  33.1 us
    pallas_call x1, Pallas kernels, body(): pl.pallas_call(forward_kernel, grid=(1,), in_specs=[scalars((1, 1, 2)), s...  29.2 us
    all_to_all x1, blocking collectives, body(): landed = lax.all_to_all(terms, SHOT, 0, 0, tiled=True)  22.1 us
    pallas_call x1, Pallas kernels, body(): pl.pallas_call(adjoint_kernel, grid=(1,), in_specs=[scalars((1, 1, 2)), w...  17.9 us
    all_to_all x1, blocking collectives, body(): lax.all_to_all(jnp.broadcast_to(velocity, (4,) + velocity.shape[1:]), 'yh...  14.6 us
    unnamed x39, local copies, waits for them, and re-layouts  6.99 us
    all_to_all x1, starting transfers between devices, body(): lax.all_to_all(jnp.broadcast_to(column[None], (4,) + column.shape), 'x',...  4.29 us
  transfers between devices with their start and end apart: 13, of which 5 were waited for; matrix products, arithmetic and copies ran while one was open for 1% of the time, Pallas kernels for 0%

profile of v1, /device:TPU:72, one launch (start us, length us, event | category | flops | bytes accessed | tf_op | source)
XLA Modules:
  0.0 177.1 jit_solution(17446849176017771730)
XLA Ops:
  2.6 1.9 %collective-permute-start.1 = (f32[4,8,16,128]{3,2,1,0:T(8,128)S(1)}, f32[4,8,16,128]{3,2,1,0:T(8,128)S(1)}, u32[]{:S(2)}, u32[]{:S(2)}) collective-permute-start(f32[4,8,16,128]{3,2,1,0:T(8,128)S(1)} %constant_dynamic-update-slice_fusion.own), channel_id=1, source_target_pairs={{0,31},{1,0},{2,1},{3,2},{4,3},{5,4},{6,5},{7,6},{8,7},{9,8},{10,9... | collective-permute-start | bytes 786440 | tf_op jit(solution)/shard_map/ppermute | solution.py:217
  4.5 2.4 %collective-permute-start = (f32[4,8,16,128]{3,2,1,0:T(8,128)S(1)}, f32[4,8,16,128]{3,2,1,0:T(8,128)S(1)}, u32[]{:S(2)}, u32[]{:S(2)}) collective-permute-start(f32[4,8,16,128]{3,2,1,0:T(8,128)S(1)} %constant_dynamic-update-slice_fusion.own), channel_id=1, source_target_pairs={{0,1},{1,2},{2,3},{3,4},{4,5},{5,6},{6,7},{7,8},{8,9},{9,10},{10,1... | collective-permute-start | bytes 786440 | tf_op jit(solution)/shard_map/ppermute | solution.py:217
  6.9 14.6 %all_to_all.15 = f32[4,8,8,128]{3,2,1,0:T(8,128)S(1)} all-to-all(f32[4,8,8,128]{3,2,1,0:T(8,128)S(1)} %broadcast_in_dim.17), channel_id=1, replica_groups=mesh['x'=4,'yh'=4,'yl'=2,'z'=8,'c'=2] {'yh'}, dimensions={0} | all-to-all | bytes 262144 | tf_op jit(solution)/shard_map/all_to_all | solution.py:222
  21.5 0.9 broadcast_in_dim.18
  22.4 4.3 %all-to-all-start.1 = ((f32[4,4,8,8,128]{4,3,2,1,0:T(8,128)}), f32[4,4,8,8,128]{4,3,2,1,0:T(8,128)S(1)}, u32[]{:S(2)}, u32[]{:S(2)}) async-start(f32[4,4,8,8,128]{4,3,2,1,0:T(8,128)} %broadcast_in_dim.18), calls=%async_computation.1 | async-start | bytes 1048576 | tf_op jit(solution)/shard_map/all_to_all | solution.py:227
  27.5 11.7 %collective-permute-start.3 = (f32[3,4,8,16,128]{4,3,2,1,0:T(8,128)S(1)}, f32[3,4,8,16,128]{4,3,2,1,0:T(8,128)S(1)}, u32[]{:S(2)}, u32[]{:S(2)}) collective-permute-start(f32[3,4,8,16,128]{4,3,2,1,0:T(8,128)S(1)} %pad_maximum_fusion), channel_id=1, source_target_pairs={{0,29},{1,30},{2,31},{3,0},{4,1},{5,2},{6,3},{7,4},{8,5},{9,6},{10... | collective-permute-start | bytes 2359304 | tf_op jit(solution)/shard_map/ppermute | solution.py:217
  39.2 1.9 %collective-permute-start.2 = (f32[3,4,8,16,128]{4,3,2,1,0:T(8,128)S(1)}, f32[3,4,8,16,128]{4,3,2,1,0:T(8,128)S(1)}, u32[]{:S(2)}, u32[]{:S(2)}) collective-permute-start(f32[3,4,8,16,128]{4,3,2,1,0:T(8,128)S(1)} %pad_maximum_fusion), channel_id=1, source_target_pairs={{0,3},{1,4},{2,5},{3,6},{4,7},{5,8},{6,9},{7,10},{8,11},{9,12},{10... | collective-permute-start | bytes 2359304 | tf_op jit(solution)/shard_map/ppermute | solution.py:217
  42.0 1.9 %collective-permute-start.5 = (f32[2,8,8,128]{3,2,1,0:T(8,128)S(1)}, f32[2,8,8,128]{3,2,1,0:T(8,128)S(1)}, u32[]{:S(2)}, u32[]{:S(2)}) collective-permute-start(f32[2,8,8,128]{3,2,1,0:T(8,128)S(1)} %constant_dynamic-slice_fusion.vel), channel_id=1, source_target_pairs={{0,31},{1,0},{2,1},{3,2},{4,3},{5,4},{6,5},{7,6},{8,7},{9,8},{10,9... | collective-permute-start | bytes 196616 | tf_op jit(solution)/shard_map/ppermute | solution.py:217
  43.9 2.4 %collective-permute-start.4 = (f32[2,8,8,128]{3,2,1,0:T(8,128)S(1)}, f32[2,8,8,128]{3,2,1,0:T(8,128)S(1)}, u32[]{:S(2)}, u32[]{:S(2)}) collective-permute-start(f32[2,8,8,128]{3,2,1,0:T(8,128)S(1)} %constant_dynamic-slice_fusion.vel), channel_id=1, source_target_pairs={{0,1},{1,2},{2,3},{3,4},{4,5},{5,6},{6,7},{7,8},{8,9},{9,10},{10,1... | collective-permute-start | bytes 196616 | tf_op jit(solution)/shard_map/ppermute | solution.py:217
  46.4 7.9 %collective-permute-done.5.vel_right = f32[2,8,8,128]{3,2,1,0:T(8,128)S(1)} collective-permute-done((f32[2,8,8,128]{3,2,1,0:T(8,128)S(1)}, f32[2,8,8,128]{3,2,1,0:T(8,128)S(1)}, u32[]{:S(2)}, u32[]{:S(2)}) %collective-permute-start.5) | collective-permute-done | bytes 65568 | tf_op jit(solution)/shard_map/ppermute | solution.py:217
  54.3 8.3 %collective-permute-done.4.vel_left = f32[2,8,8,128]{3,2,1,0:T(8,128)S(1)} collective-permute-done((f32[2,8,8,128]{3,2,1,0:T(8,128)S(1)}, f32[2,8,8,128]{3,2,1,0:T(8,128)S(1)}, u32[]{:S(2)}, u32[]{:S(2)}) %collective-permute-start.4) | collective-permute-done | bytes 65568 | tf_op jit(solution)/shard_map/ppermute | solution.py:217
  63.2 10.3 %collective-permute-start.7 = (f32[3,2,8,8,128]{4,3,2,1,0:T(8,128)S(1)}, f32[3,2,8,8,128]{4,3,2,1,0:T(8,128)S(1)}, u32[]{:S(2)}, u32[]{:S(2)}) collective-permute-start(f32[3,2,8,8,128]{4,3,2,1,0:T(8,128)S(1)} %pad_maximum_fusion.1), channel_id=1, source_target_pairs={{0,29},{1,30},{2,31},{3,0},{4,1},{5,2},{6,3},{7,4},{8,5},{9,6},{10... | collective-permute-start | bytes 589832 | tf_op jit(solution)/shard_map/ppermute | solution.py:217
  73.5 1.9 %collective-permute-start.6 = (f32[3,2,8,8,128]{4,3,2,1,0:T(8,128)S(1)}, f32[3,2,8,8,128]{4,3,2,1,0:T(8,128)S(1)}, u32[]{:S(2)}, u32[]{:S(2)}) collective-permute-start(f32[3,2,8,8,128]{4,3,2,1,0:T(8,128)S(1)} %pad_maximum_fusion.1), channel_id=1, source_target_pairs={{0,3},{1,4},{2,5},{3,6},{4,7},{5,8},{6,9},{7,10},{8,11},{9,12},{10... | collective-permute-start | bytes 589832 | tf_op jit(solution)/shard_map/ppermute | solution.py:217
  76.7 8.2 %collective-permute-done.6.vel_far_left = f32[3,2,8,8,128]{4,3,2,1,0:T(8,128)S(1)} collective-permute-done((f32[3,2,8,8,128]{4,3,2,1,0:T(8,128)S(1)}, f32[3,2,8,8,128]{4,3,2,1,0:T(8,128)S(1)}, u32[]{:S(2)}, u32[]{:S(2)}) %collective-permute-start.6) | collective-permute-done | bytes 196640 | tf_op jit(solution)/shard_map/ppermute | solution.py:217
  85.9 0.9 copy-done.1
  86.8 29.2 %forward.1 = (f32[8,8,16,128]{3,2,1,0:T(8,128)}, f32[8,256]{1,0:T(8,128)}, f32[72,16,128]{2,1,0:T(8,128)}) custom-call(s32[1,1,2]{2,1,0:T(1,128)} %aperture.3, s32[1]{0:T(128)S(6)} %copy.15.source, s32[1]{0:T(128)S(6)} %copy.16.checkpoint, f32[1,64]{1,0:T(1,128)} %wavelet.1, f32[1,64,256]{2,1,0:T(8,128)} %observed.1, s32[1,256]{1,0:T(1,128)} %receivers.3, ...), custom_call_target="tpu_custom_call" | custom-call | tf_op jit(solution)/shard_map/forward/pallas_call | solution.py:238
  115.9 1.9 %collective-permute-start.9 = (f32[8,256]{1,0:T(8,128)}, f32[8,256]{1,0:T(8,128)S(1)}, u32[]{:S(2)}, u32[]{:S(2)}) collective-permute-start(f32[8,256]{1,0:T(8,128)} %get-tuple-element.8), channel_id=1, source_target_pairs={{0,31},{1,0},{2,1},{3,2},{4,3},{5,4},{6,5},{7,6},{8,7},{9,8},{10,9... | collective-permute-start | bytes 24584 | tf_op jit(solution)/shard_map/ppermute | solution.py:217
  117.8 2.4 %collective-permute-start.8 = (f32[8,256]{1,0:T(8,128)}, f32[8,256]{1,0:T(8,128)S(1)}, u32[]{:S(2)}, u32[]{:S(2)}) collective-permute-start(f32[8,256]{1,0:T(8,128)} %get-tuple-element.8), channel_id=1, source_target_pairs={{0,1},{1,2},{2,3},{3,4},{4,5},{5,6},{6,7},{7,8},{8,9},{9,10},{10,1... | collective-permute-start | bytes 24584 | tf_op jit(solution)/shard_map/ppermute | solution.py:217
  120.3 2.8 %collective-permute-done.8 = f32[8,256]{1,0:T(8,128)S(1)} collective-permute-done((f32[8,256]{1,0:T(8,128)}, f32[8,256]{1,0:T(8,128)S(1)}, u32[]{:S(2)}, u32[]{:S(2)}) %collective-permute-start.8) | collective-permute-done | bytes 8224 | tf_op jit(solution)/shard_map/ppermute | solution.py:217
  123.7 4.2 %collective-permute-start.11 = (f32[8,256]{1,0:T(8,128)S(1)}, f32[8,256]{1,0:T(8,128)S(1)}, u32[]{:S(2)}, u32[]{:S(2)}) collective-permute-start(f32[8,256]{1,0:T(8,128)S(1)} %add_add_fusion.misfit_near), channel_id=1, source_target_pairs={{0,29},{1,30},{2,31},{3,0},{4,1},{5,2},{6,3},{7,4},{8,5},{9,6},{10... | collective-permute-start | bytes 24584 | tf_op jit(solution)/shard_map/ppermute | solution.py:217
  127.9 1.9 %collective-permute-start.10 = (f32[8,256]{1,0:T(8,128)S(1)}, f32[8,256]{1,0:T(8,128)S(1)}, u32[]{:S(2)}, u32[]{:S(2)}) collective-permute-start(f32[8,256]{1,0:T(8,128)S(1)} %add_add_fusion.misfit_near), channel_id=1, source_target_pairs={{0,3},{1,4},{2,5},{3,6},{4,7},{5,8},{6,9},{7,10},{8,11},{9,12},{10... | collective-permute-start | bytes 24584 | tf_op jit(solution)/shard_map/ppermute | solution.py:217
  129.9 6.0 %collective-permute-done.10.misfit_left = f32[8,256]{1,0:T(8,128)S(1)} collective-permute-done((f32[8,256]{1,0:T(8,128)S(1)}, f32[8,256]{1,0:T(8,128)S(1)}, u32[]{:S(2)}, u32[]{:S(2)}) %collective-permute-start.10) | collective-permute-done | bytes 8224 | tf_op jit(solution)/shard_map/ppermute | solution.py:217
  136.5 17.9 %adjoint.1 = f32[16,8,8,128]{3,2,1,0:T(8,128)} custom-call(s32[1,1,2]{2,1,0:T(1,128)} %aperture.3, s32[1,256]{1,0:T(1,128)} %receivers.3, f32[8,256]{1,0:T(8,128)} %copy-done.13, f32[8,256]{1,0:T(8,128)} %copy-done.16, f32[8,256]{1,0:T(8,128)} %copy-done.15, f32[4,8,16,128]{3,2,1,0:T(8,128)} %copy-done.2, f32[4,8,16,128]{3,2,1,0:T(8,128)} %copy-done.4, ...), custom_call_target="tpu_custom_call" | custom-call | tf_op jit(solution)/shard_map/adjoint/pallas_call | solution.py:267
  154.3 22.1 %all_to_all.16 = f32[16,8,8,128]{3,2,1,0:T(8,128)S(1)} all-to-all(f32[16,8,8,128]{3,2,1,0:T(8,128)} %adjoint.1), channel_id=1, replica_groups=mesh['x'=4,'yh'=4,'yl'=2,'z'=8,'c'=2] {'x','yh'}, dimensions={0} | all-to-all | bytes 1048576 | tf_op jit(solution)/shard_map/all_to_all | solution.py:287
  (54 shorter events, 7.6 us)
Async XLA Ops:
  0.0 0.9 copy-start.10
  0.9 0.8 copy-start.11
  2.6 4.4 %copy-start.14 = (f32[1,8,8,128]{3,2,1,0:T(8,128)S(1)}, f32[1,8,8,128]{3,2,1,0:T(8,128)}, u32[]{:S(2)}) copy-start(f32[1,8,8,128]{3,2,1,0:T(8,128)} %param.11) | copy-start | bytes 98308
  2.6 24.2 %copy-start.2 = (f32[4,8,16,128]{3,2,1,0:T(8,128)}, f32[4,8,16,128]{3,2,1,0:T(8,128)S(1)}, u32[]{:S(2)}) copy-start(f32[4,8,16,128]{3,2,1,0:T(8,128)S(1)} %constant_dynamic-update-slice_fusion.own) | copy-start | bytes 786436
  2.6 24.1 %collective-permute-start.1 = (f32[4,8,16,128]{3,2,1,0:T(8,128)S(1)}, f32[4,8,16,128]{3,2,1,0:T(8,128)S(1)}, u32[]{:S(2)}, u32[]{:S(2)}) collective-permute-start(f32[4,8,16,128]{3,2,1,0:T(8,128)S(1)} %constant_dynamic-update-slice_fusion.own), channel_id=1, source_target_pairs={{0,31},{1,0},{2,1},{3,2},{4,3},{5,4},{6,5},{7,6},{8,7},{9,8},{10,9... | collective-permute-start | bytes 786440 | tf_op jit(solution)/shard_map/ppermute | solution.py:217
  4.5 22.2 %collective-permute-start = (f32[4,8,16,128]{3,2,1,0:T(8,128)S(1)}, f32[4,8,16,128]{3,2,1,0:T(8,128)S(1)}, u32[]{:S(2)}, u32[]{:S(2)}) collective-permute-start(f32[4,8,16,128]{3,2,1,0:T(8,128)S(1)} %constant_dynamic-update-slice_fusion.own), channel_id=1, source_target_pairs={{0,1},{1,2},{2,3},{3,4},{4,5},{5,6},{6,7},{7,8},{8,9},{9,10},{10,1... | collective-permute-start | bytes 786440 | tf_op jit(solution)/shard_map/ppermute | solution.py:217
  22.4 19.5 %all-to-all-start.1 = ((f32[4,4,8,8,128]{4,3,2,1,0:T(8,128)}), f32[4,4,8,8,128]{4,3,2,1,0:T(8,128)S(1)}, u32[]{:S(2)}, u32[]{:S(2)}) async-start(f32[4,4,8,8,128]{4,3,2,1,0:T(8,128)} %broadcast_in_dim.18), calls=%async_computation.1 | async-start | bytes 1048576 | tf_op jit(solution)/shard_map/all_to_all | solution.py:227
  27.5 57.4 %collective-permute-start.3 = (f32[3,4,8,16,128]{4,3,2,1,0:T(8,128)S(1)}, f32[3,4,8,16,128]{4,3,2,1,0:T(8,128)S(1)}, u32[]{:S(2)}, u32[]{:S(2)}) collective-permute-start(f32[3,4,8,16,128]{4,3,2,1,0:T(8,128)S(1)} %pad_maximum_fusion), channel_id=1, source_target_pairs={{0,29},{1,30},{2,31},{3,0},{4,1},{5,2},{6,3},{7,4},{8,5},{9,6},{10... | collective-permute-start | bytes 2359304 | tf_op jit(solution)/shard_map/ppermute | solution.py:217
  39.2 45.7 %collective-permute-start.2 = (f32[3,4,8,16,128]{4,3,2,1,0:T(8,128)S(1)}, f32[3,4,8,16,128]{4,3,2,1,0:T(8,128)S(1)}, u32[]{:S(2)}, u32[]{:S(2)}) collective-permute-start(f32[3,4,8,16,128]{4,3,2,1,0:T(8,128)S(1)} %pad_maximum_fusion), channel_id=1, source_target_pairs={{0,3},{1,4},{2,5},{3,6},{4,7},{5,8},{6,9},{7,10},{8,11},{9,12},{10... | collective-permute-start | bytes 2359304 | tf_op jit(solution)/shard_map/ppermute | solution.py:217
  42.0 4.4 %copy-start.5 = (f32[2,8,8,128]{3,2,1,0:T(8,128)}, f32[2,8,8,128]{3,2,1,0:T(8,128)S(1)}, u32[]{:S(2)}) copy-start(f32[2,8,8,128]{3,2,1,0:T(8,128)S(1)} %constant_dynamic-slice_fusion.vel) | copy-start | bytes 196612
  42.0 12.3 %collective-permute-start.5 = (f32[2,8,8,128]{3,2,1,0:T(8,128)S(1)}, f32[2,8,8,128]{3,2,1,0:T(8,128)S(1)}, u32[]{:S(2)}, u32[]{:S(2)}) collective-permute-start(f32[2,8,8,128]{3,2,1,0:T(8,128)S(1)} %constant_dynamic-slice_fusion.vel), channel_id=1, source_target_pairs={{0,31},{1,0},{2,1},{3,2},{4,3},{5,4},{6,5},{7,6},{8,7},{9,8},{10,9... | collective-permute-start | bytes 196616 | tf_op jit(solution)/shard_map/ppermute | solution.py:217
  43.9 18.6 %collective-permute-start.4 = (f32[2,8,8,128]{3,2,1,0:T(8,128)S(1)}, f32[2,8,8,128]{3,2,1,0:T(8,128)S(1)}, u32[]{:S(2)}, u32[]{:S(2)}) collective-permute-start(f32[2,8,8,128]{3,2,1,0:T(8,128)S(1)} %constant_dynamic-slice_fusion.vel), channel_id=1, source_target_pairs={{0,1},{1,2},{2,3},{3,4},{4,5},{5,6},{6,7},{7,8},{8,9},{9,10},{10,1... | collective-permute-start | bytes 196616 | tf_op jit(solution)/shard_map/ppermute | solution.py:217
  54.3 8.3 %copy-start.6 = (f32[2,8,8,128]{3,2,1,0:T(8,128)}, f32[2,8,8,128]{3,2,1,0:T(8,128)S(1)}, u32[]{:S(2)}) copy-start(f32[2,8,8,128]{3,2,1,0:T(8,128)S(1)} %collective-permute-done.5.vel_right) | copy-start | bytes 196612
  63.2 13.5 %collective-permute-start.7 = (f32[3,2,8,8,128]{4,3,2,1,0:T(8,128)S(1)}, f32[3,2,8,8,128]{4,3,2,1,0:T(8,128)S(1)}, u32[]{:S(2)}, u32[]{:S(2)}) collective-permute-start(f32[3,2,8,8,128]{4,3,2,1,0:T(8,128)S(1)} %pad_maximum_fusion.1), channel_id=1, source_target_pairs={{0,29},{1,30},{2,31},{3,0},{4,1},{5,2},{6,3},{7,4},{8,5},{9,6},{10... | collective-permute-start | bytes 589832 | tf_op jit(solution)/shard_map/ppermute | solution.py:217
  73.5 11.4 %collective-permute-start.6 = (f32[3,2,8,8,128]{4,3,2,1,0:T(8,128)S(1)}, f32[3,2,8,8,128]{4,3,2,1,0:T(8,128)S(1)}, u32[]{:S(2)}, u32[]{:S(2)}) collective-permute-start(f32[3,2,8,8,128]{4,3,2,1,0:T(8,128)S(1)} %pad_maximum_fusion.1), channel_id=1, source_target_pairs={{0,3},{1,4},{2,5},{3,6},{4,7},{5,8},{6,9},{7,10},{8,11},{9,12},{10... | collective-permute-start | bytes 589832 | tf_op jit(solution)/shard_map/ppermute | solution.py:217
  76.7 8.2 %copy-start.8 = (f32[3,2,8,8,128]{4,3,2,1,0:T(8,128)}, f32[3,2,8,8,128]{4,3,2,1,0:T(8,128)S(1)}, u32[]{:S(2)}) copy-start(f32[3,2,8,8,128]{4,3,2,1,0:T(8,128)S(1)} %collective-permute-done.7.vel_far_right) | copy-start | bytes 589828
  84.9 1.0 copy-start
  85.9 0.9 copy-start.1
  115.9 4.3 %collective-permute-start.9 = (f32[8,256]{1,0:T(8,128)}, f32[8,256]{1,0:T(8,128)S(1)}, u32[]{:S(2)}, u32[]{:S(2)}) collective-permute-start(f32[8,256]{1,0:T(8,128)} %get-tuple-element.8), channel_id=1, source_target_pairs={{0,31},{1,0},{2,1},{3,2},{4,3},{5,4},{6,5},{7,6},{8,7},{9,8},{10,9... | collective-permute-start | bytes 24584 | tf_op jit(solution)/shard_map/ppermute | solution.py:217
  117.8 5.2 %collective-permute-start.8 = (f32[8,256]{1,0:T(8,128)}, f32[8,256]{1,0:T(8,128)S(1)}, u32[]{:S(2)}, u32[]{:S(2)}) collective-permute-start(f32[8,256]{1,0:T(8,128)} %get-tuple-element.8), channel_id=1, source_target_pairs={{0,1},{1,2},{2,3},{3,4},{4,5},{5,6},{6,7},{7,8},{8,9},{9,10},{10,1... | collective-permute-start | bytes 24584 | tf_op jit(solution)/shard_map/ppermute | solution.py:217
  123.7 12.2 %copy-start.13 = (f32[8,256]{1,0:T(8,128)}, f32[8,256]{1,0:T(8,128)S(1)}, u32[]{:S(2)}) copy-start(f32[8,256]{1,0:T(8,128)S(1)} %add_add_fusion.misfit_near) | copy-start | bytes 24580
  123.7 6.1 %collective-permute-start.11 = (f32[8,256]{1,0:T(8,128)S(1)}, f32[8,256]{1,0:T(8,128)S(1)}, u32[]{:S(2)}, u32[]{:S(2)}) collective-permute-start(f32[8,256]{1,0:T(8,128)S(1)} %add_add_fusion.misfit_near), channel_id=1, source_target_pairs={{0,29},{1,30},{2,31},{3,0},{4,1},{5,2},{6,3},{7,4},{8,5},{9,6},{10... | collective-permute-start | bytes 24584 | tf_op jit(solution)/shard_map/ppermute | solution.py:217
  127.9 8.0 %collective-permute-start.10 = (f32[8,256]{1,0:T(8,128)S(1)}, f32[8,256]{1,0:T(8,128)S(1)}, u32[]{:S(2)}, u32[]{:S(2)}) collective-permute-start(f32[8,256]{1,0:T(8,128)S(1)} %add_add_fusion.misfit_near), channel_id=1, source_target_pairs={{0,3},{1,4},{2,5},{3,6},{4,7},{5,8},{6,9},{7,10},{8,11},{9,12},{10... | collective-permute-start | bytes 24584 | tf_op jit(solution)/shard_map/ppermute | solution.py:217
  129.8 6.0 %copy-start.15 = (f32[8,256]{1,0:T(8,128)}, f32[8,256]{1,0:T(8,128)S(1)}, u32[]{:S(2)}) copy-start(f32[8,256]{1,0:T(8,128)S(1)} %collective-permute-done.11.misfit_right) | copy-start | bytes 24580
  (7 other events, 4.9 us)

commit v2 on v1

v2 whole, which is shorter than its diff:
```python
import jax
import jax.numpy as jnp
from jax import lax
from jax.experimental import pallas as pl
from jax.experimental.pallas import tpu as pltpu
from jax.sharding import Mesh, PartitionSpec as P

STEPS = 8
STENCIL_WEIGHTS = (-205.0 / 72.0, 8.0 / 5.0, -1.0 / 5.0, 8.0 / 315.0, -1.0 / 560.0)
STEP_SCALE = 0.088
DOM = ("yl", "z", "c")
SHOT = ("x", "yh")
SLABS = 32
TX, AY, TZ = 8, 16, 128
PLANES = 9 * TX
OWN = 4 * TX
PAD = 8
NREC = 256


def split2(x):
    high = x.astype(jnp.bfloat16)
    return high, (x - high.astype(jnp.float32)).astype(jnp.bfloat16)


def along_z():
    apart = jnp.abs(
        lax.broadcasted_iota(jnp.int32, (TZ, TZ), 0) - lax.broadcasted_iota(jnp.int32, (TZ, TZ), 1)
    )
    band = jnp.where(apart == 0, 3.0 * STENCIL_WEIGHTS[0], 0.0)
    for s in range(1, 5):
        band = jnp.where(apart == s, STENCIL_WEIGHTS[s], band)
    high, low = split2(band)
    top = jnp.concatenate([high, low], axis=1)
    return jnp.concatenate([top, jnp.concatenate([high, jnp.zeros_like(low)], axis=1)], axis=0)


def stack_parts(x):
    return jnp.concatenate(split2(x), axis=1)


def halves(product):
    return product[:, :TZ] + product[:, TZ:]


def z_pass(field, cur, matrix, low, high, zpart):
    for p in range(low, high, 16):
        q = min(p + 16, high)
        rows = field[cur, p:q, PAD : PAD + AY, :].reshape((q - p) * AY, TZ)
        product = jnp.dot(stack_parts(rows), matrix[...], preferred_element_type=jnp.float32)
        zpart[p:q] = halves(product).reshape(q - p, AY, TZ)


def xy_block(field, cur, p, h, zpart):
    y = PAD + 8 * h
    column = field[cur, pl.ds(p - 4, 16), y : y + 8, :]
    acc = zpart[pl.ds(p, 8), 8 * h : 8 * h + 8, :]
    for s in range(1, 5):
        near = column[4 + s : 12 + s] + column[4 - s : 12 - s]
        near = near + (field[cur, pl.ds(p, 8), y + s : y + 8 + s, :] + field[cur, pl.ds(p, 8), y - s : y + 8 - s, :])
        acc = acc + STENCIL_WEIGHTS[s] * near
    return column[4:12], acc


def assemble(field, which, item, slab, own, other, near, far, swapped_near, swapped_far):
    def put(j, value):
        there = slab + j
        inside = (there >= 0) & (there < SLABS)
        field[which, TX * (j + 4) : TX * (j + 5), PAD : PAD + AY, :] = jnp.where(inside, value, 0.0)

    put(0, own[item])

    @pl.when((slab & 1) == 0)
    def _():
        put(-4, far[0, item])
        put(-3, far[1, item])
        put(-2, near[0, item])
        put(-1, near[1, item])
        put(1, other[item])
        put(2, swapped_near[1, item])
        put(3, swapped_near[0, item])
        put(4, swapped_far[1, item])

    @pl.when((slab & 1) == 1)
    def _():
        put(-4, swapped_far[1, item])
        put(-3, swapped_near[0, item])
        put(-2, swapped_near[1, item])
        put(-1, other[item])
        put(1, near[1, item])
        put(2, near[0, item])
        put(3, far[1, item])
        put(4, far[0, item])


def clear_pads(field):
    zero = jnp.zeros((PLANES, PAD, TZ), jnp.float32)
    for b in range(2):
        field[b, :, 0:PAD, :] = zero
        field[b, :, PAD + AY : PAD + AY + PAD, :] = zero


def forward_kernel(
    aperture, source, checkpoint, wavelet, observed, receivers,
    own, other, near, far, swapped_near, swapped_far,
    vel, vel_left, vel_right, vel_far_left, vel_far_right,
    curvature, misfit, courant,
    field, update, samples, zpart, matrix,
):
    slab = aperture[0, 0, 0] & (SLABS - 1)
    clear_pads(field)
    matrix[...] = along_z()
    for item in range(2):
        assemble(field, item, item, slab, own, other, near, far, swapped_near, swapped_far)
    tiles = (
        [(vel_far_left, k) for k in range(3)] + [(vel_left, None), (vel, None), (vel_right, None)] + [(vel_far_right, k) for k in range(3)]
    )
    for j in range(9):
        there = slab + (j - 4)
        inside = (there >= 0) & (there < SLABS)
        ref, k = tiles[j]
        for row in range(2):
            speed = ref[row] if k is None else ref[k, row]
            speed = jnp.where(inside, STEP_SCALE * speed, 0.0)
            courant[TX * j : TX * (j + 1), 8 * row : 8 * row + 8, :] = speed * speed

    lane = lax.broadcasted_iota(jnp.int32, (AY, TZ), 1)
    suby = lax.broadcasted_iota(jnp.int32, (AY, TZ), 0)
    cell = source[0]
    source_x = (cell >> 11) - (slab - 4) * TX
    source_here = (source_x >= 0) & (source_x < PLANES)
    source_own = (source_x >= OWN) & (source_x < OWN + TX)
    spot = (suby == ((cell >> 7) & 15)) & (lane == (cell & 127))
    start = checkpoint[0]

    for n in range(STEPS):
        prev, cur = n & 1, 1 - (n & 1)
        low, high = 4 + 4 * n, PLANES - 4 - 4 * n
        z_pass(field, cur, matrix, low, high, zpart)

        def planes(b, _, prev=prev, cur=cur, low=low):
            p = low + 8 * b
            for h in range(2):
                y = PAD + 8 * h
                middle, acc = xy_block(field, cur, p, h, zpart)
                change = courant[pl.ds(p, 8), 8 * h : 8 * h + 8, :] * acc
                update[pl.ds(p, 8), 8 * h : 8 * h + 8, :] = change
                field[prev, pl.ds(p, 8), y : y + 8, :] = (middle + middle) - field[prev, pl.ds(p, 8), y : y + 8, :] + change
            return 0

        lax.fori_loop(0, (high - low) // 8, planes, 0)
        pulse = jnp.where(spot, wavelet[0, start + n], 0.0)

        @pl.when(source_here)
        def _(prev=prev, pulse=pulse):
            field[prev, source_x, PAD : PAD + AY, :] = field[prev, source_x, PAD : PAD + AY, :] + pulse

        @pl.when(source_own)
        def _(pulse=pulse):
            update[source_x] = update[source_x] + pulse

        curvature[n] = update[OWN : OWN + TX]
        samples[n] = field[prev, OWN : OWN + TX, PAD : PAD + AY, :].reshape(TX * AY, TZ)

    spots = receivers[...]
    row = (spots >> 7) - slab * (TX * AY)
    rows = lax.broadcasted_iota(jnp.int32, (TX * AY, NREC), 0)
    at_row = jnp.where(rows == row, 1.0, 0.0)
    at_lane = jnp.where(rows == (spots & 127), 1.0, 0.0).astype(jnp.bfloat16)
    at_lane = jnp.concatenate([at_lane, at_lane], axis=0)
    here = (row >= 0) & (row < TX * AY)
    taken = []
    for n in range(STEPS):
        product = jnp.dot(stack_parts(samples[n]), at_lane, preferred_element_type=jnp.float32)
        recorded = observed[0, pl.ds(start + n, 1), :]
        taken.append(jnp.sum(product * at_row, axis=0, keepdims=True) - jnp.where(here, recorded, 0.0))
    misfit[...] = jnp.concatenate(taken, axis=0)


def adjoint_kernel(
    aperture, receivers, misfit_near, misfit_left, misfit_right,
    own, other, near, far, swapped_near, swapped_far,
    vel, courant, curvature,
    out,
    field, injected, image, zpart, matrix, at_row,
):
    slab = aperture[0, 0, 0] & (SLABS - 1)
    first_row = aperture[0, 0, 0] >> 5
    clear_pads(field)
    matrix[...] = along_z()
    for item in range(2):
        assemble(field, item, 2 + item, slab, own, other, near, far, swapped_near, swapped_far)
    misfit = misfit_near[...] + misfit_left[...] + misfit_right[...]
    spots = receivers[...]
    row = (spots >> 7) - (slab - 4) * (TX * AY)
    rows = lax.broadcasted_iota(jnp.int32, (PLANES * AY, NREC), 0)
    at_row[...] = jnp.where(rows == row, 1.0, 0.0).astype(jnp.bfloat16)
    at_lane = rows[0:TZ] == (spots & 127)
    image[...] = jnp.zeros((TX, AY, TZ), jnp.float32)
    for i in range(STEPS):
        n = STEPS - i
        prev, cur = i & 1, 1 - (i & 1)
        low, high = 4 + 4 * i, PLANES - 4 - 4 * i
        parts = [jnp.where(at_lane, part.astype(jnp.float32), 0.0).astype(jnp.bfloat16) for part in split2(misfit[n - 1 : n])]
        sent = jnp.concatenate(parts, axis=0)
        for p in range(low, high, 16):
            q = min(p + 16, high)
            product = lax.dot_general(
                at_row[p * AY : q * AY], sent, (((1,), (1,)), ((), ())), preferred_element_type=jnp.float32
            )
            injected[p:q] = halves(product).reshape(q - p, AY, TZ)
        z_pass(field, cur, matrix, low, high, zpart)

        def planes(b, _, prev=prev, cur=cur, low=low):
            p = low + 8 * b
            for h in range(2):
                y = PAD + 8 * h
                middle, acc = xy_block(field, cur, p, h, zpart)
                change = courant[pl.ds(p, 8), 8 * h : 8 * h + 8, :] * acc + injected[pl.ds(p, 8), 8 * h : 8 * h + 8, :]
                field[prev, pl.ds(p, 8), y : y + 8, :] = (middle + middle) - field[prev, pl.ds(p, 8), y : y + 8, :] + change
            return 0

        lax.fori_loop(0, (high - low) // 8, planes, 0)
        image[...] += field[prev, OWN : OWN + TX, PAD : PAD + AY, :] * curvature[n - 1]
    out[...] = jnp.zeros(out.shape, jnp.float32)
    for k in range(2):
        speed = vel[k]
        out[first_row + k] = 2.0 / (speed * speed * speed) * image[:, 8 * k : 8 * k + 8, :]


def in_vmem(count):
    return [pl.BlockSpec(memory_space=pltpu.VMEM)] * count


def in_smem(count):
    return [pl.BlockSpec(memory_space=pltpu.SMEM)] * count


def body(
    velocity,
    aperture,
    source_cell,
    wavelet,
    observed,
    receivers,
    checkpoint,
    forward_previous,
    forward_current,
    adjoint_next,
    adjoint_current,
):
    def shift(cells, by):
        return lax.ppermute(cells, DOM, [(i, (i + by) % SLABS) for i in range(SLABS)])

    def partner(cells):
        return lax.ppermute(cells, DOM, [(i, i ^ 1) for i in range(SLABS)])

    def next_chip(cells):
        return lax.ppermute(cells, DOM, [(i, (i + (-2 if i % 2 else 2)) % SLABS) for i in range(SLABS)])

    own = jnp.concatenate([forward_previous, forward_current, adjoint_next, adjoint_current], axis=0)
    other = partner(own)
    column = lax.all_to_all(
        jnp.broadcast_to(velocity[None], (4,) + velocity.shape), "yh", 0, 0, tiled=True
    )
    near = next_chip(jnp.stack([own, other]))
    rows = lax.all_to_all(jnp.broadcast_to(column[None], (4,) + column.shape), "x", 0, 0, tiled=True)
    far = next_chip(near)
    swapped_near, swapped_far = partner(near), partner(far)
    fields = (own, other, near, far, swapped_near, swapped_far)

    rows = rows.reshape((16,) + velocity.shape[1:])
    vel = lax.dynamic_slice_in_dim(rows, aperture[0, 0, 0] // SLABS, 2, 0)
    vel_left, vel_right = shift(vel, 1), shift(vel, -1)
    vel_packed = jnp.stack([vel_left, vel, vel_right])
    vel_far_left, vel_far_right = shift(vel_packed, 3), shift(vel_packed, -3)

    slab_steps = (STEPS, TX, AY, TZ)
    region = (PLANES, AY, TZ)
    f32 = jnp.float32
    padded = pltpu.VMEM((2, PLANES, AY + 2 * PAD, TZ), f32)
    matrix = pltpu.VMEM((2 * TZ, 2 * TZ), jnp.bfloat16)
    limit = pltpu.CompilerParams(vmem_limit_bytes=32 << 20)
    curvature, misfit, courant = pl.pallas_call(
        forward_kernel,
        in_specs=in_smem(4) + in_vmem(13),
        out_specs=in_vmem(3),
        out_shape=[
            jax.ShapeDtypeStruct(slab_steps, f32),
            jax.ShapeDtypeStruct((STEPS, NREC), f32),
            jax.ShapeDtypeStruct(region, f32),
        ],
        scratch_shapes=[
            padded,
            pltpu.VMEM(region, f32),
            pltpu.VMEM((STEPS, TX * AY, TZ), f32),
            pltpu.VMEM(region, f32),
            matrix,
        ],
        compiler_params=limit,
        name="forward",
    )(
        aperture, source_cell, checkpoint, wavelet, observed, receivers, *fields,
        vel, vel_left, vel_right, vel_far_left, vel_far_right,
    )

    near = misfit + shift(misfit, 1) + shift(misfit, -1)
    misfit_left, misfit_right = shift(near, 3), shift(near, -3)

    terms = pl.pallas_call(
        adjoint_kernel,
        in_specs=in_smem(1) + in_vmem(13),
        out_specs=in_vmem(1)[0],
        out_shape=jax.ShapeDtypeStruct((16, TX, 8, TZ), f32),
        scratch_shapes=[
            padded,
            pltpu.VMEM(region, f32),
            pltpu.VMEM((TX, AY, TZ), f32),
            pltpu.VMEM(region, f32),
            matrix,
            pltpu.VMEM((PLANES * AY, NREC), jnp.bfloat16),
        ],
        compiler_params=limit,
        name="adjoint",
    )(
        aperture, receivers, near, misfit_left, misfit_right, *fields,
        vel, courant, curvature,
    )
    landed = lax.all_to_all(terms, SHOT, 0, 0, tiled=True)
    return jnp.sum(landed, axis=0, keepdims=True)


def solution(mesh):
    split = Mesh(mesh.devices.reshape(4, 4, 2, 8, 2), SHOT + DOM)
    placed = (
        P(SHOT + DOM, None, None, None),
        P(SHOT, DOM, None),
        P(SHOT),
        P(SHOT, None),
        P(SHOT, None, None),
        P(SHOT, None),
        P(SHOT),
        P(SHOT, DOM, None, None),
        P(SHOT, DOM, None, None),
        P(SHOT, DOM, None, None),
        P(SHOT, DOM, None, None),
    )
    return jax.shard_map(
        body,
        mesh=split,
        in_specs=placed,
        out_specs=P(SHOT + DOM, None, None, None),
        check_vma=False,
    )
```

time: 178 us -> 125 us (0.70)
  Pallas kernels: 47 us -> 13.3 us
  blocking collectives: 36.7 us -> 24.4 us
  local copies, waits for them, and re-layouts: 7.91 us -> 4.76 us
  waiting for transfers between devices: 33.2 us -> 31.4 us
    pallas_call x2, Pallas kernels: 47 us -> 13.3 us  [the longest x1 6.82 us: body(): pl.pallas_call(adjoint_kernel, in_specs=in_smem(1) + in_vmem(13), out_spe...]
    ppermute x12 -> x8, starting transfers between devices: 44.9 us -> 22.2 us  [shift(): lax.ppermute(cells, DOM, [(i, (i + by) % SLABS) for i in range(SLABS)])]
    ppermute x0 -> x5, starting transfers between devices: none -> 14.8 us  [the longest x2 8.55 us: next_chip(): lax.ppermute(cells, DOM, [(i, (i + (-2 if i % 2 else 2)) % SLABS) for i i...]
    all_to_all x1 -> x0, blocking collectives: 14.6 us -> none  [body(): lax.all_to_all(jnp.broadcast_to(velocity, (4,) + velocity.shape[1:]), 'yh...]
    ppermute x12 -> x8, waiting for transfers between devices: 33.1 us -> 21.9 us  [shift(): lax.ppermute(cells, DOM, [(i, (i + by) % SLABS) for i in range(SLABS)])]
    all_to_all x0 -> x1, starting transfers between devices: none -> 6.19 us  [body(): lax.all_to_all(jnp.broadcast_to(velocity[None], (4,) + velocity.shape), '...]
    all_to_all x0 -> x1, waiting for transfers between devices: none -> 4.21 us  [body(): lax.all_to_all(jnp.broadcast_to(velocity[None], (4,) + velocity.shape), '...]
    all_to_all x1, waiting for transfers between devices: 0.01 us -> 3.83 us  [body(): lax.all_to_all(jnp.broadcast_to(column[None], (4,) + column.shape), 'x',...]
  transfers between devices with their start and end apart: 13 -> 15, of which waited for: 5 -> 8; matrix products, arithmetic and copies ran while one was open for 1% -> 1% of each run, Pallas kernels for 0% -> 0%
where the time goes in v2:
time: 125 us; the launch traced here: 124 us
  starting transfers between devices  48 us (38%)
  waiting for transfers between devices  31.4 us (25%)
  blocking collectives  24.4 us (20%)
  Pallas kernels  13.3 us (11%)
  local copies, waits for them, and re-layouts  4.76 us (4%)
  between operations  1.71 us (1%)
    all_to_all x1, blocking collectives, body(): landed = lax.all_to_all(terms, SHOT, 0, 0, tiled=True)  24.4 us
    ppermute x8, starting transfers between devices, shift(): lax.ppermute(cells, DOM, [(i, (i + by) % SLABS) for i in range(SLABS)])  22.2 us
    ppermute x8, waiting for transfers between devices, shift(): lax.ppermute(cells, DOM, [(i, (i + by) % SLABS) for i in range(SLABS)])  21.9 us
    ppermute x2, starting transfers between devices, next_chip(): lax.ppermute(cells, DOM, [(i, (i + (-2 if i % 2 else 2)) % SLABS) for i i...  8.55 us
    pallas_call x1, Pallas kernels, body(): pl.pallas_call(adjoint_kernel, in_specs=in_smem(1) + in_vmem(13), out_spe...  6.82 us
    pallas_call x1, Pallas kernels, body(): pl.pallas_call(forward_kernel, in_specs=in_smem(4) + in_vmem(13), out_spe...  6.47 us
    ppermute x3, starting transfers between devices, partner(): return lax.ppermute(cells, DOM, [(i, i ^ 1) for i in range(SLABS)])  6.24 us
    all_to_all x1, starting transfers between devices, body(): lax.all_to_all(jnp.broadcast_to(velocity[None], (4,) + velocity.shape), '...  6.19 us
  transfers between devices with their start and end apart: 15, of which 8 were waited for; matrix products, arithmetic and copies ran while one was open for 1% of the time, Pallas kernels for 0%

profile of v2, /device:TPU:72, one launch (start us, length us, event | category | flops | bytes accessed | tf_op | source)
XLA Modules:
  0.0 124.3 jit_solution(958503325046318944)
XLA Ops:
  6.0 4.3 %collective-permute-start.1 = (f32[2,4,8,16,128]{4,3,2,1,0:T(8,128)S(1)}, f32[2,4,8,16,128]{4,3,2,1,0:T(8,128)S(1)}, u32[]{:S(2)}, u32[]{:S(2)}) collective-permute-start(f32[2,4,8,16,128]{4,3,2,1,0:T(8,128)S(1)} %pad_maximum_fusion), channel_id=1, source_target_pairs={{0,2},{1,31},{2,4},{3,1},{4,6},{5,3},{6,8},{7,5},{8,10},{9,7},{10,... | collective-permute-start | bytes 1572872 | tf_op jit(solution)/shard_map/ppermute | solution.py:259
  11.0 6.2 %all-to-all-start = ((f32[4,1,8,8,128]{4,3,2,1,0:T(8,128)}), f32[4,1,8,8,128]{4,3,2,1,0:T(8,128)S(1)}, u32[]{:S(2)}, u32[]{:S(2)}) async-start(f32[4,1,8,8,128]{4,3,2,1,0:T(8,128)} %broadcast_in_dim.20), calls=%async_computation | async-start | bytes 262144 | tf_op jit(solution)/shard_map/all_to_all | solution.py:263
  17.2 4.3 %collective-permute-start.2 = (f32[2,4,8,16,128]{4,3,2,1,0:T(8,128)S(1)}, f32[2,4,8,16,128]{4,3,2,1,0:T(8,128)S(1)}, u32[]{:S(2)}, u32[]{:S(2)}) collective-permute-start(f32[2,4,8,16,128]{4,3,2,1,0:T(8,128)S(1)} %collective-permute-done.1.near), channel_id=1, source_target_pairs={{0,2},{1,31},{2,4},{3,1},{4,6},{5,3},{6,8},{7,5},{8,10},{9,7},{10,... | collective-permute-start | bytes 1572872 | tf_op jit(solution)/shard_map/ppermute | solution.py:259
  21.5 4.2 %all-to-all-done = f32[4,1,8,8,128]{4,3,2,1,0:T(8,128)S(1)} async-done(((f32[4,1,8,8,128]{4,3,2,1,0:T(8,128)}), f32[4,1,8,8,128]{4,3,2,1,0:T(8,128)S(1)}, u32[]{:S(2)}, u32[]{:S(2)}) %all-to-all-start) | async-done | bytes 131104 | tf_op jit(solution)/shard_map/all_to_all | solution.py:263
  26.5 4.8 %all-to-all-start.1 = ((f32[4,4,1,8,8,128]{5,4,3,1,2,0:T(8,128)}), f32[4,4,1,8,8,128]{5,4,3,1,2,0:T(8,128)S(1)}, u32[]{:S(2)}, u32[]{:S(2)}) async-start(f32[4,4,1,8,8,128]{5,4,3,1,2,0:T(8,128)} %broadcast_in_dim.22), calls=%async_computation.1 | async-start | bytes 1048576 | tf_op jit(solution)/shard_map/all_to_all | solution.py:267
  32.1 1.9 %collective-permute-start.3 = (f32[2,4,8,16,128]{4,3,2,1,0:T(8,128)S(1)}, f32[2,4,8,16,128]{4,3,2,1,0:T(8,128)S(1)}, u32[]{:S(2)}, u32[]{:S(2)}) collective-permute-start(f32[2,4,8,16,128]{4,3,2,1,0:T(8,128)S(1)} %collective-permute-done.1.near), channel_id=1, source_target_pairs={{0,1},{1,0},{2,3},{3,2},{4,5},{5,4},{6,7},{7,6},{8,9},{9,8},{10,11... | collective-permute-start | bytes 1572872 | tf_op jit(solution)/shard_map/ppermute | solution.py:256
  34.1 2.4 %collective-permute-start.4 = (f32[2,4,8,16,128]{4,3,2,1,0:T(8,128)S(1)}, f32[2,4,8,16,128]{4,3,2,1,0:T(8,128)S(1)}, u32[]{:S(2)}, u32[]{:S(2)}) collective-permute-start(f32[2,4,8,16,128]{4,3,2,1,0:T(8,128)S(1)} %collective-permute-done.2.far), channel_id=1, source_target_pairs={{0,1},{1,0},{2,3},{3,2},{4,5},{5,4},{6,7},{7,6},{8,9},{9,8},{10,11... | collective-permute-start | bytes 1572872 | tf_op jit(solution)/shard_map/ppermute | solution.py:256
  36.5 3.8 %all-to-all-done.1 = f32[4,4,1,8,8,128]{5,4,3,1,2,0:T(8,128)S(1)} async-done(((f32[4,4,1,8,8,128]{5,4,3,1,2,0:T(8,128)}), f32[4,4,1,8,8,128]{5,4,3,1,2,0:T(8,128)S(1)}, u32[]{:S(2)}, u32[]{:S(2)}) %all-to-all-start.1) | async-done | bytes 524320 | tf_op jit(solution)/shard_map/all_to_all | solution.py:267
  40.3 4.1 %collective-permute-start.6 = (f32[2,8,8,128]{3,2,1,0:T(8,128)S(1)}, f32[2,8,8,128]{3,2,1,0:T(8,128)S(1)}, u32[]{:S(2)}, u32[]{:S(2)}) collective-permute-start(f32[2,8,8,128]{3,2,1,0:T(8,128)S(1)} %constant_dynamic-slice_fusion.vel), channel_id=1, source_target_pairs={{0,31},{1,0},{2,1},{3,2},{4,3},{5,4},{6,5},{7,6},{8,7},{9,8},{10,9... | collective-permute-start | bytes 196616 | tf_op jit(solution)/shard_map/ppermute | solution.py:253
  44.4 1.9 %collective-permute-start.5 = (f32[2,8,8,128]{3,2,1,0:T(8,128)S(1)}, f32[2,8,8,128]{3,2,1,0:T(8,128)S(1)}, u32[]{:S(2)}, u32[]{:S(2)}) collective-permute-start(f32[2,8,8,128]{3,2,1,0:T(8,128)S(1)} %constant_dynamic-slice_fusion.vel), channel_id=1, source_target_pairs={{0,1},{1,2},{2,3},{3,4},{4,5},{5,6},{6,7},{7,8},{8,9},{9,10},{10,1... | collective-permute-start | bytes 196616 | tf_op jit(solution)/shard_map/ppermute | solution.py:253
  46.4 3.6 %collective-permute-done.5.vel_left = f32[2,8,8,128]{3,2,1,0:T(8,128)S(1)} collective-permute-done((f32[2,8,8,128]{3,2,1,0:T(8,128)S(1)}, f32[2,8,8,128]{3,2,1,0:T(8,128)S(1)}, u32[]{:S(2)}, u32[]{:S(2)}) %collective-permute-start.5) | collective-permute-done | bytes 65568 | tf_op jit(solution)/shard_map/ppermute | solution.py:253
  50.0 3.8 %collective-permute-start.8 = (f32[3,2,8,8,128]{4,3,2,1,0:T(8,128)S(1)}, f32[3,2,8,8,128]{4,3,2,1,0:T(8,128)S(1)}, u32[]{:S(2)}, u32[]{:S(2)}) collective-permute-start(f32[3,2,8,8,128]{4,3,2,1,0:T(8,128)S(1)} %pad_maximum_fusion.1), channel_id=1, source_target_pairs={{0,29},{1,30},{2,31},{3,0},{4,1},{5,2},{6,3},{7,4},{8,5},{9,6},{10... | collective-permute-start | bytes 589832 | tf_op jit(solution)/shard_map/ppermute | solution.py:253
  53.8 1.9 %collective-permute-start.7 = (f32[3,2,8,8,128]{4,3,2,1,0:T(8,128)S(1)}, f32[3,2,8,8,128]{4,3,2,1,0:T(8,128)S(1)}, u32[]{:S(2)}, u32[]{:S(2)}) collective-permute-start(f32[3,2,8,8,128]{4,3,2,1,0:T(8,128)S(1)} %pad_maximum_fusion.1), channel_id=1, source_target_pairs={{0,3},{1,4},{2,5},{3,6},{4,7},{5,8},{6,9},{7,10},{8,11},{9,12},{10... | collective-permute-start | bytes 589832 | tf_op jit(solution)/shard_map/ppermute | solution.py:253
  57.0 3.6 %collective-permute-done.8.vel_far_right = f32[3,2,8,8,128]{4,3,2,1,0:T(8,128)S(1)} collective-permute-done((f32[3,2,8,8,128]{4,3,2,1,0:T(8,128)S(1)}, f32[3,2,8,8,128]{4,3,2,1,0:T(8,128)S(1)}, u32[]{:S(2)}, u32[]{:S(2)}) %collective-permute-start.8) | collective-permute-done | bytes 196640 | tf_op jit(solution)/shard_map/ppermute | solution.py:253
  60.6 6.2 %collective-permute-done.7.vel_far_left = f32[3,2,8,8,128]{4,3,2,1,0:T(8,128)S(1)} collective-permute-done((f32[3,2,8,8,128]{4,3,2,1,0:T(8,128)S(1)}, f32[3,2,8,8,128]{4,3,2,1,0:T(8,128)S(1)}, u32[]{:S(2)}, u32[]{:S(2)}) %collective-permute-start.7) | collective-permute-done | bytes 196640 | tf_op jit(solution)/shard_map/ppermute | solution.py:253
  66.9 6.5 %forward.1 = (f32[8,8,16,128]{3,2,1,0:T(8,128)S(1)}, f32[8,256]{1,0:T(8,128)S(1)}, f32[72,16,128]{2,1,0:T(8,128)S(1)}) custom-call(s32[1,1,2]{2,1,0:T(1,128)S(1)} %copy-done.1, s32[1]{0:T(128)S(6)} %copy.15.source, s32[1]{0:T(128)S(6)} %copy.16.checkpoint, f32[1,64]{1,0:T(1,128)S(1)} %copy-done.3, f32[1,64,256]{2,1,0:T(8,128)S(1)} %copy-done, ...), custom_call_target="tpu_custom_call" | custom-call | tf_op jit(solution)/shard_map/forward/pallas_call | solution.py:284
  73.4 3.0 %collective-permute-start.10 = (f32[8,256]{1,0:T(8,128)S(1)}, f32[8,256]{1,0:T(8,128)S(1)}, u32[]{:S(2)}, u32[]{:S(2)}) collective-permute-start(f32[8,256]{1,0:T(8,128)S(1)} %get-tuple-element.8), channel_id=1, source_target_pairs={{0,31},{1,0},{2,1},{3,2},{4,3},{5,4},{6,5},{7,6},{8,7},{9,8},{10,9... | collective-permute-start | bytes 24584 | tf_op jit(solution)/shard_map/ppermute | solution.py:253
  76.4 1.9 %collective-permute-start.9 = (f32[8,256]{1,0:T(8,128)S(1)}, f32[8,256]{1,0:T(8,128)S(1)}, u32[]{:S(2)}, u32[]{:S(2)}) collective-permute-start(f32[8,256]{1,0:T(8,128)S(1)} %get-tuple-element.8), channel_id=1, source_target_pairs={{0,1},{1,2},{2,3},{3,4},{4,5},{5,6},{6,7},{7,8},{8,9},{9,10},{10,1... | collective-permute-start | bytes 24584 | tf_op jit(solution)/shard_map/ppermute | solution.py:253
  78.3 3.0 %collective-permute-done.9 = f32[8,256]{1,0:T(8,128)S(1)} collective-permute-done((f32[8,256]{1,0:T(8,128)S(1)}, f32[8,256]{1,0:T(8,128)S(1)}, u32[]{:S(2)}, u32[]{:S(2)}) %collective-permute-start.9) | collective-permute-done | bytes 8224 | tf_op jit(solution)/shard_map/ppermute | solution.py:253
  81.4 3.0 %collective-permute-start.12 = (f32[8,256]{1,0:T(8,128)S(1)}, f32[8,256]{1,0:T(8,128)S(1)}, u32[]{:S(2)}, u32[]{:S(2)}) collective-permute-start(f32[8,256]{1,0:T(8,128)S(1)} %add_add_fusion.misfit_near), channel_id=1, source_target_pairs={{0,29},{1,30},{2,31},{3,0},{4,1},{5,2},{6,3},{7,4},{8,5},{9,6},{10... | collective-permute-start | bytes 24584 | tf_op jit(solution)/shard_map/ppermute | solution.py:253
  84.4 2.5 %collective-permute-start.11 = (f32[8,256]{1,0:T(8,128)S(1)}, f32[8,256]{1,0:T(8,128)S(1)}, u32[]{:S(2)}, u32[]{:S(2)}) collective-permute-start(f32[8,256]{1,0:T(8,128)S(1)} %add_add_fusion.misfit_near), channel_id=1, source_target_pairs={{0,3},{1,4},{2,5},{3,6},{4,7},{5,8},{6,9},{7,10},{8,11},{9,12},{10... | collective-permute-start | bytes 24584 | tf_op jit(solution)/shard_map/ppermute | solution.py:253
  87.0 5.4 %collective-permute-done.11.misfit_left = f32[8,256]{1,0:T(8,128)S(1)} collective-permute-done((f32[8,256]{1,0:T(8,128)S(1)}, f32[8,256]{1,0:T(8,128)S(1)}, u32[]{:S(2)}, u32[]{:S(2)}) %collective-permute-start.11) | collective-permute-done | bytes 8224 | tf_op jit(solution)/shard_map/ppermute | solution.py:253
  92.4 6.8 %adjoint.1 = f32[16,8,8,128]{3,2,1,0:T(8,128)S(1)} custom-call(s32[1,1,2]{2,1,0:T(1,128)S(1)} %copy-done.1, s32[1,256]{1,0:T(1,128)S(1)} %copy-done.2, f32[8,256]{1,0:T(8,128)S(1)} %add_add_fusion.misfit_near, f32[8,256]{1,0:T(8,128)S(1)} %collective-permute-done.11.misfit_left, f32[8,256]{1,0:T(8,128)S(1)} %collective-permute-done.12.misfit_right, ...), custom_call_target="tpu_custom_call" | custom-call | tf_op jit(solution)/shard_map/adjoint/pallas_call | solution.py:310
  99.2 24.4 %all_to_all.15 = f32[16,8,8,128]{3,2,1,0:T(8,128)S(1)} all-to-all(f32[16,8,8,128]{3,2,1,0:T(8,128)S(1)} %adjoint.1), channel_id=1, replica_groups=mesh['x'=4,'yh'=4,'yl'=2,'z'=8,'c'=2] {'x','yh'}, dimensions={0} | all-to-all | bytes 1048576 | tf_op jit(solution)/shard_map/all_to_all | solution.py:329
  (37 shorter events, 8.9 us)
Async XLA Ops:
  0.0 0.9 copy-start.4
  0.9 0.8 copy-start.5
  1.7 0.8 copy-start.6
  2.6 3.4 %collective-permute-start = (f32[4,8,16,128]{3,2,1,0:T(8,128)S(1)}, f32[4,8,16,128]{3,2,1,0:T(8,128)S(1)}, u32[]{:S(2)}, u32[]{:S(2)}) collective-permute-start(f32[4,8,16,128]{3,2,1,0:T(8,128)S(1)} %constant_dynamic-update-slice_fusion.own), channel_id=1, source_target_pairs={{0,1},{1,0},{2,3},{3,2},{4,5},{5,4},{6,7},{7,6},{8,9},{9,8},{10,11... | collective-permute-start | bytes 786440 | tf_op jit(solution)/shard_map/ppermute | solution.py:256
  6.0 4.3 %copy-start.7 = (f32[1,8,8,128]{3,2,1,0:T(8,128)S(1)}, f32[1,8,8,128]{3,2,1,0:T(8,128)}, u32[]{:S(2)}) copy-start(f32[1,8,8,128]{3,2,1,0:T(8,128)} %param.11) | copy-start | bytes 98308
  6.0 11.2 %collective-permute-start.1 = (f32[2,4,8,16,128]{4,3,2,1,0:T(8,128)S(1)}, f32[2,4,8,16,128]{4,3,2,1,0:T(8,128)S(1)}, u32[]{:S(2)}, u32[]{:S(2)}) collective-permute-start(f32[2,4,8,16,128]{4,3,2,1,0:T(8,128)S(1)} %pad_maximum_fusion), channel_id=1, source_target_pairs={{0,2},{1,31},{2,4},{3,1},{4,6},{5,3},{6,8},{7,5},{8,10},{9,7},{10,... | collective-permute-start | bytes 1572872 | tf_op jit(solution)/shard_map/ppermute | solution.py:259
  11.0 14.7 %all-to-all-start = ((f32[4,1,8,8,128]{4,3,2,1,0:T(8,128)}), f32[4,1,8,8,128]{4,3,2,1,0:T(8,128)S(1)}, u32[]{:S(2)}, u32[]{:S(2)}) async-start(f32[4,1,8,8,128]{4,3,2,1,0:T(8,128)} %broadcast_in_dim.20), calls=%async_computation | async-start | bytes 262144 | tf_op jit(solution)/shard_map/all_to_all | solution.py:263
  17.2 16.9 %collective-permute-start.2 = (f32[2,4,8,16,128]{4,3,2,1,0:T(8,128)S(1)}, f32[2,4,8,16,128]{4,3,2,1,0:T(8,128)S(1)}, u32[]{:S(2)}, u32[]{:S(2)}) collective-permute-start(f32[2,4,8,16,128]{4,3,2,1,0:T(8,128)S(1)} %collective-permute-done.1.near), channel_id=1, source_target_pairs={{0,2},{1,31},{2,4},{3,1},{4,6},{5,3},{6,8},{7,5},{8,10},{9,7},{10,... | collective-permute-start | bytes 1572872 | tf_op jit(solution)/shard_map/ppermute | solution.py:259
  26.5 13.8 %all-to-all-start.1 = ((f32[4,4,1,8,8,128]{5,4,3,1,2,0:T(8,128)}), f32[4,4,1,8,8,128]{5,4,3,1,2,0:T(8,128)S(1)}, u32[]{:S(2)}, u32[]{:S(2)}) async-start(f32[4,4,1,8,8,128]{5,4,3,1,2,0:T(8,128)} %broadcast_in_dim.22), calls=%async_computation.1 | async-start | bytes 1048576 | tf_op jit(solution)/shard_map/all_to_all | solution.py:267
  31.3 0.7 copy-start.1
  32.1 34.7 %collective-permute-start.3 = (f32[2,4,8,16,128]{4,3,2,1,0:T(8,128)S(1)}, f32[2,4,8,16,128]{4,3,2,1,0:T(8,128)S(1)}, u32[]{:S(2)}, u32[]{:S(2)}) collective-permute-start(f32[2,4,8,16,128]{4,3,2,1,0:T(8,128)S(1)} %collective-permute-done.1.near), channel_id=1, source_target_pairs={{0,1},{1,0},{2,3},{3,2},{4,5},{5,4},{6,7},{7,6},{8,9},{9,8},{10,11... | collective-permute-start | bytes 1572872 | tf_op jit(solution)/shard_map/ppermute | solution.py:256
  34.1 32.8 %collective-permute-start.4 = (f32[2,4,8,16,128]{4,3,2,1,0:T(8,128)S(1)}, f32[2,4,8,16,128]{4,3,2,1,0:T(8,128)S(1)}, u32[]{:S(2)}, u32[]{:S(2)}) collective-permute-start(f32[2,4,8,16,128]{4,3,2,1,0:T(8,128)S(1)} %collective-permute-done.2.far), channel_id=1, source_target_pairs={{0,1},{1,0},{2,3},{3,2},{4,5},{5,4},{6,7},{7,6},{8,9},{9,8},{10,11... | collective-permute-start | bytes 1572872 | tf_op jit(solution)/shard_map/ppermute | solution.py:256
  40.3 6.0 %collective-permute-start.6 = (f32[2,8,8,128]{3,2,1,0:T(8,128)S(1)}, f32[2,8,8,128]{3,2,1,0:T(8,128)S(1)}, u32[]{:S(2)}, u32[]{:S(2)}) collective-permute-start(f32[2,8,8,128]{3,2,1,0:T(8,128)S(1)} %constant_dynamic-slice_fusion.vel), channel_id=1, source_target_pairs={{0,31},{1,0},{2,1},{3,2},{4,3},{5,4},{6,5},{7,6},{8,7},{9,8},{10,9... | collective-permute-start | bytes 196616 | tf_op jit(solution)/shard_map/ppermute | solution.py:253
  44.4 5.6 %collective-permute-start.5 = (f32[2,8,8,128]{3,2,1,0:T(8,128)S(1)}, f32[2,8,8,128]{3,2,1,0:T(8,128)S(1)}, u32[]{:S(2)}, u32[]{:S(2)}) collective-permute-start(f32[2,8,8,128]{3,2,1,0:T(8,128)S(1)} %constant_dynamic-slice_fusion.vel), channel_id=1, source_target_pairs={{0,1},{1,2},{2,3},{3,4},{4,5},{5,6},{6,7},{7,8},{8,9},{9,10},{10,1... | collective-permute-start | bytes 196616 | tf_op jit(solution)/shard_map/ppermute | solution.py:253
  50.0 16.9 %copy-start = (f32[1,64,256]{2,1,0:T(8,128)S(1)}, f32[1,64,256]{2,1,0:T(8,128)}, u32[]{:S(2)}) copy-start(f32[1,64,256]{2,1,0:T(8,128)} %observed.1) | copy-start | bytes 196612
  50.0 10.6 %collective-permute-start.8 = (f32[3,2,8,8,128]{4,3,2,1,0:T(8,128)S(1)}, f32[3,2,8,8,128]{4,3,2,1,0:T(8,128)S(1)}, u32[]{:S(2)}, u32[]{:S(2)}) collective-permute-start(f32[3,2,8,8,128]{4,3,2,1,0:T(8,128)S(1)} %pad_maximum_fusion.1), channel_id=1, source_target_pairs={{0,29},{1,30},{2,31},{3,0},{4,1},{5,2},{6,3},{7,4},{8,5},{9,6},{10... | collective-permute-start | bytes 589832 | tf_op jit(solution)/shard_map/ppermute | solution.py:253
  53.8 13.1 %collective-permute-start.7 = (f32[3,2,8,8,128]{4,3,2,1,0:T(8,128)S(1)}, f32[3,2,8,8,128]{4,3,2,1,0:T(8,128)S(1)}, u32[]{:S(2)}, u32[]{:S(2)}) collective-permute-start(f32[3,2,8,8,128]{4,3,2,1,0:T(8,128)S(1)} %pad_maximum_fusion.1), channel_id=1, source_target_pairs={{0,3},{1,4},{2,5},{3,6},{4,7},{5,8},{6,9},{7,10},{8,11},{9,12},{10... | collective-permute-start | bytes 589832 | tf_op jit(solution)/shard_map/ppermute | solution.py:253
  56.4 10.5 %copy-start.2 = (s32[1,256]{1,0:T(1,128)S(1)}, s32[1,256]{1,0:T(1,128)}, u32[]{:S(2)}) copy-start(s32[1,256]{1,0:T(1,128)} %receivers.3) | copy-start | bytes 3076
  56.4 10.5 %copy-start.3 = (f32[1,64]{1,0:T(1,128)S(1)}, f32[1,64]{1,0:T(1,128)}, u32[]{:S(2)}) copy-start(f32[1,64]{1,0:T(1,128)} %wavelet.1) | copy-start | bytes 772
  73.4 5.0 %collective-permute-start.10 = (f32[8,256]{1,0:T(8,128)S(1)}, f32[8,256]{1,0:T(8,128)S(1)}, u32[]{:S(2)}, u32[]{:S(2)}) collective-permute-start(f32[8,256]{1,0:T(8,128)S(1)} %get-tuple-element.8), channel_id=1, source_target_pairs={{0,31},{1,0},{2,1},{3,2},{4,3},{5,4},{6,5},{7,6},{8,7},{9,8},{10,9... | collective-permute-start | bytes 24584 | tf_op jit(solution)/shard_map/ppermute | solution.py:253
  76.4 5.0 %collective-permute-start.9 = (f32[8,256]{1,0:T(8,128)S(1)}, f32[8,256]{1,0:T(8,128)S(1)}, u32[]{:S(2)}, u32[]{:S(2)}) collective-permute-start(f32[8,256]{1,0:T(8,128)S(1)} %get-tuple-element.8), channel_id=1, source_target_pairs={{0,1},{1,2},{2,3},{3,4},{4,5},{5,6},{6,7},{7,8},{8,9},{9,10},{10,1... | collective-permute-start | bytes 24584 | tf_op jit(solution)/shard_map/ppermute | solution.py:253
  81.4 5.6 %collective-permute-start.12 = (f32[8,256]{1,0:T(8,128)S(1)}, f32[8,256]{1,0:T(8,128)S(1)}, u32[]{:S(2)}, u32[]{:S(2)}) collective-permute-start(f32[8,256]{1,0:T(8,128)S(1)} %add_add_fusion.misfit_near), channel_id=1, source_target_pairs={{0,29},{1,30},{2,31},{3,0},{4,1},{5,2},{6,3},{7,4},{8,5},{9,6},{10... | collective-permute-start | bytes 24584 | tf_op jit(solution)/shard_map/ppermute | solution.py:253
  84.4 8.0 %collective-permute-start.11 = (f32[8,256]{1,0:T(8,128)S(1)}, f32[8,256]{1,0:T(8,128)S(1)}, u32[]{:S(2)}, u32[]{:S(2)}) collective-permute-start(f32[8,256]{1,0:T(8,128)S(1)} %add_add_fusion.misfit_near), channel_id=1, source_target_pairs={{0,3},{1,4},{2,5},{3,6},{4,7},{5,8},{6,9},{7,10},{8,11},{9,12},{10... | collective-permute-start | bytes 24584 | tf_op jit(solution)/shard_map/ppermute | solution.py:253

commit v3 on v2

--- a/solution.py
+++ b/solution.py
@@ -4,6 +4,7 @@
 from jax.experimental import pallas as pl
 from jax.experimental.pallas import tpu as pltpu
 from jax.sharding import Mesh, PartitionSpec as P
+
 
 STEPS = 8
 STENCIL_WEIGHTS = (-205.0 / 72.0, 8.0 / 5.0, -1.0 / 5.0, 8.0 / 315.0, -1.0 / 560.0)
@@ -174,11 +175,13 @@
         product = jnp.dot(stack_parts(samples[n]), at_lane, preferred_element_type=jnp.float32)
         recorded = observed[0, pl.ds(start + n, 1), :]
         taken.append(jnp.sum(product * at_row, axis=0, keepdims=True) - jnp.where(here, recorded, 0.0))
-    misfit[...] = jnp.concatenate(taken, axis=0)
+    found = jnp.concatenate(taken, axis=0)
+    for k in range(SLABS):
+        misfit[k] = found
 
 
 def adjoint_kernel(
-    aperture, receivers, misfit_near, misfit_left, misfit_right,
+    aperture, receivers, misfits,
     own, other, near, far, swapped_near, swapped_far,
     vel, courant, curvature,
     out,
@@ -190,7 +193,7 @@
     matrix[...] = along_z()
     for item in range(2):
         assemble(field, item, 2 + item, slab, own, other, near, far, swapped_near, swapped_far)
-    misfit = misfit_near[...] + misfit_left[...] + misfit_right[...]
+    misfit = jnp.sum(misfits[...], axis=0)
     spots = receivers[...]
     row = (spots >> 7) - (slab - 4) * (TX * AY)
     rows = lax.broadcasted_iota(jnp.int32, (PLANES * AY, NREC), 0)
@@ -236,7 +239,7 @@
     return [pl.BlockSpec(memory_space=pltpu.SMEM)] * count
 
 
-def body(
+def inner(
     velocity,
     aperture,
     source_cell,
@@ -259,21 +262,23 @@
         return lax.ppermute(cells, DOM, [(i, (i + (-2 if i % 2 else 2)) % SLABS) for i in range(SLABS)])
 
     own = jnp.concatenate([forward_previous, forward_current, adjoint_next, adjoint_current], axis=0)
-    other = partner(own)
     column = lax.all_to_all(
         jnp.broadcast_to(velocity[None], (4,) + velocity.shape), "yh", 0, 0, tiled=True
     )
+    other = partner(own)
+    rows = lax.all_to_all(jnp.broadcast_to(column[None], (4,) + column.shape), "x", 0, 0, tiled=True)
     near = next_chip(jnp.stack([own, other]))
-    rows = lax.all_to_all(jnp.broadcast_to(column[None], (4,) + column.shape), "x", 0, 0, tiled=True)
-    far = next_chip(near)
-    swapped_near, swapped_far = partner(near), partner(far)
-    fields = (own, other, near, far, swapped_near, swapped_far)
-
     rows = rows.reshape((16,) + velocity.shape[1:])
     vel = lax.dynamic_slice_in_dim(rows, aperture[0, 0, 0] // SLABS, 2, 0)
-    vel_left, vel_right = shift(vel, 1), shift(vel, -1)
+    vel_left = shift(vel, 1)
+    vel_right = shift(vel, -1)
+    far = next_chip(near)
     vel_packed = jnp.stack([vel_left, vel, vel_right])
-    vel_far_left, vel_far_right = shift(vel_packed, 3), shift(vel_packed, -3)
+    vel_far_left = shift(vel_packed, 3)
+    vel_far_right = shift(vel_packed, -3)
+    swapped_near = partner(near)
+    swapped_far = partner(far)
+    fields = (own, other, near, far, swapped_near, swapped_far)
 
     slab_steps = (STEPS, TX, AY, TZ)
     region = (PLANES, AY, TZ)
@@ -287,7 +292,7 @@
         out_specs=in_vmem(3),
         out_shape=[
             jax.ShapeDtypeStruct(slab_steps, f32),
-            jax.ShapeDtypeStruct((STEPS, NREC), f32),
+            jax.ShapeDtypeStruct((SLABS, STEPS, NREC), f32),
             jax.ShapeDtypeStruct(region, f32),
         ],
         scratch_shapes=[
@@ -304,12 +309,11 @@
         vel, vel_left, vel_right, vel_far_left, vel_far_right,
     )
 
-    near = misfit + shift(misfit, 1) + shift(misfit, -1)
-    misfit_left, misfit_right = shift(near, 3), shift(near, -3)
+    misfits = lax.all_to_all(misfit[:, None], DOM, 0, 0, tiled=True).reshape(SLABS, STEPS, NREC)
 
     terms = pl.pallas_call(
         adjoint_kernel,
-        in_specs=in_smem(1) + in_vmem(13),
+        in_specs=in_smem(1) + in_vmem(11),
         out_specs=in_vmem(1)[0],
         out_shape=jax.ShapeDtypeStruct((16, TX, 8, TZ), f32),
         scratch_shapes=[
@@ -323,7 +327,7 @@
         compiler_params=limit,
         name="adjoint",
     )(
-        aperture, receivers, near, misfit_left, misfit_right, *fields,
+        aperture, receivers, misfits, *fields,
         vel, courant, curvature,
     )
     landed = lax.all_to_all(terms, SHOT, 0, 0, tiled=True)
@@ -346,7 +350,7 @@
         P(SHOT, DOM, None, None),
     )
     return jax.shard_map(
-        body,
+        inner,
         mesh=split,
         in_specs=placed,
         out_specs=P(SHOT + DOM, None, None, None),

time: 125 us -> 125 us (level)
  the two profiles are of different devices: /device:TPU:72 before, /device:TPU:8 now
where the time goes in v3:
time: 125 us; the launch traced here: 124 us
  blocking collectives  42.4 us (34%)
  starting transfers between devices  38.8 us (31%)
  waiting for transfers between devices  22.2 us (18%)
  Pallas kernels  13.3 us (11%)
  local copies, waits for them, and re-layouts  4.77 us (4%)
  between operations  1.67 us (1%)
    all_to_all x1, blocking collectives, inner(): landed = lax.all_to_all(terms, SHOT, 0, 0, tiled=True)  26.2 us
    all_to_all x1, blocking collectives, inner(): lax.all_to_all(misfit[:, None], DOM, 0, 0, tiled=True)  16.2 us
    ppermute x4, waiting for transfers between devices, shift(): lax.ppermute(cells, DOM, [(i, (i + by) % SLABS) for i in range(SLABS)])  12.9 us
    ppermute x4, starting transfers between devices, shift(): lax.ppermute(cells, DOM, [(i, (i + by) % SLABS) for i in range(SLABS)])  12.1 us
    ppermute x3, starting transfers between devices, partner(): return lax.ppermute(cells, DOM, [(i, i ^ 1) for i in range(SLABS)])  9.95 us
    ppermute x2, waiting for transfers between devices, next_chip(): lax.ppermute(cells, DOM, [(i, (i + (-2 if i % 2 else 2)) % SLABS) for i i...  6.83 us
    pallas_call x1, Pallas kernels, inner(): pl.pallas_call(adjoint_kernel, in_specs=in_smem(1) + in_vmem(11), out_spe...  6.83 us
    pallas_call x1, Pallas kernels, inner(): pl.pallas_call(forward_kernel, in_specs=in_smem(4) + in_vmem(13), out_spe...  6.51 us
  transfers between devices with their start and end apart: 11, of which 6 were waited for; matrix products, arithmetic and copies ran while one was open for 1% of the time, Pallas kernels for 0%

profile of v3, /device:TPU:8, one launch (start us, length us, event | category | flops | bytes accessed | tf_op | source)
XLA Modules:
  0.0 123.8 jit_solution(11285682740367170109)
XLA Ops:
  0.0 0.9 constant_dynamic-update-slice_fusion.3
  1.7 0.8 copy-done.6
  2.6 1.9 %collective-permute-start = (f32[4,8,16,128]{3,2,1,0:T(8,128)S(1)}, f32[4,8,16,128]{3,2,1,0:T(8,128)S(1)}, u32[]{:S(2)}, u32[]{:S(2)}) collective-permute-start(f32[4,8,16,128]{3,2,1,0:T(8,128)S(1)} %constant_dynamic-update-slice_fusion.own), channel_id=1, source_target_pairs={{0,1},{1,0},{2,3},{3,2},{4,5},{5,4},{6,7},{7,6},{8,9},{9,8},{10,11... | collective-permute-start | bytes 786440 | tf_op jit(solution)/shard_map/ppermute | solution.py:259
  4.5 1.5 %collective-permute-done.other = f32[4,8,16,128]{3,2,1,0:T(8,128)S(1)} collective-permute-done((f32[4,8,16,128]{3,2,1,0:T(8,128)S(1)}, f32[4,8,16,128]{3,2,1,0:T(8,128)S(1)}, u32[]{:S(2)}, u32[]{:S(2)}) %collective-permute-start) | collective-permute-done | bytes 262176 | tf_op jit(solution)/shard_map/ppermute | solution.py:259
  6.0 4.3 %collective-permute-start.1 = (f32[2,4,8,16,128]{4,3,2,1,0:T(8,128)S(1)}, f32[2,4,8,16,128]{4,3,2,1,0:T(8,128)S(1)}, u32[]{:S(2)}, u32[]{:S(2)}) collective-permute-start(f32[2,4,8,16,128]{4,3,2,1,0:T(8,128)S(1)} %pad_maximum_fusion), channel_id=1, source_target_pairs={{0,2},{1,31},{2,4},{3,1},{4,6},{5,3},{6,8},{7,5},{8,10},{9,7},{10,... | collective-permute-start | bytes 1572872 | tf_op jit(solution)/shard_map/ppermute | solution.py:262
  11.0 6.2 %all-to-all-start = ((f32[4,1,8,8,128]{4,3,2,1,0:T(8,128)}), f32[4,1,8,8,128]{4,3,2,1,0:T(8,128)S(1)}, u32[]{:S(2)}, u32[]{:S(2)}) async-start(f32[4,1,8,8,128]{4,3,2,1,0:T(8,128)} %broadcast_in_dim.23), calls=%async_computation | async-start | bytes 262144 | tf_op jit(solution)/shard_map/all_to_all | solution.py:265
  17.2 6.8 %collective-permute-done.1.near = f32[2,4,8,16,128]{4,3,2,1,0:T(8,128)S(1)} collective-permute-done((f32[2,4,8,16,128]{4,3,2,1,0:T(8,128)S(1)}, f32[2,4,8,16,128]{4,3,2,1,0:T(8,128)S(1)}, u32[]{:S(2)}, u32[]{:S(2)}) %collective-permute-start.1) | collective-permute-done | bytes 524320 | tf_op jit(solution)/shard_map/ppermute | solution.py:262
  24.0 1.9 %collective-permute-start.2 = (f32[2,4,8,16,128]{4,3,2,1,0:T(8,128)S(1)}, f32[2,4,8,16,128]{4,3,2,1,0:T(8,128)S(1)}, u32[]{:S(2)}, u32[]{:S(2)}) collective-permute-start(f32[2,4,8,16,128]{4,3,2,1,0:T(8,128)S(1)} %collective-permute-done.1.near), channel_id=1, source_target_pairs={{0,2},{1,31},{2,4},{3,1},{4,6},{5,3},{6,8},{7,5},{8,10},{9,7},{10,... | collective-permute-start | bytes 1572872 | tf_op jit(solution)/shard_map/ppermute | solution.py:262
  25.9 1.0 all-to-all-done
  27.0 0.9 broadcast_in_dim.25
  27.8 4.3 %all-to-all-start.1 = ((f32[4,4,1,8,8,128]{5,4,3,1,2,0:T(8,128)}), f32[4,4,1,8,8,128]{5,4,3,1,2,0:T(8,128)S(1)}, u32[]{:S(2)}, u32[]{:S(2)}) async-start(f32[4,4,1,8,8,128]{5,4,3,1,2,0:T(8,128)} %broadcast_in_dim.25), calls=%async_computation.1 | async-start | bytes 1048576 | tf_op jit(solution)/shard_map/all_to_all | solution.py:269
  32.9 6.1 %collective-permute-start.3 = (f32[2,4,8,16,128]{4,3,2,1,0:T(8,128)S(1)}, f32[2,4,8,16,128]{4,3,2,1,0:T(8,128)S(1)}, u32[]{:S(2)}, u32[]{:S(2)}) collective-permute-start(f32[2,4,8,16,128]{4,3,2,1,0:T(8,128)S(1)} %collective-permute-done.1.near), channel_id=1, source_target_pairs={{0,1},{1,0},{2,3},{3,2},{4,5},{5,4},{6,7},{7,6},{8,9},{9,8},{10,11... | collective-permute-start | bytes 1572872 | tf_op jit(solution)/shard_map/ppermute | solution.py:259
  39.1 1.9 %collective-permute-start.4 = (f32[2,4,8,16,128]{4,3,2,1,0:T(8,128)S(1)}, f32[2,4,8,16,128]{4,3,2,1,0:T(8,128)S(1)}, u32[]{:S(2)}, u32[]{:S(2)}) collective-permute-start(f32[2,4,8,16,128]{4,3,2,1,0:T(8,128)S(1)} %collective-permute-done.2.far), channel_id=1, source_target_pairs={{0,1},{1,0},{2,3},{3,2},{4,5},{5,4},{6,7},{7,6},{8,9},{9,8},{10,11... | collective-permute-start | bytes 1572872 | tf_op jit(solution)/shard_map/ppermute | solution.py:259
  41.0 4.6 %collective-permute-start.6 = (f32[2,8,8,128]{3,2,1,0:T(8,128)S(1)}, f32[2,8,8,128]{3,2,1,0:T(8,128)S(1)}, u32[]{:S(2)}, u32[]{:S(2)}) collective-permute-start(f32[2,8,8,128]{3,2,1,0:T(8,128)S(1)} %constant_dynamic-slice_fusion.vel), channel_id=1, source_target_pairs={{0,31},{1,0},{2,1},{3,2},{4,3},{5,4},{6,5},{7,6},{8,7},{9,8},{10,9... | collective-permute-start | bytes 196616 | tf_op jit(solution)/shard_map/ppermute | solution.py:256
  45.7 1.9 %collective-permute-start.5 = (f32[2,8,8,128]{3,2,1,0:T(8,128)S(1)}, f32[2,8,8,128]{3,2,1,0:T(8,128)S(1)}, u32[]{:S(2)}, u32[]{:S(2)}) collective-permute-start(f32[2,8,8,128]{3,2,1,0:T(8,128)S(1)} %constant_dynamic-slice_fusion.vel), channel_id=1, source_target_pairs={{0,1},{1,2},{2,3},{3,4},{4,5},{5,6},{6,7},{7,8},{8,9},{9,10},{10,1... | collective-permute-start | bytes 196616 | tf_op jit(solution)/shard_map/ppermute | solution.py:256
  47.6 5.7 %collective-permute-done.5.vel_left = f32[2,8,8,128]{3,2,1,0:T(8,128)S(1)} collective-permute-done((f32[2,8,8,128]{3,2,1,0:T(8,128)S(1)}, f32[2,8,8,128]{3,2,1,0:T(8,128)S(1)}, u32[]{:S(2)}, u32[]{:S(2)}) %collective-permute-start.5) | collective-permute-done | bytes 65568 | tf_op jit(solution)/shard_map/ppermute | solution.py:256
  53.4 1.9 %collective-permute-start.8 = (f32[3,2,8,8,128]{4,3,2,1,0:T(8,128)S(1)}, f32[3,2,8,8,128]{4,3,2,1,0:T(8,128)S(1)}, u32[]{:S(2)}, u32[]{:S(2)}) collective-permute-start(f32[3,2,8,8,128]{4,3,2,1,0:T(8,128)S(1)} %pad_maximum_fusion.1), channel_id=1, source_target_pairs={{0,29},{1,30},{2,31},{3,0},{4,1},{5,2},{6,3},{7,4},{8,5},{9,6},{10... | collective-permute-start | bytes 589832 | tf_op jit(solution)/shard_map/ppermute | solution.py:256
  55.3 3.6 %collective-permute-start.7 = (f32[3,2,8,8,128]{4,3,2,1,0:T(8,128)S(1)}, f32[3,2,8,8,128]{4,3,2,1,0:T(8,128)S(1)}, u32[]{:S(2)}, u32[]{:S(2)}) collective-permute-start(f32[3,2,8,8,128]{4,3,2,1,0:T(8,128)S(1)} %pad_maximum_fusion.1), channel_id=1, source_target_pairs={{0,3},{1,4},{2,5},{3,6},{4,7},{5,8},{6,9},{7,10},{8,11},{9,12},{10... | collective-permute-start | bytes 589832 | tf_op jit(solution)/shard_map/ppermute | solution.py:256
  60.3 2.7 %collective-permute-done.8.vel_far_right = f32[3,2,8,8,128]{4,3,2,1,0:T(8,128)S(1)} collective-permute-done((f32[3,2,8,8,128]{4,3,2,1,0:T(8,128)S(1)}, f32[3,2,8,8,128]{4,3,2,1,0:T(8,128)S(1)}, u32[]{:S(2)}, u32[]{:S(2)}) %collective-permute-start.8) | collective-permute-done | bytes 196640 | tf_op jit(solution)/shard_map/ppermute | solution.py:256
  63.0 4.4 %collective-permute-done.7.vel_far_left = f32[3,2,8,8,128]{4,3,2,1,0:T(8,128)S(1)} collective-permute-done((f32[3,2,8,8,128]{4,3,2,1,0:T(8,128)S(1)}, f32[3,2,8,8,128]{4,3,2,1,0:T(8,128)S(1)}, u32[]{:S(2)}, u32[]{:S(2)}) %collective-permute-start.7) | collective-permute-done | bytes 196640 | tf_op jit(solution)/shard_map/ppermute | solution.py:256
  67.4 6.5 %forward.1 = (f32[8,8,16,128]{3,2,1,0:T(8,128)S(1)}, f32[32,8,256]{2,1,0:T(8,128)S(1)}, f32[72,16,128]{2,1,0:T(8,128)S(1)}) custom-call(s32[1,1,2]{2,1,0:T(1,128)S(1)} %copy-done.1, s32[1]{0:T(128)S(6)} %copy.16.source, s32[1]{0:T(128)S(6)} %copy.17.checkpoint, f32[1,64]{1,0:T(1,128)S(1)} %copy-done.3, f32[1,64,256]{2,1,0:T(8,128)S(1)} %copy-done, ...), custom_call_target="tpu_custom_call" | custom-call | tf_op jit(solution)/shard_map/forward/pallas_call | solution.py:289
  74.0 16.2 %all_to_all.20 = f32[32,1,8,256]{3,2,1,0:T(8,128)S(1)} all-to-all(f32[32,1,8,256]{3,2,1,0:T(8,128)S(1)} %bitcast.19), channel_id=1, replica_groups=mesh['x'=4,'yh'=4,'yl'=2,'z'=8,'c'=2] {'yl','z','c'}, dimensions={0} | all-to-all | bytes 524288 | tf_op jit(solution)/shard_map/all_to_all | solution.py:312
  90.1 6.8 %adjoint.1 = f32[16,8,8,128]{3,2,1,0:T(8,128)S(1)} custom-call(s32[1,1,2]{2,1,0:T(1,128)S(1)} %copy-done.1, s32[1,256]{1,0:T(1,128)S(1)} %copy-done.2, f32[32,8,256]{2,1,0:T(8,128)S(1)} %bitcast.18, f32[4,8,16,128]{3,2,1,0:T(8,128)S(1)} %constant_dynamic-update-slice_fusion.own, f32[4,8,16,128]{3,2,1,0:T(8,128)S(1)} %collective-permute-done.other, ...), custom_call_target="tpu_custom_call" | custom-call | tf_op jit(solution)/shard_map/adjoint/pallas_call | solution.py:314
  97.0 26.2 %all_to_all.21 = f32[16,8,8,128]{3,2,1,0:T(8,128)S(1)} all-to-all(f32[16,8,8,128]{3,2,1,0:T(8,128)S(1)} %adjoint.1), channel_id=1, replica_groups=mesh['x'=4,'yh'=4,'yl'=2,'z'=8,'c'=2] {'x','yh'}, dimensions={0} | all-to-all | bytes 1048576 | tf_op jit(solution)/shard_map/all_to_all | solution.py:333
  (29 shorter events, 2.9 us)
Async XLA Ops:
  0.0 0.9 copy-start.4
  0.9 0.8 copy-start.5
  1.7 0.8 copy-start.6
  2.6 3.4 %collective-permute-start = (f32[4,8,16,128]{3,2,1,0:T(8,128)S(1)}, f32[4,8,16,128]{3,2,1,0:T(8,128)S(1)}, u32[]{:S(2)}, u32[]{:S(2)}) collective-permute-start(f32[4,8,16,128]{3,2,1,0:T(8,128)S(1)} %constant_dynamic-update-slice_fusion.own), channel_id=1, source_target_pairs={{0,1},{1,0},{2,3},{3,2},{4,5},{5,4},{6,7},{7,6},{8,9},{9,8},{10,11... | collective-permute-start | bytes 786440 | tf_op jit(solution)/shard_map/ppermute | solution.py:259
  6.0 4.3 %copy-start.7 = (f32[1,8,8,128]{3,2,1,0:T(8,128)S(1)}, f32[1,8,8,128]{3,2,1,0:T(8,128)}, u32[]{:S(2)}) copy-start(f32[1,8,8,128]{3,2,1,0:T(8,128)} %param.11) | copy-start | bytes 98308
  6.0 18.0 %collective-permute-start.1 = (f32[2,4,8,16,128]{4,3,2,1,0:T(8,128)S(1)}, f32[2,4,8,16,128]{4,3,2,1,0:T(8,128)S(1)}, u32[]{:S(2)}, u32[]{:S(2)}) collective-permute-start(f32[2,4,8,16,128]{4,3,2,1,0:T(8,128)S(1)} %pad_maximum_fusion), channel_id=1, source_target_pairs={{0,2},{1,31},{2,4},{3,1},{4,6},{5,3},{6,8},{7,5},{8,10},{9,7},{10,... | collective-permute-start | bytes 1572872 | tf_op jit(solution)/shard_map/ppermute | solution.py:262
  11.0 16.0 %all-to-all-start = ((f32[4,1,8,8,128]{4,3,2,1,0:T(8,128)}), f32[4,1,8,8,128]{4,3,2,1,0:T(8,128)S(1)}, u32[]{:S(2)}, u32[]{:S(2)}) async-start(f32[4,1,8,8,128]{4,3,2,1,0:T(8,128)} %broadcast_in_dim.23), calls=%async_computation | async-start | bytes 262144 | tf_op jit(solution)/shard_map/all_to_all | solution.py:265
  24.0 15.0 %collective-permute-start.2 = (f32[2,4,8,16,128]{4,3,2,1,0:T(8,128)S(1)}, f32[2,4,8,16,128]{4,3,2,1,0:T(8,128)S(1)}, u32[]{:S(2)}, u32[]{:S(2)}) collective-permute-start(f32[2,4,8,16,128]{4,3,2,1,0:T(8,128)S(1)} %collective-permute-done.1.near), channel_id=1, source_target_pairs={{0,2},{1,31},{2,4},{3,1},{4,6},{5,3},{6,8},{7,5},{8,10},{9,7},{10,... | collective-permute-start | bytes 1572872 | tf_op jit(solution)/shard_map/ppermute | solution.py:262
  27.8 13.2 %all-to-all-start.1 = ((f32[4,4,1,8,8,128]{5,4,3,1,2,0:T(8,128)}), f32[4,4,1,8,8,128]{5,4,3,1,2,0:T(8,128)S(1)}, u32[]{:S(2)}, u32[]{:S(2)}) async-start(f32[4,4,1,8,8,128]{5,4,3,1,2,0:T(8,128)} %broadcast_in_dim.25), calls=%async_computation.1 | async-start | bytes 1048576 | tf_op jit(solution)/shard_map/all_to_all | solution.py:269
  32.1 0.7 copy-start.1
  32.9 34.5 %collective-permute-start.3 = (f32[2,4,8,16,128]{4,3,2,1,0:T(8,128)S(1)}, f32[2,4,8,16,128]{4,3,2,1,0:T(8,128)S(1)}, u32[]{:S(2)}, u32[]{:S(2)}) collective-permute-start(f32[2,4,8,16,128]{4,3,2,1,0:T(8,128)S(1)} %collective-permute-done.1.near), channel_id=1, source_target_pairs={{0,1},{1,0},{2,3},{3,2},{4,5},{5,4},{6,7},{7,6},{8,9},{9,8},{10,11... | collective-permute-start | bytes 1572872 | tf_op jit(solution)/shard_map/ppermute | solution.py:259
  39.1 28.4 %collective-permute-start.4 = (f32[2,4,8,16,128]{4,3,2,1,0:T(8,128)S(1)}, f32[2,4,8,16,128]{4,3,2,1,0:T(8,128)S(1)}, u32[]{:S(2)}, u32[]{:S(2)}) collective-permute-start(f32[2,4,8,16,128]{4,3,2,1,0:T(8,128)S(1)} %collective-permute-done.2.far), channel_id=1, source_target_pairs={{0,1},{1,0},{2,3},{3,2},{4,5},{5,4},{6,7},{7,6},{8,9},{9,8},{10,11... | collective-permute-start | bytes 1572872 | tf_op jit(solution)/shard_map/ppermute | solution.py:259
  41.0 6.6 %collective-permute-start.6 = (f32[2,8,8,128]{3,2,1,0:T(8,128)S(1)}, f32[2,8,8,128]{3,2,1,0:T(8,128)S(1)}, u32[]{:S(2)}, u32[]{:S(2)}) collective-permute-start(f32[2,8,8,128]{3,2,1,0:T(8,128)S(1)} %constant_dynamic-slice_fusion.vel), channel_id=1, source_target_pairs={{0,31},{1,0},{2,1},{3,2},{4,3},{5,4},{6,5},{7,6},{8,7},{9,8},{10,9... | collective-permute-start | bytes 196616 | tf_op jit(solution)/shard_map/ppermute | solution.py:256
  45.7 7.7 %collective-permute-start.5 = (f32[2,8,8,128]{3,2,1,0:T(8,128)S(1)}, f32[2,8,8,128]{3,2,1,0:T(8,128)S(1)}, u32[]{:S(2)}, u32[]{:S(2)}) collective-permute-start(f32[2,8,8,128]{3,2,1,0:T(8,128)S(1)} %constant_dynamic-slice_fusion.vel), channel_id=1, source_target_pairs={{0,1},{1,2},{2,3},{3,4},{4,5},{5,6},{6,7},{7,8},{8,9},{9,10},{10,1... | collective-permute-start | bytes 196616 | tf_op jit(solution)/shard_map/ppermute | solution.py:256
  53.4 14.1 %copy-start = (f32[1,64,256]{2,1,0:T(8,128)S(1)}, f32[1,64,256]{2,1,0:T(8,128)}, u32[]{:S(2)}) copy-start(f32[1,64,256]{2,1,0:T(8,128)} %observed.1) | copy-start | bytes 196612
  53.4 9.6 %collective-permute-start.8 = (f32[3,2,8,8,128]{4,3,2,1,0:T(8,128)S(1)}, f32[3,2,8,8,128]{4,3,2,1,0:T(8,128)S(1)}, u32[]{:S(2)}, u32[]{:S(2)}) collective-permute-start(f32[3,2,8,8,128]{4,3,2,1,0:T(8,128)S(1)} %pad_maximum_fusion.1), channel_id=1, source_target_pairs={{0,29},{1,30},{2,31},{3,0},{4,1},{5,2},{6,3},{7,4},{8,5},{9,6},{10... | collective-permute-start | bytes 589832 | tf_op jit(solution)/shard_map/ppermute | solution.py:256
  55.3 12.1 %collective-permute-start.7 = (f32[3,2,8,8,128]{4,3,2,1,0:T(8,128)S(1)}, f32[3,2,8,8,128]{4,3,2,1,0:T(8,128)S(1)}, u32[]{:S(2)}, u32[]{:S(2)}) collective-permute-start(f32[3,2,8,8,128]{4,3,2,1,0:T(8,128)S(1)} %pad_maximum_fusion.1), channel_id=1, source_target_pairs={{0,3},{1,4},{2,5},{3,6},{4,7},{5,8},{6,9},{7,10},{8,11},{9,12},{10... | collective-permute-start | bytes 589832 | tf_op jit(solution)/shard_map/ppermute | solution.py:256
  59.6 7.8 %copy-start.2 = (s32[1,256]{1,0:T(1,128)S(1)}, s32[1,256]{1,0:T(1,128)}, u32[]{:S(2)}) copy-start(s32[1,256]{1,0:T(1,128)} %receivers.3) | copy-start | bytes 3076
  59.6 7.8 %copy-start.3 = (f32[1,64]{1,0:T(1,128)S(1)}, f32[1,64]{1,0:T(1,128)}, u32[]{:S(2)}) copy-start(f32[1,64]{1,0:T(1,128)} %wavelet.1) | copy-start | bytes 772

commit v4 on v3

--- a/solution.py
+++ b/solution.py
@@ -231,6 +231,25 @@
         out[first_row + k] = 2.0 / (speed * speed * speed) * image[:, 8 * k : 8 * k + 8, :]
 
 
+def pack_kernel(a, b, c, d, out, sems):
+    copies = [pltpu.make_async_copy(ref.at[0], out.at[k], sems.at[k]) for k, ref in enumerate((a, b, c, d))]
+    for copy in copies:
+        copy.start()
+    for copy in copies:
+        copy.wait()
+
+
+def pack(*fields):
+    return pl.pallas_call(
+        pack_kernel,
+        in_specs=[pl.BlockSpec(memory_space=pltpu.HBM)] * 4,
+        out_specs=pl.BlockSpec(memory_space=pltpu.VMEM),
+        out_shape=jax.ShapeDtypeStruct((4,) + fields[0].shape[1:], jnp.float32),
+        scratch_shapes=[pltpu.SemaphoreType.DMA((4,))],
+        name="pack",
+    )(*fields)
+
+
 def in_vmem(count):
     return [pl.BlockSpec(memory_space=pltpu.VMEM)] * count
 
@@ -261,7 +280,7 @@
     def next_chip(cells):
         return lax.ppermute(cells, DOM, [(i, (i + (-2 if i % 2 else 2)) % SLABS) for i in range(SLABS)])
 
-    own = jnp.concatenate([forward_previous, forward_current, adjoint_next, adjoint_current], axis=0)
+    own = pack(forward_previous, forward_current, adjoint_next, adjoint_current)
     column = lax.all_to_all(
         jnp.broadcast_to(velocity[None], (4,) + velocity.shape), "yh", 0, 0, tiled=True
     )
@@ -285,7 +304,7 @@
     f32 = jnp.float32
     padded = pltpu.VMEM((2, PLANES, AY + 2 * PAD, TZ), f32)
     matrix = pltpu.VMEM((2 * TZ, 2 * TZ), jnp.bfloat16)
-    limit = pltpu.CompilerParams(vmem_limit_bytes=32 << 20)
+    limit = pltpu.CompilerParams(vmem_limit_bytes=16 << 20)
     curvature, misfit, courant = pl.pallas_call(
         forward_kernel,
         in_specs=in_smem(4) + in_vmem(13),

time: 125 us -> 125 us (level)
  local copies, waits for them, and re-layouts: 4.77 us -> 2.21 us
  Pallas kernels: 13.3 us -> 14.7 us
    unnamed x19 -> x12, local copies, waits for them, and re-layouts: 3.22 us -> 0.68 us
    pallas_call x0 -> x1, Pallas kernels: none -> 1.67 us  [pack(): pl.pallas_call(pack_kernel, in_specs=[pl.BlockSpec(memory_space=pltpu.HBM...]
where the time goes in v4:
time: 125 us; the launch traced here: 124 us
  blocking collectives  42.4 us (34%)
  starting transfers between devices  38.9 us (31%)
  waiting for transfers between devices  22.4 us (18%)
  Pallas kernels  14.7 us (12%)
  local copies, waits for them, and re-layouts  2.21 us (2%)
  between operations  1.69 us (1%)
  other arithmetic  1.65 us (1%)
    all_to_all x1, blocking collectives, inner(): landed = lax.all_to_all(terms, SHOT, 0, 0, tiled=True)  26.3 us
    all_to_all x1, blocking collectives, inner(): lax.all_to_all(misfit[:, None], DOM, 0, 0, tiled=True)  16.2 us
    ppermute x4, waiting for transfers between devices, shift(): lax.ppermute(cells, DOM, [(i, (i + by) % SLABS) for i in range(SLABS)])  12.9 us
    ppermute x4, starting transfers between devices, shift(): lax.ppermute(cells, DOM, [(i, (i + by) % SLABS) for i in range(SLABS)])  12.3 us
    ppermute x3, starting transfers between devices, partner(): return lax.ppermute(cells, DOM, [(i, i ^ 1) for i in range(SLABS)])  9.96 us
    ppermute x2, waiting for transfers between devices, next_chip(): lax.ppermute(cells, DOM, [(i, (i + (-2 if i % 2 else 2)) % SLABS) for i i...  6.83 us
    pallas_call x1, Pallas kernels, inner(): pl.pallas_call(adjoint_kernel, in_specs=in_smem(1) + in_vmem(11), out_spe...  6.71 us
    pallas_call x1, Pallas kernels, inner(): pl.pallas_call(forward_kernel, in_specs=in_smem(4) + in_vmem(13), out_spe...  6.3 us
  transfers between devices with their start and end apart: 11, of which 6 were waited for; matrix products, arithmetic and copies ran while one was open for 1% of the time, Pallas kernels for 0%

profile of v4, /device:TPU:8, one launch (start us, length us, event | category | flops | bytes accessed | tf_op | source)
XLA Modules:
  0.0 124.0 jit_solution(7003887567888621043)
XLA Ops:
  0.0 1.7 %pack.1.own = f32[4,8,16,128]{3,2,1,0:T(8,128)} custom-call(f32[1,8,16,128]{3,2,1,0:T(8,128)} %a.1, f32[1,8,16,128]{3,2,1,0:T(8,128)} %b.1, f32[1,8,16,128]{3,2,1,0:T(8,128)} %c.1, f32[1,8,16,128]{3,2,1,0:T(8,128)} %d.1), custom_call_target="tpu_custom_call" | custom-call | tf_op jit(solution)/shard_map/pack/pallas_call | solution.py:243
  1.7 1.9 %collective-permute-start = (f32[4,8,16,128]{3,2,1,0:T(8,128)}, f32[4,8,16,128]{3,2,1,0:T(8,128)S(1)}, u32[]{:S(2)}, u32[]{:S(2)}) collective-permute-start(f32[4,8,16,128]{3,2,1,0:T(8,128)} %pack.1.own), channel_id=1, source_target_pairs={{0,1},{1,0},{2,3},{3,2},{4,5},{5,4},{6,7},{7,6},{8,9},{9,8},{10,11... | collective-permute-start | bytes 786440 | tf_op jit(solution)/shard_map/ppermute | solution.py:278
  3.6 1.7 %collective-permute-done.other = f32[4,8,16,128]{3,2,1,0:T(8,128)S(1)} collective-permute-done((f32[4,8,16,128]{3,2,1,0:T(8,128)}, f32[4,8,16,128]{3,2,1,0:T(8,128)S(1)}, u32[]{:S(2)}, u32[]{:S(2)}) %collective-permute-start) | collective-permute-done | bytes 262176 | tf_op jit(solution)/shard_map/ppermute | solution.py:278
  5.3 1.0 pad_maximum_fusion
  6.3 4.3 %collective-permute-start.1 = (f32[2,4,8,16,128]{4,3,2,1,0:T(8,128)S(1)}, f32[2,4,8,16,128]{4,3,2,1,0:T(8,128)S(1)}, u32[]{:S(2)}, u32[]{:S(2)}) collective-permute-start(f32[2,4,8,16,128]{4,3,2,1,0:T(8,128)S(1)} %pad_maximum_fusion), channel_id=1, source_target_pairs={{0,2},{1,31},{2,4},{3,1},{4,6},{5,3},{6,8},{7,5},{8,10},{9,7},{10,... | collective-permute-start | bytes 1572872 | tf_op jit(solution)/shard_map/ppermute | solution.py:281
  11.3 6.2 %all-to-all-start = ((f32[4,1,8,8,128]{4,3,2,1,0:T(8,128)}), f32[4,1,8,8,128]{4,3,2,1,0:T(8,128)S(1)}, u32[]{:S(2)}, u32[]{:S(2)}) async-start(f32[4,1,8,8,128]{4,3,2,1,0:T(8,128)} %broadcast_in_dim.23), calls=%async_computation | async-start | bytes 262144 | tf_op jit(solution)/shard_map/all_to_all | solution.py:284
  17.5 6.8 %collective-permute-done.1.near = f32[2,4,8,16,128]{4,3,2,1,0:T(8,128)S(1)} collective-permute-done((f32[2,4,8,16,128]{4,3,2,1,0:T(8,128)S(1)}, f32[2,4,8,16,128]{4,3,2,1,0:T(8,128)S(1)}, u32[]{:S(2)}, u32[]{:S(2)}) %collective-permute-start.1) | collective-permute-done | bytes 524320 | tf_op jit(solution)/shard_map/ppermute | solution.py:281
  24.3 1.9 %collective-permute-start.2 = (f32[2,4,8,16,128]{4,3,2,1,0:T(8,128)S(1)}, f32[2,4,8,16,128]{4,3,2,1,0:T(8,128)S(1)}, u32[]{:S(2)}, u32[]{:S(2)}) collective-permute-start(f32[2,4,8,16,128]{4,3,2,1,0:T(8,128)S(1)} %collective-permute-done.1.near), channel_id=1, source_target_pairs={{0,2},{1,31},{2,4},{3,1},{4,6},{5,3},{6,8},{7,5},{8,10},{9,7},{10,... | collective-permute-start | bytes 1572872 | tf_op jit(solution)/shard_map/ppermute | solution.py:281
  26.2 1.0 all-to-all-done
  27.2 0.8 broadcast_in_dim.25
  28.1 4.3 %all-to-all-start.1 = ((f32[4,4,1,8,8,128]{5,4,3,1,2,0:T(8,128)}), f32[4,4,1,8,8,128]{5,4,3,1,2,0:T(8,128)S(1)}, u32[]{:S(2)}, u32[]{:S(2)}) async-start(f32[4,4,1,8,8,128]{5,4,3,1,2,0:T(8,128)} %broadcast_in_dim.25), calls=%async_computation.1 | async-start | bytes 1048576 | tf_op jit(solution)/shard_map/all_to_all | solution.py:288
  33.2 6.1 %collective-permute-start.3 = (f32[2,4,8,16,128]{4,3,2,1,0:T(8,128)S(1)}, f32[2,4,8,16,128]{4,3,2,1,0:T(8,128)S(1)}, u32[]{:S(2)}, u32[]{:S(2)}) collective-permute-start(f32[2,4,8,16,128]{4,3,2,1,0:T(8,128)S(1)} %collective-permute-done.1.near), channel_id=1, source_target_pairs={{0,1},{1,0},{2,3},{3,2},{4,5},{5,4},{6,7},{7,6},{8,9},{9,8},{10,11... | collective-permute-start | bytes 1572872 | tf_op jit(solution)/shard_map/ppermute | solution.py:278
  39.3 1.9 %collective-permute-start.4 = (f32[2,4,8,16,128]{4,3,2,1,0:T(8,128)S(1)}, f32[2,4,8,16,128]{4,3,2,1,0:T(8,128)S(1)}, u32[]{:S(2)}, u32[]{:S(2)}) collective-permute-start(f32[2,4,8,16,128]{4,3,2,1,0:T(8,128)S(1)} %collective-permute-done.2.far), channel_id=1, source_target_pairs={{0,1},{1,0},{2,3},{3,2},{4,5},{5,4},{6,7},{7,6},{8,9},{9,8},{10,11... | collective-permute-start | bytes 1572872 | tf_op jit(solution)/shard_map/ppermute | solution.py:278
  41.3 4.8 %collective-permute-start.6 = (f32[2,8,8,128]{3,2,1,0:T(8,128)S(1)}, f32[2,8,8,128]{3,2,1,0:T(8,128)S(1)}, u32[]{:S(2)}, u32[]{:S(2)}) collective-permute-start(f32[2,8,8,128]{3,2,1,0:T(8,128)S(1)} %constant_dynamic-slice_fusion.vel), channel_id=1, source_target_pairs={{0,31},{1,0},{2,1},{3,2},{4,3},{5,4},{6,5},{7,6},{8,7},{9,8},{10,9... | collective-permute-start | bytes 196616 | tf_op jit(solution)/shard_map/ppermute | solution.py:275
  46.1 1.9 %collective-permute-start.5 = (f32[2,8,8,128]{3,2,1,0:T(8,128)S(1)}, f32[2,8,8,128]{3,2,1,0:T(8,128)S(1)}, u32[]{:S(2)}, u32[]{:S(2)}) collective-permute-start(f32[2,8,8,128]{3,2,1,0:T(8,128)S(1)} %constant_dynamic-slice_fusion.vel), channel_id=1, source_target_pairs={{0,1},{1,2},{2,3},{3,4},{4,5},{5,6},{6,7},{7,8},{8,9},{9,10},{10,1... | collective-permute-start | bytes 196616 | tf_op jit(solution)/shard_map/ppermute | solution.py:275
  48.1 5.7 %collective-permute-done.5.vel_left = f32[2,8,8,128]{3,2,1,0:T(8,128)S(1)} collective-permute-done((f32[2,8,8,128]{3,2,1,0:T(8,128)S(1)}, f32[2,8,8,128]{3,2,1,0:T(8,128)S(1)}, u32[]{:S(2)}, u32[]{:S(2)}) %collective-permute-start.5) | collective-permute-done | bytes 65568 | tf_op jit(solution)/shard_map/ppermute | solution.py:275
  53.8 1.9 %collective-permute-start.8 = (f32[3,2,8,8,128]{4,3,2,1,0:T(8,128)S(1)}, f32[3,2,8,8,128]{4,3,2,1,0:T(8,128)S(1)}, u32[]{:S(2)}, u32[]{:S(2)}) collective-permute-start(f32[3,2,8,8,128]{4,3,2,1,0:T(8,128)S(1)} %pad_maximum_fusion.1), channel_id=1, source_target_pairs={{0,29},{1,30},{2,31},{3,0},{4,1},{5,2},{6,3},{7,4},{8,5},{9,6},{10... | collective-permute-start | bytes 589832 | tf_op jit(solution)/shard_map/ppermute | solution.py:275
  55.7 3.6 %collective-permute-start.7 = (f32[3,2,8,8,128]{4,3,2,1,0:T(8,128)S(1)}, f32[3,2,8,8,128]{4,3,2,1,0:T(8,128)S(1)}, u32[]{:S(2)}, u32[]{:S(2)}) collective-permute-start(f32[3,2,8,8,128]{4,3,2,1,0:T(8,128)S(1)} %pad_maximum_fusion.1), channel_id=1, source_target_pairs={{0,3},{1,4},{2,5},{3,6},{4,7},{5,8},{6,9},{7,10},{8,11},{9,12},{10... | collective-permute-start | bytes 589832 | tf_op jit(solution)/shard_map/ppermute | solution.py:275
  60.7 2.7 %collective-permute-done.8.vel_far_right = f32[3,2,8,8,128]{4,3,2,1,0:T(8,128)S(1)} collective-permute-done((f32[3,2,8,8,128]{4,3,2,1,0:T(8,128)S(1)}, f32[3,2,8,8,128]{4,3,2,1,0:T(8,128)S(1)}, u32[]{:S(2)}, u32[]{:S(2)}) %collective-permute-start.8) | collective-permute-done | bytes 196640 | tf_op jit(solution)/shard_map/ppermute | solution.py:275
  63.4 4.4 %collective-permute-done.7.vel_far_left = f32[3,2,8,8,128]{4,3,2,1,0:T(8,128)S(1)} collective-permute-done((f32[3,2,8,8,128]{4,3,2,1,0:T(8,128)S(1)}, f32[3,2,8,8,128]{4,3,2,1,0:T(8,128)S(1)}, u32[]{:S(2)}, u32[]{:S(2)}) %collective-permute-start.7) | collective-permute-done | bytes 196640 | tf_op jit(solution)/shard_map/ppermute | solution.py:275
  67.9 6.3 %forward.1 = (f32[8,8,16,128]{3,2,1,0:T(8,128)S(1)}, f32[32,8,256]{2,1,0:T(8,128)S(1)}, f32[72,16,128]{2,1,0:T(8,128)S(1)}) custom-call(s32[1,1,2]{2,1,0:T(1,128)S(1)} %copy-done.2, s32[1]{0:T(128)S(6)} %copy.13.source, s32[1]{0:T(128)S(6)} %copy.14.checkpoint, f32[1,64]{1,0:T(1,128)S(1)} %copy-done.4, f32[1,64,256]{2,1,0:T(8,128)S(1)} %copy-done.1, ...), custom_call_target="tpu_custom_call" | custom-call | tf_op jit(solution)/shard_map/forward/pallas_call | solution.py:308
  74.2 16.2 %all_to_all.20 = f32[32,1,8,256]{3,2,1,0:T(8,128)S(1)} all-to-all(f32[32,1,8,256]{3,2,1,0:T(8,128)S(1)} %bitcast.19), channel_id=1, replica_groups=mesh['x'=4,'yh'=4,'yl'=2,'z'=8,'c'=2] {'yl','z','c'}, dimensions={0} | all-to-all | bytes 524288 | tf_op jit(solution)/shard_map/all_to_all | solution.py:331
  90.4 6.7 %adjoint.1 = f32[16,8,8,128]{3,2,1,0:T(8,128)S(1)} custom-call(s32[1,1,2]{2,1,0:T(1,128)S(1)} %copy-done.2, s32[1,256]{1,0:T(1,128)S(1)} %copy-done.3, f32[32,8,256]{2,1,0:T(8,128)S(1)} %bitcast.18, f32[4,8,16,128]{3,2,1,0:T(8,128)S(1)} %copy-done, f32[4,8,16,128]{3,2,1,0:T(8,128)S(1)} %collective-permute-done.other, ...), custom_call_target="tpu_custom_call" | custom-call | tf_op jit(solution)/shard_map/adjoint/pallas_call | solution.py:333
  97.1 26.3 %all_to_all.21 = f32[16,8,8,128]{3,2,1,0:T(8,128)S(1)} all-to-all(f32[16,8,8,128]{3,2,1,0:T(8,128)S(1)} %adjoint.1), channel_id=1, replica_groups=mesh['x'=4,'yh'=4,'yl'=2,'z'=8,'c'=2] {'x','yh'}, dimensions={0} | all-to-all | bytes 1048576 | tf_op jit(solution)/shard_map/all_to_all | solution.py:352
  (22 shorter events, 2.0 us)
Async XLA Ops:
  1.7 3.6 %collective-permute-start = (f32[4,8,16,128]{3,2,1,0:T(8,128)}, f32[4,8,16,128]{3,2,1,0:T(8,128)S(1)}, u32[]{:S(2)}, u32[]{:S(2)}) collective-permute-start(f32[4,8,16,128]{3,2,1,0:T(8,128)} %pack.1.own), channel_id=1, source_target_pairs={{0,1},{1,0},{2,3},{3,2},{4,5},{5,4},{6,7},{7,6},{8,9},{9,8},{10,11... | collective-permute-start | bytes 786440 | tf_op jit(solution)/shard_map/ppermute | solution.py:278
  5.3 5.3 %copy-start.5 = (f32[1,8,8,128]{3,2,1,0:T(8,128)S(1)}, f32[1,8,8,128]{3,2,1,0:T(8,128)}, u32[]{:S(2)}) copy-start(f32[1,8,8,128]{3,2,1,0:T(8,128)} %param.11) | copy-start | bytes 98308
  6.3 18.0 %collective-permute-start.1 = (f32[2,4,8,16,128]{4,3,2,1,0:T(8,128)S(1)}, f32[2,4,8,16,128]{4,3,2,1,0:T(8,128)S(1)}, u32[]{:S(2)}, u32[]{:S(2)}) collective-permute-start(f32[2,4,8,16,128]{4,3,2,1,0:T(8,128)S(1)} %pad_maximum_fusion), channel_id=1, source_target_pairs={{0,2},{1,31},{2,4},{3,1},{4,6},{5,3},{6,8},{7,5},{8,10},{9,7},{10,... | collective-permute-start | bytes 1572872 | tf_op jit(solution)/shard_map/ppermute | solution.py:281
  11.3 16.0 %all-to-all-start = ((f32[4,1,8,8,128]{4,3,2,1,0:T(8,128)}), f32[4,1,8,8,128]{4,3,2,1,0:T(8,128)S(1)}, u32[]{:S(2)}, u32[]{:S(2)}) async-start(f32[4,1,8,8,128]{4,3,2,1,0:T(8,128)} %broadcast_in_dim.23), calls=%async_computation | async-start | bytes 262144 | tf_op jit(solution)/shard_map/all_to_all | solution.py:284
  24.3 15.0 %collective-permute-start.2 = (f32[2,4,8,16,128]{4,3,2,1,0:T(8,128)S(1)}, f32[2,4,8,16,128]{4,3,2,1,0:T(8,128)S(1)}, u32[]{:S(2)}, u32[]{:S(2)}) collective-permute-start(f32[2,4,8,16,128]{4,3,2,1,0:T(8,128)S(1)} %collective-permute-done.1.near), channel_id=1, source_target_pairs={{0,2},{1,31},{2,4},{3,1},{4,6},{5,3},{6,8},{7,5},{8,10},{9,7},{10,... | collective-permute-start | bytes 1572872 | tf_op jit(solution)/shard_map/ppermute | solution.py:281
  28.1 13.2 %all-to-all-start.1 = ((f32[4,4,1,8,8,128]{5,4,3,1,2,0:T(8,128)}), f32[4,4,1,8,8,128]{5,4,3,1,2,0:T(8,128)S(1)}, u32[]{:S(2)}, u32[]{:S(2)}) async-start(f32[4,4,1,8,8,128]{5,4,3,1,2,0:T(8,128)} %broadcast_in_dim.25), calls=%async_computation.1 | async-start | bytes 1048576 | tf_op jit(solution)/shard_map/all_to_all | solution.py:288
  32.4 0.7 copy-start.2
  33.2 34.6 %collective-permute-start.3 = (f32[2,4,8,16,128]{4,3,2,1,0:T(8,128)S(1)}, f32[2,4,8,16,128]{4,3,2,1,0:T(8,128)S(1)}, u32[]{:S(2)}, u32[]{:S(2)}) collective-permute-start(f32[2,4,8,16,128]{4,3,2,1,0:T(8,128)S(1)} %collective-permute-done.1.near), channel_id=1, source_target_pairs={{0,1},{1,0},{2,3},{3,2},{4,5},{5,4},{6,7},{7,6},{8,9},{9,8},{10,11... | collective-permute-start | bytes 1572872 | tf_op jit(solution)/shard_map/ppermute | solution.py:278
  39.3 28.5 %collective-permute-start.4 = (f32[2,4,8,16,128]{4,3,2,1,0:T(8,128)S(1)}, f32[2,4,8,16,128]{4,3,2,1,0:T(8,128)S(1)}, u32[]{:S(2)}, u32[]{:S(2)}) collective-permute-start(f32[2,4,8,16,128]{4,3,2,1,0:T(8,128)S(1)} %collective-permute-done.2.far), channel_id=1, source_target_pairs={{0,1},{1,0},{2,3},{3,2},{4,5},{5,4},{6,7},{7,6},{8,9},{9,8},{10,11... | collective-permute-start | bytes 1572872 | tf_op jit(solution)/shard_map/ppermute | solution.py:278
  41.3 26.5 %copy-start = (f32[4,8,16,128]{3,2,1,0:T(8,128)S(1)}, f32[4,8,16,128]{3,2,1,0:T(8,128)}, u32[]{:S(2)}) copy-start(f32[4,8,16,128]{3,2,1,0:T(8,128)} %pack.1.own) | copy-start | bytes 786436
  41.3 6.7 %collective-permute-start.6 = (f32[2,8,8,128]{3,2,1,0:T(8,128)S(1)}, f32[2,8,8,128]{3,2,1,0:T(8,128)S(1)}, u32[]{:S(2)}, u32[]{:S(2)}) collective-permute-start(f32[2,8,8,128]{3,2,1,0:T(8,128)S(1)} %constant_dynamic-slice_fusion.vel), channel_id=1, source_target_pairs={{0,31},{1,0},{2,1},{3,2},{4,3},{5,4},{6,5},{7,6},{8,7},{9,8},{10,9... | collective-permute-start | bytes 196616 | tf_op jit(solution)/shard_map/ppermute | solution.py:275
  46.1 7.7 %collective-permute-start.5 = (f32[2,8,8,128]{3,2,1,0:T(8,128)S(1)}, f32[2,8,8,128]{3,2,1,0:T(8,128)S(1)}, u32[]{:S(2)}, u32[]{:S(2)}) collective-permute-start(f32[2,8,8,128]{3,2,1,0:T(8,128)S(1)} %constant_dynamic-slice_fusion.vel), channel_id=1, source_target_pairs={{0,1},{1,2},{2,3},{3,4},{4,5},{5,6},{6,7},{7,8},{8,9},{9,10},{10,1... | collective-permute-start | bytes 196616 | tf_op jit(solution)/shard_map/ppermute | solution.py:275
  53.8 14.1 %copy-start.1 = (f32[1,64,256]{2,1,0:T(8,128)S(1)}, f32[1,64,256]{2,1,0:T(8,128)}, u32[]{:S(2)}) copy-start(f32[1,64,256]{2,1,0:T(8,128)} %observed.1) | copy-start | bytes 196612
  53.8 9.6 %collective-permute-start.8 = (f32[3,2,8,8,128]{4,3,2,1,0:T(8,128)S(1)}, f32[3,2,8,8,128]{4,3,2,1,0:T(8,128)S(1)}, u32[]{:S(2)}, u32[]{:S(2)}) collective-permute-start(f32[3,2,8,8,128]{4,3,2,1,0:T(8,128)S(1)} %pad_maximum_fusion.1), channel_id=1, source_target_pairs={{0,29},{1,30},{2,31},{3,0},{4,1},{5,2},{6,3},{7,4},{8,5},{9,6},{10... | collective-permute-start | bytes 589832 | tf_op jit(solution)/shard_map/ppermute | solution.py:275
  55.7 12.1 %collective-permute-start.7 = (f32[3,2,8,8,128]{4,3,2,1,0:T(8,128)S(1)}, f32[3,2,8,8,128]{4,3,2,1,0:T(8,128)S(1)}, u32[]{:S(2)}, u32[]{:S(2)}) collective-permute-start(f32[3,2,8,8,128]{4,3,2,1,0:T(8,128)S(1)} %pad_maximum_fusion.1), channel_id=1, source_target_pairs={{0,3},{1,4},{2,5},{3,6},{4,7},{5,8},{6,9},{7,10},{8,11},{9,12},{10... | collective-permute-start | bytes 589832 | tf_op jit(solution)/shard_map/ppermute | solution.py:275
  60.0 7.8 %copy-start.3 = (s32[1,256]{1,0:T(1,128)S(1)}, s32[1,256]{1,0:T(1,128)}, u32[]{:S(2)}) copy-start(s32[1,256]{1,0:T(1,128)} %receivers.3) | copy-start | bytes 3076
  60.0 7.8 %copy-start.4 = (f32[1,64]{1,0:T(1,128)S(1)}, f32[1,64]{1,0:T(1,128)}, u32[]{:S(2)}) copy-start(f32[1,64]{1,0:T(1,128)} %wavelet.1) | copy-start | bytes 772

commit v5 on v4

--- a/solution.py
+++ b/solution.py
@@ -228,7 +228,9 @@
     out[...] = jnp.zeros(out.shape, jnp.float32)
     for k in range(2):
         speed = vel[k]
-        out[first_row + k] = 2.0 / (speed * speed * speed) * image[:, 8 * k : 8 * k + 8, :]
+        target = first_row + k
+        out[target & 3, 0:TX] = 2.0 / (speed * speed * speed) * image[:, 8 * k : 8 * k + 8, :]
+        out[target & 3, TX] = jnp.full((8, TZ), target >> 2, jnp.int32).astype(jnp.float32)
 
 
 def pack_kernel(a, b, c, d, out, sems):
@@ -334,7 +336,7 @@
         adjoint_kernel,
         in_specs=in_smem(1) + in_vmem(11),
         out_specs=in_vmem(1)[0],
-        out_shape=jax.ShapeDtypeStruct((16, TX, 8, TZ), f32),
+        out_shape=jax.ShapeDtypeStruct((4, TX + 1, 8, TZ), f32),
         scratch_shapes=[
             padded,
             pltpu.VMEM(region, f32),
@@ -349,7 +351,10 @@
         aperture, receivers, misfits, *fields,
         vel, courant, curvature,
     )
-    landed = lax.all_to_all(terms, SHOT, 0, 0, tiled=True)
+    landed = lax.all_to_all(terms, "yh", 0, 0, tiled=True)
+    tags = jnp.arange(4, dtype=jnp.float32).reshape(4, 1, 1, 1, 1)
+    sums = jnp.sum(jnp.where(landed[None, :, TX:] == tags, landed[None, :, 0:TX], 0.0), axis=1)
+    landed = lax.all_to_all(sums, "x", 0, 0, tiled=True)
     return jnp.sum(landed, axis=0, keepdims=True)
 
 

time: 125 us -> 123 us (0.984)
  blocking collectives: 42.4 us -> 40.6 us
    all_to_all x1 -> x2, blocking collectives: 26.3 us -> 24.4 us  [the longest x1 16.1 us: inner(): landed = lax.all_to_all(terms, 'yh', 0, 0, tiled=True)]
where the time goes in v5:
time: 123 us; the launch traced here: 122 us
  blocking collectives  40.6 us (33%)
  starting transfers between devices  38.9 us (32%)
  waiting for transfers between devices  22.4 us (18%)
  Pallas kernels  14.7 us (12%)
  local copies, waits for them, and re-layouts  2.22 us (2%)
  between operations  1.71 us (1%)
  other arithmetic  1.68 us (1%)
    all_to_all x1, blocking collectives, inner(): lax.all_to_all(misfit[:, None], DOM, 0, 0, tiled=True)  16.2 us
    all_to_all x1, blocking collectives, inner(): landed = lax.all_to_all(terms, 'yh', 0, 0, tiled=True)  16.1 us
    ppermute x4, waiting for transfers between devices, shift(): lax.ppermute(cells, DOM, [(i, (i + by) % SLABS) for i in range(SLABS)])  12.9 us
    ppermute x4, starting transfers between devices, shift(): lax.ppermute(cells, DOM, [(i, (i + by) % SLABS) for i in range(SLABS)])  12.3 us
    ppermute x3, starting transfers between devices, partner(): return lax.ppermute(cells, DOM, [(i, i ^ 1) for i in range(SLABS)])  9.96 us
    all_to_all x1, blocking collectives, inner(): landed = lax.all_to_all(sums, 'x', 0, 0, tiled=True)  8.36 us
    ppermute x2, waiting for transfers between devices, next_chip(): lax.ppermute(cells, DOM, [(i, (i + (-2 if i % 2 else 2)) % SLABS) for i i...  6.84 us
    pallas_call x1, Pallas kernels, inner(): pl.pallas_call(adjoint_kernel, in_specs=in_smem(1) + in_vmem(11), out_spe...  6.71 us
  transfers between devices with their start and end apart: 11, of which 6 were waited for; matrix products, arithmetic and copies ran while one was open for 1% of the time, Pallas kernels for 0%

profile of v5, /device:TPU:8, one launch (start us, length us, event | category | flops | bytes accessed | tf_op | source)
XLA Modules:
  0.0 122.2 jit_solution(5370749737683500275)
XLA Ops:
  0.0 1.7 %pack.1.own = f32[4,8,16,128]{3,2,1,0:T(8,128)} custom-call(f32[1,8,16,128]{3,2,1,0:T(8,128)} %a.1, f32[1,8,16,128]{3,2,1,0:T(8,128)} %b.1, f32[1,8,16,128]{3,2,1,0:T(8,128)} %c.1, f32[1,8,16,128]{3,2,1,0:T(8,128)} %d.1), custom_call_target="tpu_custom_call" | custom-call | tf_op jit(solution)/shard_map/pack/pallas_call | solution.py:245
  1.7 1.9 %collective-permute-start = (f32[4,8,16,128]{3,2,1,0:T(8,128)}, f32[4,8,16,128]{3,2,1,0:T(8,128)S(1)}, u32[]{:S(2)}, u32[]{:S(2)}) collective-permute-start(f32[4,8,16,128]{3,2,1,0:T(8,128)} %pack.1.own), channel_id=1, source_target_pairs={{0,1},{1,0},{2,3},{3,2},{4,5},{5,4},{6,7},{7,6},{8,9},{9,8},{10,11... | collective-permute-start | bytes 786440 | tf_op jit(solution)/shard_map/ppermute | solution.py:280
  3.6 1.7 %collective-permute-done.other = f32[4,8,16,128]{3,2,1,0:T(8,128)S(1)} collective-permute-done((f32[4,8,16,128]{3,2,1,0:T(8,128)}, f32[4,8,16,128]{3,2,1,0:T(8,128)S(1)}, u32[]{:S(2)}, u32[]{:S(2)}) %collective-permute-start) | collective-permute-done | bytes 262176 | tf_op jit(solution)/shard_map/ppermute | solution.py:280
  5.3 1.0 pad_maximum_fusion
  6.3 4.3 %collective-permute-start.1 = (f32[2,4,8,16,128]{4,3,2,1,0:T(8,128)S(1)}, f32[2,4,8,16,128]{4,3,2,1,0:T(8,128)S(1)}, u32[]{:S(2)}, u32[]{:S(2)}) collective-permute-start(f32[2,4,8,16,128]{4,3,2,1,0:T(8,128)S(1)} %pad_maximum_fusion), channel_id=1, source_target_pairs={{0,2},{1,31},{2,4},{3,1},{4,6},{5,3},{6,8},{7,5},{8,10},{9,7},{10,... | collective-permute-start | bytes 1572872 | tf_op jit(solution)/shard_map/ppermute | solution.py:283
  11.3 6.2 %all-to-all-start = ((f32[4,1,8,8,128]{4,3,2,1,0:T(8,128)}), f32[4,1,8,8,128]{4,3,2,1,0:T(8,128)S(1)}, u32[]{:S(2)}, u32[]{:S(2)}) async-start(f32[4,1,8,8,128]{4,3,2,1,0:T(8,128)} %broadcast_in_dim.45), calls=%async_computation | async-start | bytes 262144 | tf_op jit(solution)/shard_map/all_to_all | solution.py:286
  17.5 6.8 %collective-permute-done.1.near = f32[2,4,8,16,128]{4,3,2,1,0:T(8,128)S(1)} collective-permute-done((f32[2,4,8,16,128]{4,3,2,1,0:T(8,128)S(1)}, f32[2,4,8,16,128]{4,3,2,1,0:T(8,128)S(1)}, u32[]{:S(2)}, u32[]{:S(2)}) %collective-permute-start.1) | collective-permute-done | bytes 524320 | tf_op jit(solution)/shard_map/ppermute | solution.py:283
  24.3 1.9 %collective-permute-start.2 = (f32[2,4,8,16,128]{4,3,2,1,0:T(8,128)S(1)}, f32[2,4,8,16,128]{4,3,2,1,0:T(8,128)S(1)}, u32[]{:S(2)}, u32[]{:S(2)}) collective-permute-start(f32[2,4,8,16,128]{4,3,2,1,0:T(8,128)S(1)} %collective-permute-done.1.near), channel_id=1, source_target_pairs={{0,2},{1,31},{2,4},{3,1},{4,6},{5,3},{6,8},{7,5},{8,10},{9,7},{10,... | collective-permute-start | bytes 1572872 | tf_op jit(solution)/shard_map/ppermute | solution.py:283
  26.2 1.0 all-to-all-done
  28.1 4.3 %all-to-all-start.1 = ((f32[4,4,1,8,8,128]{5,4,3,1,2,0:T(8,128)}), f32[4,4,1,8,8,128]{5,4,3,1,2,0:T(8,128)S(1)}, u32[]{:S(2)}, u32[]{:S(2)}) async-start(f32[4,4,1,8,8,128]{5,4,3,1,2,0:T(8,128)} %broadcast_in_dim.47), calls=%async_computation.1 | async-start | bytes 1048576 | tf_op jit(solution)/shard_map/all_to_all | solution.py:290
  33.2 6.1 %collective-permute-start.3 = (f32[2,4,8,16,128]{4,3,2,1,0:T(8,128)S(1)}, f32[2,4,8,16,128]{4,3,2,1,0:T(8,128)S(1)}, u32[]{:S(2)}, u32[]{:S(2)}) collective-permute-start(f32[2,4,8,16,128]{4,3,2,1,0:T(8,128)S(1)} %collective-permute-done.1.near), channel_id=1, source_target_pairs={{0,1},{1,0},{2,3},{3,2},{4,5},{5,4},{6,7},{7,6},{8,9},{9,8},{10,11... | collective-permute-start | bytes 1572872 | tf_op jit(solution)/shard_map/ppermute | solution.py:280
  39.4 1.9 %collective-permute-start.4 = (f32[2,4,8,16,128]{4,3,2,1,0:T(8,128)S(1)}, f32[2,4,8,16,128]{4,3,2,1,0:T(8,128)S(1)}, u32[]{:S(2)}, u32[]{:S(2)}) collective-permute-start(f32[2,4,8,16,128]{4,3,2,1,0:T(8,128)S(1)} %collective-permute-done.2.far), channel_id=1, source_target_pairs={{0,1},{1,0},{2,3},{3,2},{4,5},{5,4},{6,7},{7,6},{8,9},{9,8},{10,11... | collective-permute-start | bytes 1572872 | tf_op jit(solution)/shard_map/ppermute | solution.py:280
  41.3 4.8 %collective-permute-start.6 = (f32[2,8,8,128]{3,2,1,0:T(8,128)S(1)}, f32[2,8,8,128]{3,2,1,0:T(8,128)S(1)}, u32[]{:S(2)}, u32[]{:S(2)}) collective-permute-start(f32[2,8,8,128]{3,2,1,0:T(8,128)S(1)} %constant_dynamic-slice_fusion.vel), channel_id=1, source_target_pairs={{0,31},{1,0},{2,1},{3,2},{4,3},{5,4},{6,5},{7,6},{8,7},{9,8},{10,9... | collective-permute-start | bytes 196616 | tf_op jit(solution)/shard_map/ppermute | solution.py:277
  46.1 1.9 %collective-permute-start.5 = (f32[2,8,8,128]{3,2,1,0:T(8,128)S(1)}, f32[2,8,8,128]{3,2,1,0:T(8,128)S(1)}, u32[]{:S(2)}, u32[]{:S(2)}) collective-permute-start(f32[2,8,8,128]{3,2,1,0:T(8,128)S(1)} %constant_dynamic-slice_fusion.vel), channel_id=1, source_target_pairs={{0,1},{1,2},{2,3},{3,4},{4,5},{5,6},{6,7},{7,8},{8,9},{9,10},{10,1... | collective-permute-start | bytes 196616 | tf_op jit(solution)/shard_map/ppermute | solution.py:277
  48.1 5.7 %collective-permute-done.5.vel_left = f32[2,8,8,128]{3,2,1,0:T(8,128)S(1)} collective-permute-done((f32[2,8,8,128]{3,2,1,0:T(8,128)S(1)}, f32[2,8,8,128]{3,2,1,0:T(8,128)S(1)}, u32[]{:S(2)}, u32[]{:S(2)}) %collective-permute-start.5) | collective-permute-done | bytes 65568 | tf_op jit(solution)/shard_map/ppermute | solution.py:277
  53.8 1.9 %collective-permute-start.8 = (f32[3,2,8,8,128]{4,3,2,1,0:T(8,128)S(1)}, f32[3,2,8,8,128]{4,3,2,1,0:T(8,128)S(1)}, u32[]{:S(2)}, u32[]{:S(2)}) collective-permute-start(f32[3,2,8,8,128]{4,3,2,1,0:T(8,128)S(1)} %pad_maximum_fusion.1), channel_id=1, source_target_pairs={{0,29},{1,30},{2,31},{3,0},{4,1},{5,2},{6,3},{7,4},{8,5},{9,6},{10... | collective-permute-start | bytes 589832 | tf_op jit(solution)/shard_map/ppermute | solution.py:277
  55.8 3.6 %collective-permute-start.7 = (f32[3,2,8,8,128]{4,3,2,1,0:T(8,128)S(1)}, f32[3,2,8,8,128]{4,3,2,1,0:T(8,128)S(1)}, u32[]{:S(2)}, u32[]{:S(2)}) collective-permute-start(f32[3,2,8,8,128]{4,3,2,1,0:T(8,128)S(1)} %pad_maximum_fusion.1), channel_id=1, source_target_pairs={{0,3},{1,4},{2,5},{3,6},{4,7},{5,8},{6,9},{7,10},{8,11},{9,12},{10... | collective-permute-start | bytes 589832 | tf_op jit(solution)/shard_map/ppermute | solution.py:277
  60.7 2.7 %collective-permute-done.8.vel_far_right = f32[3,2,8,8,128]{4,3,2,1,0:T(8,128)S(1)} collective-permute-done((f32[3,2,8,8,128]{4,3,2,1,0:T(8,128)S(1)}, f32[3,2,8,8,128]{4,3,2,1,0:T(8,128)S(1)}, u32[]{:S(2)}, u32[]{:S(2)}) %collective-permute-start.8) | collective-permute-done | bytes 196640 | tf_op jit(solution)/shard_map/ppermute | solution.py:277
  63.4 4.4 %collective-permute-done.7.vel_far_left = f32[3,2,8,8,128]{4,3,2,1,0:T(8,128)S(1)} collective-permute-done((f32[3,2,8,8,128]{4,3,2,1,0:T(8,128)S(1)}, f32[3,2,8,8,128]{4,3,2,1,0:T(8,128)S(1)}, u32[]{:S(2)}, u32[]{:S(2)}) %collective-permute-start.7) | collective-permute-done | bytes 196640 | tf_op jit(solution)/shard_map/ppermute | solution.py:277
  67.9 6.3 %forward.1 = (f32[8,8,16,128]{3,2,1,0:T(8,128)S(1)}, f32[32,8,256]{2,1,0:T(8,128)S(1)}, f32[72,16,128]{2,1,0:T(8,128)S(1)}) custom-call(s32[1,1,2]{2,1,0:T(1,128)S(1)} %copy-done.2, s32[1]{0:T(128)S(6)} %copy.14.source, s32[1]{0:T(128)S(6)} %copy.15.checkpoint, f32[1,64]{1,0:T(1,128)S(1)} %copy-done.4, f32[1,64,256]{2,1,0:T(8,128)S(1)} %copy-done.1, ...), custom_call_target="tpu_custom_call" | custom-call | tf_op jit(solution)/shard_map/forward/pallas_call | solution.py:310
  74.2 16.2 %all_to_all.25 = f32[32,1,8,256]{3,2,1,0:T(8,128)S(1)} all-to-all(f32[32,1,8,256]{3,2,1,0:T(8,128)S(1)} %bitcast.21), channel_id=1, replica_groups=mesh['x'=4,'yh'=4,'yl'=2,'z'=8,'c'=2] {'yl','z','c'}, dimensions={0} | all-to-all | bytes 524288 | tf_op jit(solution)/shard_map/all_to_all | solution.py:333
  90.4 6.7 %adjoint.1 = f32[4,9,8,128]{3,2,1,0:T(8,128)S(1)} custom-call(s32[1,1,2]{2,1,0:T(1,128)S(1)} %copy-done.2, s32[1,256]{1,0:T(1,128)S(1)} %copy-done.3, f32[32,8,256]{2,1,0:T(8,128)S(1)} %bitcast.20, f32[4,8,16,128]{3,2,1,0:T(8,128)S(1)} %copy-done, f32[4,8,16,128]{3,2,1,0:T(8,128)S(1)} %collective-permute-done.other, ...), custom_call_target="tpu_custom_call" | custom-call | tf_op jit(solution)/shard_map/adjoint/pallas_call | solution.py:335
  97.1 16.1 %all_to_all.26 = f32[4,9,8,128]{3,2,1,0:T(8,128)S(1)} all-to-all(f32[4,9,8,128]{3,2,1,0:T(8,128)S(1)} %adjoint.1), channel_id=1, replica_groups=mesh['x'=4,'yh'=4,'yl'=2,'z'=8,'c'=2] {'yh'}, dimensions={0} | all-to-all | bytes 294912 | tf_op jit(solution)/shard_map/all_to_all | solution.py:354
  113.3 8.4 %all_to_all.27 = f32[4,8,8,128]{3,2,1,0:T(8,128)S(1)} all-to-all(f32[4,8,8,128]{3,2,1,0:T(8,128)S(1)} %select_reduce_fusion), channel_id=1, replica_groups=mesh['x'=4,'yh'=4,'yl'=2,'z'=8,'c'=2] {'x'}, dimensions={0} | all-to-all | bytes 262144 | tf_op jit(solution)/shard_map/all_to_all | solution.py:357
  (27 shorter events, 2.9 us)
Async XLA Ops:
  1.7 3.6 %collective-permute-start = (f32[4,8,16,128]{3,2,1,0:T(8,128)}, f32[4,8,16,128]{3,2,1,0:T(8,128)S(1)}, u32[]{:S(2)}, u32[]{:S(2)}) collective-permute-start(f32[4,8,16,128]{3,2,1,0:T(8,128)} %pack.1.own), channel_id=1, source_target_pairs={{0,1},{1,0},{2,3},{3,2},{4,5},{5,4},{6,7},{7,6},{8,9},{9,8},{10,11... | collective-permute-start | bytes 786440 | tf_op jit(solution)/shard_map/ppermute | solution.py:280
  5.3 5.3 %copy-start.5 = (f32[1,8,8,128]{3,2,1,0:T(8,128)S(1)}, f32[1,8,8,128]{3,2,1,0:T(8,128)}, u32[]{:S(2)}) copy-start(f32[1,8,8,128]{3,2,1,0:T(8,128)} %param.11) | copy-start | bytes 98308
  6.3 18.0 %collective-permute-start.1 = (f32[2,4,8,16,128]{4,3,2,1,0:T(8,128)S(1)}, f32[2,4,8,16,128]{4,3,2,1,0:T(8,128)S(1)}, u32[]{:S(2)}, u32[]{:S(2)}) collective-permute-start(f32[2,4,8,16,128]{4,3,2,1,0:T(8,128)S(1)} %pad_maximum_fusion), channel_id=1, source_target_pairs={{0,2},{1,31},{2,4},{3,1},{4,6},{5,3},{6,8},{7,5},{8,10},{9,7},{10,... | collective-permute-start | bytes 1572872 | tf_op jit(solution)/shard_map/ppermute | solution.py:283
  11.3 16.0 %all-to-all-start = ((f32[4,1,8,8,128]{4,3,2,1,0:T(8,128)}), f32[4,1,8,8,128]{4,3,2,1,0:T(8,128)S(1)}, u32[]{:S(2)}, u32[]{:S(2)}) async-start(f32[4,1,8,8,128]{4,3,2,1,0:T(8,128)} %broadcast_in_dim.45), calls=%async_computation | async-start | bytes 262144 | tf_op jit(solution)/shard_map/all_to_all | solution.py:286
  24.3 15.0 %collective-permute-start.2 = (f32[2,4,8,16,128]{4,3,2,1,0:T(8,128)S(1)}, f32[2,4,8,16,128]{4,3,2,1,0:T(8,128)S(1)}, u32[]{:S(2)}, u32[]{:S(2)}) collective-permute-start(f32[2,4,8,16,128]{4,3,2,1,0:T(8,128)S(1)} %collective-permute-done.1.near), channel_id=1, source_target_pairs={{0,2},{1,31},{2,4},{3,1},{4,6},{5,3},{6,8},{7,5},{8,10},{9,7},{10,... | collective-permute-start | bytes 1572872 | tf_op jit(solution)/shard_map/ppermute | solution.py:283
  28.1 13.2 %all-to-all-start.1 = ((f32[4,4,1,8,8,128]{5,4,3,1,2,0:T(8,128)}), f32[4,4,1,8,8,128]{5,4,3,1,2,0:T(8,128)S(1)}, u32[]{:S(2)}, u32[]{:S(2)}) async-start(f32[4,4,1,8,8,128]{5,4,3,1,2,0:T(8,128)} %broadcast_in_dim.47), calls=%async_computation.1 | async-start | bytes 1048576 | tf_op jit(solution)/shard_map/all_to_all | solution.py:290
  32.4 0.7 copy-start.2
  33.2 34.6 %collective-permute-start.3 = (f32[2,4,8,16,128]{4,3,2,1,0:T(8,128)S(1)}, f32[2,4,8,16,128]{4,3,2,1,0:T(8,128)S(1)}, u32[]{:S(2)}, u32[]{:S(2)}) collective-permute-start(f32[2,4,8,16,128]{4,3,2,1,0:T(8,128)S(1)} %collective-permute-done.1.near), channel_id=1, source_target_pairs={{0,1},{1,0},{2,3},{3,2},{4,5},{5,4},{6,7},{7,6},{8,9},{9,8},{10,11... | collective-permute-start | bytes 1572872 | tf_op jit(solution)/shard_map/ppermute | solution.py:280
  39.4 28.5 %collective-permute-start.4 = (f32[2,4,8,16,128]{4,3,2,1,0:T(8,128)S(1)}, f32[2,4,8,16,128]{4,3,2,1,0:T(8,128)S(1)}, u32[]{:S(2)}, u32[]{:S(2)}) collective-permute-start(f32[2,4,8,16,128]{4,3,2,1,0:T(8,128)S(1)} %collective-permute-done.2.far), channel_id=1, source_target_pairs={{0,1},{1,0},{2,3},{3,2},{4,5},{5,4},{6,7},{7,6},{8,9},{9,8},{10,11... | collective-permute-start | bytes 1572872 | tf_op jit(solution)/shard_map/ppermute | solution.py:280
  41.3 26.5 %copy-start = (f32[4,8,16,128]{3,2,1,0:T(8,128)S(1)}, f32[4,8,16,128]{3,2,1,0:T(8,128)}, u32[]{:S(2)}) copy-start(f32[4,8,16,128]{3,2,1,0:T(8,128)} %pack.1.own) | copy-start | bytes 786436
  41.3 6.7 %collective-permute-start.6 = (f32[2,8,8,128]{3,2,1,0:T(8,128)S(1)}, f32[2,8,8,128]{3,2,1,0:T(8,128)S(1)}, u32[]{:S(2)}, u32[]{:S(2)}) collective-permute-start(f32[2,8,8,128]{3,2,1,0:T(8,128)S(1)} %constant_dynamic-slice_fusion.vel), channel_id=1, source_target_pairs={{0,31},{1,0},{2,1},{3,2},{4,3},{5,4},{6,5},{7,6},{8,7},{9,8},{10,9... | collective-permute-start | bytes 196616 | tf_op jit(solution)/shard_map/ppermute | solution.py:277
  46.1 7.7 %collective-permute-start.5 = (f32[2,8,8,128]{3,2,1,0:T(8,128)S(1)}, f32[2,8,8,128]{3,2,1,0:T(8,128)S(1)}, u32[]{:S(2)}, u32[]{:S(2)}) collective-permute-start(f32[2,8,8,128]{3,2,1,0:T(8,128)S(1)} %constant_dynamic-slice_fusion.vel), channel_id=1, source_target_pairs={{0,1},{1,2},{2,3},{3,4},{4,5},{5,6},{6,7},{7,8},{8,9},{9,10},{10,1... | collective-permute-start | bytes 196616 | tf_op jit(solution)/shard_map/ppermute | solution.py:277
  53.8 14.1 %copy-start.1 = (f32[1,64,256]{2,1,0:T(8,128)S(1)}, f32[1,64,256]{2,1,0:T(8,128)}, u32[]{:S(2)}) copy-start(f32[1,64,256]{2,1,0:T(8,128)} %observed.1) | copy-start | bytes 196612
  53.8 9.6 %collective-permute-start.8 = (f32[3,2,8,8,128]{4,3,2,1,0:T(8,128)S(1)}, f32[3,2,8,8,128]{4,3,2,1,0:T(8,128)S(1)}, u32[]{:S(2)}, u32[]{:S(2)}) collective-permute-start(f32[3,2,8,8,128]{4,3,2,1,0:T(8,128)S(1)} %pad_maximum_fusion.1), channel_id=1, source_target_pairs={{0,29},{1,30},{2,31},{3,0},{4,1},{5,2},{6,3},{7,4},{8,5},{9,6},{10... | collective-permute-start | bytes 589832 | tf_op jit(solution)/shard_map/ppermute | solution.py:277
  55.8 12.1 %collective-permute-start.7 = (f32[3,2,8,8,128]{4,3,2,1,0:T(8,128)S(1)}, f32[3,2,8,8,128]{4,3,2,1,0:T(8,128)S(1)}, u32[]{:S(2)}, u32[]{:S(2)}) collective-permute-start(f32[3,2,8,8,128]{4,3,2,1,0:T(8,128)S(1)} %pad_maximum_fusion.1), channel_id=1, source_target_pairs={{0,3},{1,4},{2,5},{3,6},{4,7},{5,8},{6,9},{7,10},{8,11},{9,12},{10... | collective-permute-start | bytes 589832 | tf_op jit(solution)/shard_map/ppermute | solution.py:277
  60.0 7.8 %copy-start.3 = (s32[1,256]{1,0:T(1,128)S(1)}, s32[1,256]{1,0:T(1,128)}, u32[]{:S(2)}) copy-start(s32[1,256]{1,0:T(1,128)} %receivers.3) | copy-start | bytes 3076
  60.1 7.8 %copy-start.4 = (f32[1,64]{1,0:T(1,128)S(1)}, f32[1,64]{1,0:T(1,128)}, u32[]{:S(2)}) copy-start(f32[1,64]{1,0:T(1,128)} %wavelet.1) | copy-start | bytes 772

commit v6 on v5

--- a/solution.py
+++ b/solution.py
@@ -113,17 +113,18 @@
     matrix[...] = along_z()
     for item in range(2):
         assemble(field, item, item, slab, own, other, near, far, swapped_near, swapped_far)
-    tiles = (
-        [(vel_far_left, k) for k in range(3)] + [(vel_left, None), (vel, None), (vel_right, None)] + [(vel_far_right, k) for k in range(3)]
-    )
-    for j in range(9):
-        there = slab + (j - 4)
+    pieces = (
+        (-4, 4, 4, vel_far_left, 0), (-3, 0, 8, vel_far_left, 4), (-2, 0, 8, vel_far_left, 12),
+        (-1, 0, 8, vel_left, 0), (0, 0, 8, vel, 0), (1, 0, 8, vel_right, 0),
+        (2, 0, 8, vel_far_right, 0), (3, 0, 8, vel_far_right, 8), (4, 0, 4, vel_far_right, 16),
+    )
+    for j, first, count, ref, begin in pieces:
+        there = slab + j
         inside = (there >= 0) & (there < SLABS)
-        ref, k = tiles[j]
+        plane = TX * (j + 4) + first
         for row in range(2):
-            speed = ref[row] if k is None else ref[k, row]
-            speed = jnp.where(inside, STEP_SCALE * speed, 0.0)
-            courant[TX * j : TX * (j + 1), 8 * row : 8 * row + 8, :] = speed * speed
+            speed = jnp.where(inside, STEP_SCALE * ref[row, begin : begin + count], 0.0)
+            courant[plane : plane + count, 8 * row : 8 * row + 8, :] = speed * speed
 
     lane = lax.broadcasted_iota(jnp.int32, (AY, TZ), 1)
     suby = lax.broadcasted_iota(jnp.int32, (AY, TZ), 0)
@@ -294,9 +295,10 @@
     vel_left = shift(vel, 1)
     vel_right = shift(vel, -1)
     far = next_chip(near)
-    vel_packed = jnp.stack([vel_left, vel, vel_right])
-    vel_far_left = shift(vel_packed, 3)
-    vel_far_right = shift(vel_packed, -3)
+    rightward = jnp.concatenate([vel_left[:, 4:], vel, vel_right], axis=1)
+    leftward = jnp.concatenate([vel_left, vel, vel_right[:, :4]], axis=1)
+    vel_far_left = shift(rightward, 3)
+    vel_far_right = shift(leftward, -3)
     swapped_near = partner(near)
     swapped_far = partner(far)
     fields = (own, other, near, far, swapped_near, swapped_far)

time: 123 us -> 123 us (level)
  local copies, waits for them, and re-layouts: 2.22 us -> 3.6 us
    ppermute x4, waiting for transfers between devices: 12.9 us -> 11.6 us  [shift(): lax.ppermute(cells, DOM, [(i, (i + by) % SLABS) for i in range(SLABS)])]
  transfers between devices with their start and end apart: 11 -> 11, of which waited for: 6 -> 6; matrix products, arithmetic and copies ran while one was open for 1% -> 2% of each run, Pallas kernels for 0% -> 0%
where the time goes in v6:
time: 123 us
  blocking collectives  40.2 us (33%)
  starting transfers between devices  38.8 us (32%)
  waiting for transfers between devices  21.2 us (17%)
  Pallas kernels  14.7 us (12%)
  local copies, waits for them, and re-layouts  3.6 us (3%)
  other arithmetic  2.6 us (2%)
  between operations  1.72 us (1%)
    all_to_all x1, blocking collectives, inner(): landed = lax.all_to_all(terms, 'yh', 0, 0, tiled=True)  16.1 us
    all_to_all x1, blocking collectives, inner(): lax.all_to_all(misfit[:, None], DOM, 0, 0, tiled=True)  15.8 us
    ppermute x4, starting transfers between devices, shift(): lax.ppermute(cells, DOM, [(i, (i + by) % SLABS) for i in range(SLABS)])  12.1 us
    ppermute x4, waiting for transfers between devices, shift(): lax.ppermute(cells, DOM, [(i, (i + by) % SLABS) for i in range(SLABS)])  11.6 us
    ppermute x3, starting transfers between devices, partner(): return lax.ppermute(cells, DOM, [(i, i ^ 1) for i in range(SLABS)])  9.95 us
    all_to_all x1, blocking collectives, inner(): landed = lax.all_to_all(sums, 'x', 0, 0, tiled=True)  8.36 us
    ppermute x2, waiting for transfers between devices, next_chip(): lax.ppermute(cells, DOM, [(i, (i + (-2 if i % 2 else 2)) % SLABS) for i i...  6.83 us
    pallas_call x1, Pallas kernels, inner(): pl.pallas_call(adjoint_kernel, in_specs=in_smem(1) + in_vmem(11), out_spe...  6.71 us
  transfers between devices with their start and end apart: 11, of which 6 were waited for; matrix products, arithmetic and copies ran while one was open for 2% of the time, Pallas kernels for 0%

profile of v6, /device:TPU:8, one launch (start us, length us, event | category | flops | bytes accessed | tf_op | source)
XLA Modules:
  0.0 122.7 jit_solution(256960955128706311)
XLA Ops:
  0.0 1.7 %pack.1.own = f32[4,8,16,128]{3,2,1,0:T(8,128)} custom-call(f32[1,8,16,128]{3,2,1,0:T(8,128)} %a.1, f32[1,8,16,128]{3,2,1,0:T(8,128)} %b.1, f32[1,8,16,128]{3,2,1,0:T(8,128)} %c.1, f32[1,8,16,128]{3,2,1,0:T(8,128)} %d.1), custom_call_target="tpu_custom_call" | custom-call | tf_op jit(solution)/shard_map/pack/pallas_call | solution.py:246
  1.7 1.9 %collective-permute-start = (f32[4,8,16,128]{3,2,1,0:T(8,128)}, f32[4,8,16,128]{3,2,1,0:T(8,128)S(1)}, u32[]{:S(2)}, u32[]{:S(2)}) collective-permute-start(f32[4,8,16,128]{3,2,1,0:T(8,128)} %pack.1.own), channel_id=1, source_target_pairs={{0,1},{1,0},{2,3},{3,2},{4,5},{5,4},{6,7},{7,6},{8,9},{9,8},{10,11... | collective-permute-start | bytes 786440 | tf_op jit(solution)/shard_map/ppermute | solution.py:281
  3.6 1.7 %collective-permute-done.other = f32[4,8,16,128]{3,2,1,0:T(8,128)S(1)} collective-permute-done((f32[4,8,16,128]{3,2,1,0:T(8,128)}, f32[4,8,16,128]{3,2,1,0:T(8,128)S(1)}, u32[]{:S(2)}, u32[]{:S(2)}) %collective-permute-start) | collective-permute-done | bytes 262176 | tf_op jit(solution)/shard_map/ppermute | solution.py:281
  5.3 1.0 pad_maximum_fusion
  6.3 4.3 %collective-permute-start.1 = (f32[2,4,8,16,128]{4,3,2,1,0:T(8,128)S(1)}, f32[2,4,8,16,128]{4,3,2,1,0:T(8,128)S(1)}, u32[]{:S(2)}, u32[]{:S(2)}) collective-permute-start(f32[2,4,8,16,128]{4,3,2,1,0:T(8,128)S(1)} %pad_maximum_fusion), channel_id=1, source_target_pairs={{0,2},{1,31},{2,4},{3,1},{4,6},{5,3},{6,8},{7,5},{8,10},{9,7},{10,... | collective-permute-start | bytes 1572872 | tf_op jit(solution)/shard_map/ppermute | solution.py:284
  11.3 6.2 %all-to-all-start = ((f32[4,1,8,8,128]{4,3,2,1,0:T(8,128)}), f32[4,1,8,8,128]{4,3,2,1,0:T(8,128)S(1)}, u32[]{:S(2)}, u32[]{:S(2)}) async-start(f32[4,1,8,8,128]{4,3,2,1,0:T(8,128)} %broadcast_in_dim.45), calls=%async_computation | async-start | bytes 262144 | tf_op jit(solution)/shard_map/all_to_all | solution.py:287
  17.5 6.8 %collective-permute-done.1.near = f32[2,4,8,16,128]{4,3,2,1,0:T(8,128)S(1)} collective-permute-done((f32[2,4,8,16,128]{4,3,2,1,0:T(8,128)S(1)}, f32[2,4,8,16,128]{4,3,2,1,0:T(8,128)S(1)}, u32[]{:S(2)}, u32[]{:S(2)}) %collective-permute-start.1) | collective-permute-done | bytes 524320 | tf_op jit(solution)/shard_map/ppermute | solution.py:284
  24.3 1.9 %collective-permute-start.2 = (f32[2,4,8,16,128]{4,3,2,1,0:T(8,128)S(1)}, f32[2,4,8,16,128]{4,3,2,1,0:T(8,128)S(1)}, u32[]{:S(2)}, u32[]{:S(2)}) collective-permute-start(f32[2,4,8,16,128]{4,3,2,1,0:T(8,128)S(1)} %collective-permute-done.1.near), channel_id=1, source_target_pairs={{0,2},{1,31},{2,4},{3,1},{4,6},{5,3},{6,8},{7,5},{8,10},{9,7},{10,... | collective-permute-start | bytes 1572872 | tf_op jit(solution)/shard_map/ppermute | solution.py:284
  26.2 1.0 all-to-all-done
  28.1 4.3 %all-to-all-start.1 = ((f32[4,4,1,8,8,128]{5,4,3,1,2,0:T(8,128)}), f32[4,4,1,8,8,128]{5,4,3,1,2,0:T(8,128)S(1)}, u32[]{:S(2)}, u32[]{:S(2)}) async-start(f32[4,4,1,8,8,128]{5,4,3,1,2,0:T(8,128)} %broadcast_in_dim.47), calls=%async_computation.1 | async-start | bytes 1048576 | tf_op jit(solution)/shard_map/all_to_all | solution.py:291
  32.4 6.1 %collective-permute-start.3 = (f32[2,4,8,16,128]{4,3,2,1,0:T(8,128)S(1)}, f32[2,4,8,16,128]{4,3,2,1,0:T(8,128)S(1)}, u32[]{:S(2)}, u32[]{:S(2)}) collective-permute-start(f32[2,4,8,16,128]{4,3,2,1,0:T(8,128)S(1)} %collective-permute-done.1.near), channel_id=1, source_target_pairs={{0,1},{1,0},{2,3},{3,2},{4,5},{5,4},{6,7},{7,6},{8,9},{9,8},{10,11... | collective-permute-start | bytes 1572872 | tf_op jit(solution)/shard_map/ppermute | solution.py:281
  38.5 1.9 %collective-permute-start.4 = (f32[2,4,8,16,128]{4,3,2,1,0:T(8,128)S(1)}, f32[2,4,8,16,128]{4,3,2,1,0:T(8,128)S(1)}, u32[]{:S(2)}, u32[]{:S(2)}) collective-permute-start(f32[2,4,8,16,128]{4,3,2,1,0:T(8,128)S(1)} %collective-permute-done.2.far), channel_id=1, source_target_pairs={{0,1},{1,0},{2,3},{3,2},{4,5},{5,4},{6,7},{7,6},{8,9},{9,8},{10,11... | collective-permute-start | bytes 1572872 | tf_op jit(solution)/shard_map/ppermute | solution.py:281
  41.3 4.7 %collective-permute-start.6 = (f32[2,8,8,128]{3,2,1,0:T(8,128)S(1)}, f32[2,8,8,128]{3,2,1,0:T(8,128)S(1)}, u32[]{:S(2)}, u32[]{:S(2)}) collective-permute-start(f32[2,8,8,128]{3,2,1,0:T(8,128)S(1)} %constant_dynamic-slice_fusion.vel), channel_id=1, source_target_pairs={{0,31},{1,0},{2,1},{3,2},{4,3},{5,4},{6,5},{7,6},{8,7},{9,8},{10,9... | collective-permute-start | bytes 196616 | tf_op jit(solution)/shard_map/ppermute | solution.py:278
  46.0 1.9 %collective-permute-start.5 = (f32[2,8,8,128]{3,2,1,0:T(8,128)S(1)}, f32[2,8,8,128]{3,2,1,0:T(8,128)S(1)}, u32[]{:S(2)}, u32[]{:S(2)}) collective-permute-start(f32[2,8,8,128]{3,2,1,0:T(8,128)S(1)} %constant_dynamic-slice_fusion.vel), channel_id=1, source_target_pairs={{0,1},{1,2},{2,3},{3,4},{4,5},{5,6},{6,7},{7,8},{8,9},{9,10},{10,1... | collective-permute-start | bytes 196616 | tf_op jit(solution)/shard_map/ppermute | solution.py:278
  48.5 5.1 %collective-permute-done.5.vel_left = f32[2,8,8,128]{3,2,1,0:T(8,128)S(1)} collective-permute-done((f32[2,8,8,128]{3,2,1,0:T(8,128)S(1)}, f32[2,8,8,128]{3,2,1,0:T(8,128)S(1)}, u32[]{:S(2)}, u32[]{:S(2)}) %collective-permute-start.5) | collective-permute-done | bytes 65568 | tf_op jit(solution)/shard_map/ppermute | solution.py:278
  55.3 1.9 %collective-permute-start.8 = (f32[2,20,8,128]{3,2,1,0:T(8,128)S(1)}, f32[2,20,8,128]{3,2,1,0:T(8,128)S(1)}, u32[]{:S(2)}, u32[]{:S(2)}) collective-permute-start(f32[2,20,8,128]{3,2,1,0:T(8,128)S(1)} %get-tuple-element.11), channel_id=1, source_target_pairs={{0,29},{1,30},{2,31},{3,0},{4,1},{5,2},{6,3},{7,4},{8,5},{9,6},{10... | collective-permute-start | bytes 491528 | tf_op jit(solution)/shard_map/ppermute | solution.py:278
  57.3 3.6 %collective-permute-start.7 = (f32[2,20,8,128]{3,2,1,0:T(8,128)S(1)}, f32[2,20,8,128]{3,2,1,0:T(8,128)S(1)}, u32[]{:S(2)}, u32[]{:S(2)}) collective-permute-start(f32[2,20,8,128]{3,2,1,0:T(8,128)S(1)} %get-tuple-element.12), channel_id=1, source_target_pairs={{0,3},{1,4},{2,5},{3,6},{4,7},{5,8},{6,9},{7,10},{8,11},{9,12},{10... | collective-permute-start | bytes 491528 | tf_op jit(solution)/shard_map/ppermute | solution.py:278
  62.3 1.7 %collective-permute-done.8.vel_far_right = f32[2,20,8,128]{3,2,1,0:T(8,128)S(1)} collective-permute-done((f32[2,20,8,128]{3,2,1,0:T(8,128)S(1)}, f32[2,20,8,128]{3,2,1,0:T(8,128)S(1)}, u32[]{:S(2)}, u32[]{:S(2)}) %collective-permute-start.8) | collective-permute-done | bytes 163872 | tf_op jit(solution)/shard_map/ppermute | solution.py:278
  64.0 4.7 %collective-permute-done.7.vel_far_left = f32[2,20,8,128]{3,2,1,0:T(8,128)S(1)} collective-permute-done((f32[2,20,8,128]{3,2,1,0:T(8,128)S(1)}, f32[2,20,8,128]{3,2,1,0:T(8,128)S(1)}, u32[]{:S(2)}, u32[]{:S(2)}) %collective-permute-start.7) | collective-permute-done | bytes 163872 | tf_op jit(solution)/shard_map/ppermute | solution.py:278
  68.8 6.3 %forward.1 = (f32[8,8,16,128]{3,2,1,0:T(8,128)S(1)}, f32[32,8,256]{2,1,0:T(8,128)S(1)}, f32[72,16,128]{2,1,0:T(8,128)S(1)}) custom-call(s32[1,1,2]{2,1,0:T(1,128)S(1)} %copy-done.4, s32[1]{0:T(128)S(6)} %copy.14.source, s32[1]{0:T(128)S(6)} %copy.15.checkpoint, f32[1,64]{1,0:T(1,128)S(1)} %copy-done.6, f32[1,64,256]{2,1,0:T(8,128)S(1)} %copy-done.3, ...), custom_call_target="tpu_custom_call" | custom-call | tf_op jit(solution)/shard_map/forward/pallas_call | solution.py:312
  75.1 15.8 %all_to_all.25 = f32[32,1,8,256]{3,2,1,0:T(8,128)S(1)} all-to-all(f32[32,1,8,256]{3,2,1,0:T(8,128)S(1)} %bitcast.17), channel_id=1, replica_groups=mesh['x'=4,'yh'=4,'yl'=2,'z'=8,'c'=2] {'yl','z','c'}, dimensions={0} | all-to-all | bytes 524288 | tf_op jit(solution)/shard_map/all_to_all | solution.py:335
  90.9 6.7 %adjoint.1 = f32[4,9,8,128]{3,2,1,0:T(8,128)S(1)} custom-call(s32[1,1,2]{2,1,0:T(1,128)S(1)} %copy-done.4, s32[1,256]{1,0:T(1,128)S(1)} %copy-done.5, f32[32,8,256]{2,1,0:T(8,128)S(1)} %bitcast.16, f32[4,8,16,128]{3,2,1,0:T(8,128)S(1)} %copy-done, f32[4,8,16,128]{3,2,1,0:T(8,128)S(1)} %collective-permute-done.other, ...), custom_call_target="tpu_custom_call" | custom-call | tf_op jit(solution)/shard_map/adjoint/pallas_call | solution.py:337
  97.6 16.1 %all_to_all.26 = f32[4,9,8,128]{3,2,1,0:T(8,128)S(1)} all-to-all(f32[4,9,8,128]{3,2,1,0:T(8,128)S(1)} %adjoint.1), channel_id=1, replica_groups=mesh['x'=4,'yh'=4,'yl'=2,'z'=8,'c'=2] {'yh'}, dimensions={0} | all-to-all | bytes 294912 | tf_op jit(solution)/shard_map/all_to_all | solution.py:356
  113.7 8.4 %all_to_all.27 = f32[4,8,8,128]{3,2,1,0:T(8,128)S(1)} all-to-all(f32[4,8,8,128]{3,2,1,0:T(8,128)S(1)} %select_reduce_fusion), channel_id=1, replica_groups=mesh['x'=4,'yh'=4,'yl'=2,'z'=8,'c'=2] {'x'}, dimensions={0} | all-to-all | bytes 262144 | tf_op jit(solution)/shard_map/all_to_all | solution.py:359
  (33 shorter events, 5.2 us)
Async XLA Ops:
  1.7 3.6 %collective-permute-start = (f32[4,8,16,128]{3,2,1,0:T(8,128)}, f32[4,8,16,128]{3,2,1,0:T(8,128)S(1)}, u32[]{:S(2)}, u32[]{:S(2)}) collective-permute-start(f32[4,8,16,128]{3,2,1,0:T(8,128)} %pack.1.own), channel_id=1, source_target_pairs={{0,1},{1,0},{2,3},{3,2},{4,5},{5,4},{6,7},{7,6},{8,9},{9,8},{10,11... | collective-permute-start | bytes 786440 | tf_op jit(solution)/shard_map/ppermute | solution.py:281
  5.3 5.3 %copy-start.7 = (f32[1,8,8,128]{3,2,1,0:T(8,128)S(1)}, f32[1,8,8,128]{3,2,1,0:T(8,128)}, u32[]{:S(2)}) copy-start(f32[1,8,8,128]{3,2,1,0:T(8,128)} %param.11) | copy-start | bytes 98308
  6.3 18.0 %collective-permute-start.1 = (f32[2,4,8,16,128]{4,3,2,1,0:T(8,128)S(1)}, f32[2,4,8,16,128]{4,3,2,1,0:T(8,128)S(1)}, u32[]{:S(2)}, u32[]{:S(2)}) collective-permute-start(f32[2,4,8,16,128]{4,3,2,1,0:T(8,128)S(1)} %pad_maximum_fusion), channel_id=1, source_target_pairs={{0,2},{1,31},{2,4},{3,1},{4,6},{5,3},{6,8},{7,5},{8,10},{9,7},{10,... | collective-permute-start | bytes 1572872 | tf_op jit(solution)/shard_map/ppermute | solution.py:284
  11.3 16.0 %all-to-all-start = ((f32[4,1,8,8,128]{4,3,2,1,0:T(8,128)}), f32[4,1,8,8,128]{4,3,2,1,0:T(8,128)S(1)}, u32[]{:S(2)}, u32[]{:S(2)}) async-start(f32[4,1,8,8,128]{4,3,2,1,0:T(8,128)} %broadcast_in_dim.45), calls=%async_computation | async-start | bytes 262144 | tf_op jit(solution)/shard_map/all_to_all | solution.py:287
  24.3 14.2 %collective-permute-start.2 = (f32[2,4,8,16,128]{4,3,2,1,0:T(8,128)S(1)}, f32[2,4,8,16,128]{4,3,2,1,0:T(8,128)S(1)}, u32[]{:S(2)}, u32[]{:S(2)}) collective-permute-start(f32[2,4,8,16,128]{4,3,2,1,0:T(8,128)S(1)} %collective-permute-done.1.near), channel_id=1, source_target_pairs={{0,2},{1,31},{2,4},{3,1},{4,6},{5,3},{6,8},{7,5},{8,10},{9,7},{10,... | collective-permute-start | bytes 1572872 | tf_op jit(solution)/shard_map/ppermute | solution.py:284
  28.1 13.2 %all-to-all-start.1 = ((f32[4,4,1,8,8,128]{5,4,3,1,2,0:T(8,128)}), f32[4,4,1,8,8,128]{5,4,3,1,2,0:T(8,128)S(1)}, u32[]{:S(2)}, u32[]{:S(2)}) async-start(f32[4,4,1,8,8,128]{5,4,3,1,2,0:T(8,128)} %broadcast_in_dim.47), calls=%async_computation.1 | async-start | bytes 1048576 | tf_op jit(solution)/shard_map/all_to_all | solution.py:291
  32.4 36.3 %collective-permute-start.3 = (f32[2,4,8,16,128]{4,3,2,1,0:T(8,128)S(1)}, f32[2,4,8,16,128]{4,3,2,1,0:T(8,128)S(1)}, u32[]{:S(2)}, u32[]{:S(2)}) collective-permute-start(f32[2,4,8,16,128]{4,3,2,1,0:T(8,128)S(1)} %collective-permute-done.1.near), channel_id=1, source_target_pairs={{0,1},{1,0},{2,3},{3,2},{4,5},{5,4},{6,7},{7,6},{8,9},{9,8},{10,11... | collective-permute-start | bytes 1572872 | tf_op jit(solution)/shard_map/ppermute | solution.py:281
  38.5 30.2 %collective-permute-start.4 = (f32[2,4,8,16,128]{4,3,2,1,0:T(8,128)S(1)}, f32[2,4,8,16,128]{4,3,2,1,0:T(8,128)S(1)}, u32[]{:S(2)}, u32[]{:S(2)}) collective-permute-start(f32[2,4,8,16,128]{4,3,2,1,0:T(8,128)S(1)} %collective-permute-done.2.far), channel_id=1, source_target_pairs={{0,1},{1,0},{2,3},{3,2},{4,5},{5,4},{6,7},{7,6},{8,9},{9,8},{10,11... | collective-permute-start | bytes 1572872 | tf_op jit(solution)/shard_map/ppermute | solution.py:281
  40.4 0.7 copy-start.4
  41.3 6.6 %collective-permute-start.6 = (f32[2,8,8,128]{3,2,1,0:T(8,128)S(1)}, f32[2,8,8,128]{3,2,1,0:T(8,128)S(1)}, u32[]{:S(2)}, u32[]{:S(2)}) collective-permute-start(f32[2,8,8,128]{3,2,1,0:T(8,128)S(1)} %constant_dynamic-slice_fusion.vel), channel_id=1, source_target_pairs={{0,31},{1,0},{2,1},{3,2},{4,3},{5,4},{6,5},{7,6},{8,7},{9,8},{10,9... | collective-permute-start | bytes 196616 | tf_op jit(solution)/shard_map/ppermute | solution.py:278
  46.0 7.7 %collective-permute-start.5 = (f32[2,8,8,128]{3,2,1,0:T(8,128)S(1)}, f32[2,8,8,128]{3,2,1,0:T(8,128)S(1)}, u32[]{:S(2)}, u32[]{:S(2)}) collective-permute-start(f32[2,8,8,128]{3,2,1,0:T(8,128)S(1)} %constant_dynamic-slice_fusion.vel), channel_id=1, source_target_pairs={{0,1},{1,2},{2,3},{3,4},{4,5},{5,6},{6,7},{7,8},{8,9},{9,10},{10,1... | collective-permute-start | bytes 196616 | tf_op jit(solution)/shard_map/ppermute | solution.py:278
  47.9 0.6 copy-start.1
  53.6 0.8 slice-start
  54.4 14.3 %copy-start = (f32[4,8,16,128]{3,2,1,0:T(8,128)S(1)}, f32[4,8,16,128]{3,2,1,0:T(8,128)}, u32[]{:S(2)}) copy-start(f32[4,8,16,128]{3,2,1,0:T(8,128)} %pack.1.own) | copy-start | bytes 786436
  54.4 14.3 %copy-start.2 = (f32[2,8,8,128]{3,2,1,0:T(8,128)S(1)}, f32[2,8,8,128]{3,2,1,0:T(8,128)}, u32[]{:S(2)}) copy-start(f32[2,8,8,128]{3,2,1,0:T(8,128)} %copy-done.1) | copy-start | bytes 196612
  54.4 14.3 %copy-start.3 = (f32[1,64,256]{2,1,0:T(8,128)S(1)}, f32[1,64,256]{2,1,0:T(8,128)}, u32[]{:S(2)}) copy-start(f32[1,64,256]{2,1,0:T(8,128)} %observed.1) | copy-start | bytes 196612
  55.3 8.7 %collective-permute-start.8 = (f32[2,20,8,128]{3,2,1,0:T(8,128)S(1)}, f32[2,20,8,128]{3,2,1,0:T(8,128)S(1)}, u32[]{:S(2)}, u32[]{:S(2)}) collective-permute-start(f32[2,20,8,128]{3,2,1,0:T(8,128)S(1)} %get-tuple-element.11), channel_id=1, source_target_pairs={{0,29},{1,30},{2,31},{3,0},{4,1},{5,2},{6,3},{7,4},{8,5},{9,6},{10... | collective-permute-start | bytes 491528 | tf_op jit(solution)/shard_map/ppermute | solution.py:278
  57.3 11.4 %collective-permute-start.7 = (f32[2,20,8,128]{3,2,1,0:T(8,128)S(1)}, f32[2,20,8,128]{3,2,1,0:T(8,128)S(1)}, u32[]{:S(2)}, u32[]{:S(2)}) collective-permute-start(f32[2,20,8,128]{3,2,1,0:T(8,128)S(1)} %get-tuple-element.12), channel_id=1, source_target_pairs={{0,3},{1,4},{2,5},{3,6},{4,7},{5,8},{6,9},{7,10},{8,11},{9,12},{10... | collective-permute-start | bytes 491528 | tf_op jit(solution)/shard_map/ppermute | solution.py:278
  61.6 7.2 %copy-start.5 = (s32[1,256]{1,0:T(1,128)S(1)}, s32[1,256]{1,0:T(1,128)}, u32[]{:S(2)}) copy-start(s32[1,256]{1,0:T(1,128)} %receivers.3) | copy-start | bytes 3076
  61.6 7.2 %copy-start.6 = (f32[1,64]{1,0:T(1,128)S(1)}, f32[1,64]{1,0:T(1,128)}, u32[]{:S(2)}) copy-start(f32[1,64]{1,0:T(1,128)} %wavelet.1) | copy-start | bytes 772
